TPU v7x, 128 devices: a whole 4x4x4 slice. The times are simulated.
128 devices in a mesh: dp: 8 (over z, core), mem: 16 (over y, x).
Axes of the slice: x: 4, y: 4, z: 4, core: 2. Of those that a mesh axis runs over, the one named last changes fastest.
Arguments:
- tokens: bfloat16 [8, 3072, 2048], P('dp')
- w_query: bfloat16 [2048, 2048], P(None, 'mem'), may hold values from -0.125 to 0.125
- w_key: bfloat16 [2048, 2048], P(None, 'mem'), may hold values from -0.125 to 0.125
- w_value: bfloat16 [2048, 2048], P(None, 'mem'), may hold values from -0.125 to 0.125
- gate_bias: float32 [16], P('mem'), may hold values from -2 to 2
- memory_keys: bfloat16 [8, 24576, 2048], P('dp', 'mem')
- memory_values: bfloat16 [8, 24576, 2048], P('dp', 'mem'), may hold values from -6 to 6
- retrieval_ids: int32 [8, 16, 24, 8], P('dp', 'mem'), may hold values from 0 to 383, as said below
- retrieval_counts: int32 [8, 16, 24], P('dp', 'mem'), may hold values from 1 to 8, as said below
- cotangent: bfloat16 [8, 3072, 2048], P('dp', None, 'mem')
Outputs:
- attended: bfloat16 [8, 3072, 2048], P('dp', None, 'mem')
- grad_q: float32 [2048, 2048], P('dp', 'mem')
- grad_k: float32 [2048, 2048], P('dp', 'mem')
- grad_v: float32 [2048, 2048], P('dp', 'mem')
- grad_gate: float32 [16], P('mem')
Inputs may be any that keep to these rules, and one draw needn't show every extreme that they name: `retrieval_ids`: entry [d, h, b, j] names tile t of document d's memory, owned by index t // 24 of mem; only entries j < retrieval_counts[d, h, b] are live, the others are padding with arbitrary tile ids. Over the live entries of one head at most 12 name tiles of one owner, and in each document one owner is named by exactly 12 live entries of every head. `retrieval_counts`: the number of leading live entries of the list of block b of head h.
All inputs are finite; a program needn't handle non-finite values.
Results may differ from a plain program's by a relative error of at most 0.011.
Values may be sent and summed in bfloat16 or wider, within the bound.
No kernel may reach another device: no remote copies, remote signals or barrier semaphores. Data moves between devices by JAX's collectives and lax.ppermute only.
A program may use at most 128 MiB of HBM per device.

v0:
```python
import functools

import jax
import jax.numpy as jnp
from jax import lax
from jax.experimental import pallas as pl
from jax.experimental.pallas import tpu as pltpu
from jax.sharding import PartitionSpec as P

DH = 128
SEG = 512
QB = 128
TILE = 64
TOP = 8
SEGS = 6
TILES_DEV = 24
TOK = 3072
NQB = 24
CAP = 12
MEMS = 16
D = 2048
ENTRIES = NQB * TOP
SCALING = DH ** (-0.5)
ROWS_OUT = D // 8
GATE_ROWS = 16
F32 = jnp.float32
BF16 = jnp.bfloat16
MIB = 1 << 20

NT = (((1,), (1,)), ((), ()))
TN = (((0,), (0,)), ((), ()))


def dot(a, b, dims=(((1,), (0,)), ((), ()))):
    return lax.dot_general(a, b, dims, preferred_element_type=F32)


def iota(shape, dim):
    return lax.broadcasted_iota(jnp.int32, shape, dim)


def gate_row(bias_ref):
    return 1.0 / (1.0 + jnp.exp(-jnp.full((1, DH), bias_ref[0], F32)))


def request_kernel(ids_ref, counts_ref, table_ref, slot_ref):
    ids = ids_ref[...]
    owner = (ids // TILES_DEV).astype(F32)
    local = (ids % TILES_DEV).astype(F32)
    counts = counts_ref[...].astype(F32)
    by_block = (iota((ENTRIES, NQB), 0) // TOP == iota((ENTRIES, NQB), 1)).astype(F32)
    pick = (iota((ENTRIES, TOP), 0) % TOP == iota((ENTRIES, TOP), 1)).astype(F32)
    owner_col = jnp.sum(dot(by_block, owner) * pick, axis=1, keepdims=True)
    local_col = jnp.sum(dot(by_block, local) * pick, axis=1, keepdims=True)
    count_col = jnp.sum(by_block * counts, axis=1, keepdims=True)
    slot_col = (iota((ENTRIES, 1), 0) % TOP).astype(F32)
    owner_col = jnp.where(slot_col < count_col, owner_col, float(MEMS))
    of_block = (iota((NQB, ENTRIES), 1) // TOP == iota((NQB, ENTRIES), 0)).astype(F32)
    of_slot = (iota((TOP, ENTRIES), 1) % TOP == iota((TOP, ENTRIES), 0)).astype(F32)
    owner_row = jnp.sum(dot(owner, of_slot) * of_block, axis=0, keepdims=True)
    count_row = dot(jnp.broadcast_to(counts, (8, NQB)), of_block)[:1]
    slot_row = (iota((1, ENTRIES), 1) % TOP).astype(F32)
    owner_row = jnp.where(slot_row < count_row, owner_row, float(MEMS))
    same = owner_col == owner_row
    first = iota((ENTRIES, ENTRIES), 0)
    second = iota((ENTRIES, ENTRIES), 1)
    rank_col = jnp.sum((same & (second < first)).astype(F32), axis=1, keepdims=True)
    rank_row = jnp.sum((same & (first < second)).astype(F32), axis=0, keepdims=True)
    sends = (owner_row == iota((MEMS, ENTRIES), 0).astype(F32)).astype(F32)
    place = jnp.where(rank_col == iota((ENTRIES, 128), 1).astype(F32), local_col, 0.0)
    table_ref[...] = dot(sends, place).astype(jnp.int32)
    slot_ref[...] = jnp.clip(owner_row * CAP + rank_row, 0.0, float(MEMS * CAP - 1)).astype(jnp.int32)


def make_requests(ids, counts):
    return pl.pallas_call(
        request_kernel,
        out_shape=(
            jax.ShapeDtypeStruct((MEMS, 128), jnp.int32),
            jax.ShapeDtypeStruct((1, ENTRIES), jnp.int32),
        ),
        name="request",
    )(ids, counts)


def serve_kernel(wanted_ref, keys_ref, values_ref, out_ref, sem):
    def issue(i, _):
        dest = i // CAP
        rank = i % CAP
        rows = pl.ds(pl.multiple_of(wanted_ref[dest, rank] * TILE, TILE), TILE)
        cols = pl.ds(pl.multiple_of(dest * DH, DH), DH)
        pltpu.make_async_copy(keys_ref.at[rows, cols], out_ref.at[i, 0], sem).start()
        pltpu.make_async_copy(values_ref.at[rows, cols], out_ref.at[i, 1], sem).start()
        return 0

    lax.fori_loop(0, MEMS * CAP, issue, 0, unroll=4)
    pltpu.make_async_copy(out_ref, out_ref, sem).wait()


def serve(wanted, keys, values):
    hbm = pl.BlockSpec(memory_space=pl.ANY)
    return pl.pallas_call(
        serve_kernel,
        out_shape=jax.ShapeDtypeStruct((MEMS * CAP, 2, TILE, DH), BF16),
        in_specs=[pl.BlockSpec(memory_space=pltpu.SMEM), hbm, hbm],
        out_specs=hbm,
        scratch_shapes=[pltpu.SemaphoreType.DMA(())],
        cost_estimate=pl.CostEstimate(flops=0, bytes_accessed=12 * MIB, transcendentals=0),
        name="serve",
    )(wanted, keys, values)


def local_kernel(
    tokens_ref, wq_ref, wk_ref, wv_ref, cot_ref, bias_ref,
    queries_ref, out_ref, dq_ref, grad_ref, weights, total,
):
    step = pl.program_id(0)

    @pl.when(step == 0)
    def _():
        weights[:, :DH] = wq_ref[...]
        weights[:, DH : 2 * DH] = wk_ref[...]
        weights[:, 2 * DH :] = wv_ref[...]
        total[...] = jnp.zeros_like(total)

    x = tokens_ref[...]
    qkv = dot(x, weights[...]).astype(BF16)
    q, k, v = qkv[:, :DH], qkv[:, DH : 2 * DH], qkv[:, 2 * DH :]
    queries_ref[...] = q
    gate = gate_row(bias_ref)
    grad = ((1.0 - gate) * cot_ref[...].astype(F32)).astype(BF16)
    half = SEG // 2
    grad_k = []
    grad_v = []
    for part in range(2):
        rows = slice(part * half, (part + 1) * half)
        width = (part + 1) * half
        qs, gs, ks, vs = q[rows], grad[rows], k[:width], v[:width]
        scores = dot(qs, ks, NT) * SCALING
        keep = iota((half, width), 0) + part * half >= iota((half, width), 1)
        scores = jnp.where(keep, scores, -jnp.inf)
        raised = jnp.exp(scores - jnp.max(scores, axis=1, keepdims=True))
        probs = raised * (1.0 / jnp.sum(raised, axis=1, keepdims=True))
        rounded = probs.astype(BF16)
        out_ref[rows, :] = dot(rounded, vs)
        back = dot(gs, vs, NT)
        dscore = probs * (back - jnp.sum(back * probs, axis=1, keepdims=True)) * SCALING
        dround = dscore.astype(BF16)
        dq_ref[rows, :] = dot(dround, ks)
        grad_k.append(dot(dround, qs, TN))
        grad_v.append(dot(rounded, gs, TN))
    low = jnp.concatenate([grad_k[0] + grad_k[1][:half], grad_v[0] + grad_v[1][:half]], axis=1)
    high = jnp.concatenate([grad_k[1][half:], grad_v[1][half:]], axis=1)
    both = jnp.concatenate([low, high], axis=0).astype(BF16)
    total[...] += dot(x, both, TN)

    @pl.when(step == SEGS - 1)
    def _():
        grad_ref[...] = total[...].astype(BF16)


def local_part(tokens, w_query, w_key, w_value, cot, bias):
    seg = lambda width: pl.BlockSpec((SEG, width), lambda i: (i, 0))
    whole = pl.BlockSpec((D, DH), lambda i: (0, 0), pipeline_mode=pl.Buffered(1))
    return pl.pallas_call(
        local_kernel,
        grid=(SEGS,),
        out_shape=(
            jax.ShapeDtypeStruct((TOK, DH), BF16),
            jax.ShapeDtypeStruct((TOK, DH), F32),
            jax.ShapeDtypeStruct((TOK, DH), F32),
            jax.ShapeDtypeStruct((D, 2 * DH), BF16),
        ),
        in_specs=[seg(D), whole, whole, whole, seg(DH), pl.BlockSpec(memory_space=pltpu.SMEM)],
        out_specs=(seg(DH), seg(DH), seg(DH), pl.BlockSpec((D, 2 * DH), lambda i: (0, 0))),
        scratch_shapes=[pltpu.VMEM((D, 3 * DH), BF16), pltpu.VMEM((D, 2 * DH), F32)],
        compiler_params=pltpu.CompilerParams(
            dimension_semantics=("arbitrary",), vmem_limit_bytes=48 * MIB
        ),
        cost_estimate=pl.CostEstimate(
            flops=14_000_000_000, bytes_accessed=20 * MIB, transcendentals=1_600_000
        ),
        name="local",
    )(tokens, w_query, w_key, w_value, cot, bias)


def memory_kernel(
    counts_ref, slot_ref, bias_ref, tiles_ref, queries_ref, local_ref, ldq_ref, cot_ref, tokens_ref,
    attended_ref, grad_ref, tiles, total, grads, gate_sum, sems,
):
    step = pl.program_id(0)
    per_step = SEG // QB

    @pl.when(step == 0)
    def _():
        total[...] = jnp.zeros_like(total)
        gate_sum[...] = jnp.zeros_like(gate_sum)

        def issue(i, _):
            live = i % TOP < counts_ref[0, i // TOP]

            @pl.when(live)
            def _():
                pltpu.make_async_copy(tiles_ref.at[slot_ref[0, i]], tiles.at[i], sems.at[i]).start()

            @pl.when(jnp.logical_not(live))
            def _():
                tiles[i] = jnp.zeros((2, TILE, DH), BF16)

            return 0

        lax.fori_loop(0, ENTRIES, issue, 0)

    def arrive(i, _):
        entry = step * (per_step * TOP) + i

        @pl.when(entry % TOP < counts_ref[0, entry // TOP])
        def _():
            pltpu.make_async_copy(tiles_ref.at[0], tiles.at[entry], sems.at[entry]).wait()

        return 0

    lax.fori_loop(0, per_step * TOP, arrive, 0)
    gate = gate_row(bias_ref)
    terms = jnp.zeros((1, DH), F32)
    for part in range(per_step):
        rows = slice(part * QB, (part + 1) * QB)
        block = step * per_step + part
        entries = pl.ds(block * TOP, TOP)
        keys = tiles[entries, 0].reshape(TOP * TILE, DH)
        values = tiles[entries, 1].reshape(TOP * TILE, DH)
        up = cot_ref[rows, :].astype(F32)
        local = local_ref[rows, :]
        scores = dot(queries_ref[rows, :], keys, NT) * SCALING
        live = iota((QB, TOP * TILE), 1) < counts_ref[0, block] * TILE
        scores = jnp.where(live, scores, -jnp.inf)
        raised = jnp.exp(scores - jnp.max(scores, axis=1, keepdims=True))
        probs = raised * (1.0 / jnp.sum(raised, axis=1, keepdims=True))
        out = dot(probs.astype(BF16), values)
        back = dot((gate * up).astype(BF16), values, NT)
        dscore = probs * (back - jnp.sum(back * probs, axis=1, keepdims=True)) * SCALING
        dq = dot(dscore.astype(BF16), keys)
        attended_ref[rows, :] = (gate * out + (1.0 - gate) * local).astype(BF16)
        terms += jnp.sum(up * (out - local), axis=0, keepdims=True)
        grads[rows, :] = (dq + ldq_ref[rows, :]).astype(BF16)
    gate_sum[...] += terms
    total[...] += dot(tokens_ref[...], grads[...], TN)

    @pl.when(step == SEGS - 1)
    def _():
        grad_ref[:, :ROWS_OUT, :] = total[...].astype(BF16).reshape(8, ROWS_OUT, DH)
        term = gate_sum[...]
        high = term.astype(BF16)
        rest = term - high.astype(F32)
        mid = rest.astype(BF16)
        low = (rest - mid.astype(F32)).astype(BF16)
        at = iota((GATE_ROWS, DH), 0)
        spread = lambda row: jnp.broadcast_to(row.astype(F32), (GATE_ROWS, DH))
        extra = jnp.where(at == 0, spread(high), jnp.where(at == 1, spread(mid), spread(low)))
        extra = jnp.where(at < 3, extra, 0.0).astype(BF16)
        for owner in range(8):
            grad_ref[owner, ROWS_OUT:, :] = extra


def memory_part(counts, slots, bias, tiles, queries, local, ldq, cot, tokens):
    seg = lambda width: pl.BlockSpec((SEG, width), lambda i: (i, 0))
    smem = pl.BlockSpec(memory_space=pltpu.SMEM)
    rows = ROWS_OUT + GATE_ROWS
    return pl.pallas_call(
        memory_kernel,
        grid=(SEGS,),
        out_shape=(
            jax.ShapeDtypeStruct((TOK, DH), BF16),
            jax.ShapeDtypeStruct((8, rows, DH), BF16),
        ),
        in_specs=[smem, smem, smem, pl.BlockSpec(memory_space=pl.ANY), seg(DH), seg(DH), seg(DH), seg(DH), seg(D)],
        out_specs=(seg(DH), pl.BlockSpec((8, rows, DH), lambda i: (0, 0, 0))),
        scratch_shapes=[
            pltpu.VMEM((ENTRIES, 2, TILE, DH), BF16),
            pltpu.VMEM((D, DH), F32),
            pltpu.VMEM((SEG, DH), BF16),
            pltpu.VMEM((1, DH), F32),
            pltpu.SemaphoreType.DMA((ENTRIES,)),
        ],
        compiler_params=pltpu.CompilerParams(
            dimension_semantics=("arbitrary",), vmem_limit_bytes=48 * MIB
        ),
        cost_estimate=pl.CostEstimate(
            flops=8_000_000_000, bytes_accessed=24 * MIB, transcendentals=1_600_000
        ),
        name="memory",
    )(counts, slots, bias, tiles, queries, local, ldq, cot, tokens)


def exchange(array, axis):
    return lax.all_to_all(array, axis, split_axis=0, concat_axis=0, tiled=True)


def on_device(
    tokens,
    w_query,
    w_key,
    w_value,
    gate_bias,
    memory_keys,
    memory_values,
    retrieval_ids,
    retrieval_counts,
    cotangent,
):
    hidden = tokens[0]
    cot = cotangent[0]
    counts = retrieval_counts.reshape(1, NQB)
    table, slots = make_requests(retrieval_ids.reshape(NQB, TOP), counts)
    wanted = exchange(table, "mem")
    sent = serve(wanted, memory_keys[0], memory_values[0])
    hidden, sent = lax.optimization_barrier((hidden, sent))
    tiles = exchange(sent, "mem")
    queries, local, ldq, grad_kv = local_part(hidden, w_query, w_key, w_value, cot, gate_bias)
    shares_kv = exchange(grad_kv.reshape(8, ROWS_OUT, 2 * DH), "dp")
    sum_kv = jnp.sum(shares_kv.astype(F32), axis=0)
    attended, grad_q = memory_part(
        counts, slots, gate_bias, tiles, queries, local, ldq, cot, hidden
    )
    shares_q = exchange(grad_q, "dp").astype(F32)
    share_q = jnp.sum(shares_q[:, :ROWS_OUT], axis=0)
    gate = jax.nn.sigmoid(gate_bias)
    gate_total = jnp.sum(shares_q[:, ROWS_OUT : ROWS_OUT + 3]) * gate * (1.0 - gate)
    return (attended[None], share_q, sum_kv[:, :DH], sum_kv[:, DH:], gate_total)


def solution(mesh):
    return jax.shard_map(
        on_device,
        mesh=mesh,
        in_specs=(
            P("dp", None, None),
            P(None, "mem"),
            P(None, "mem"),
            P(None, "mem"),
            P("mem"),
            P("dp", "mem", None),
            P("dp", "mem", None),
            P("dp", "mem", None, None),
            P("dp", "mem", None),
            P("dp", None, "mem"),
        ),
        out_specs=(P("dp", None, "mem"), P("dp", "mem"), P("dp", "mem"), P("dp", "mem"), P("mem")),
        check_vma=False,
    )
```

profile of v0, /device:TPU:1, one launch (start us, length us, event | category | flops | bytes accessed | tf_op | source)
XLA Modules:
  0.0 364.4 jit_solution(4346258517811575303)
XLA Ops:
  0.6 1.4 copy.16
  2.0 1.8 request.1
  3.8 13.9 %all_to_all.26 = s32[16,1,128]{2,1,0:T(1,128)} all-to-all(s32[16,1,128]{2,1,0:T(1,128)} %bitcast.21), channel_id=1, replica_groups=mesh['dp'=8,'mem'=16] {'mem'}, dimensions={0} | all-to-all | bytes 16384 | tf_op jit(solution)/shard_map/all_to_all | solution.py:296
  17.6 192.5 %serve.1 = bf16[192,2,64,128]{3,2,1,0:T(8,128)(2,1)} custom-call(s32[16,128]{1,0:T(8,128)} %bitcast.20, bf16[1536,2048]{1,0:T(8,128)(2,1)} %bitcast.17, bf16[1536,2048]{1,0:T(8,128)(2,1)} %bitcast.18), custom_call_target="tpu_custom_call" | custom-call | bytes 12582912 | tf_op jit(solution)/shard_map/serve/pallas_call | solution.py:102
  210.1 0.0 copy-start.1
  210.1 0.0 copy-start.2
  210.2 0.0 copy-start.3
  210.2 0.0 copy-start.4
  210.2 4.8 %all-to-all-start.1 = ((bf16[192,2,64,128]{3,2,1,0:T(8,128)(2,1)}), bf16[192,2,64,128]{3,2,1,0:T(8,128)(2,1)}, u32[]{:S(2)}, u32[]{:S(2)}) async-start(bf16[192,2,64,128]{3,2,1,0:T(8,128)(2,1)} %serve.1), calls=%async_computation.1 | async-start | bytes 12582912 | tf_op jit(solution)/shard_map/all_to_all | solution.py:296
  215.6 0.0 copy-done.1
  215.6 0.0 copy-done.2
  215.6 0.0 copy-done.3
  215.6 0.0 copy-done.4
  215.7 24.0 %local.1 = (bf16[3072,128]{1,0:T(8,128)(2,1)S(1)}, f32[3072,128]{1,0:T(8,128)S(1)}, f32[3072,128]{1,0:T(8,128)}, bf16[2048,256]{1,0:T(8,128)(2,1)}) custom-call(bf16[3072,2048]{1,0:T(8,128)(2,1)} %bitcast.22, bf16[2048,128]{1,0:T(8,128)(2,1)S(1)} %copy-done.2, bf16[2048,128]{1,0:T(8,128)(2,1)S(1)} %copy-done.3, bf16[2048,128]{1,0:T(8,128)(2,1)S(1)} %copy-done.4, ...), custom_call_target="tpu_custom_call" | custom-call | flops 14000000000 | bytes 20971520 | tf_op jit(solution)/shard_map/local/pallas_call | solution.py:165
  239.7 0.0 copy-start.6
  239.7 1.1 copy-done.6
  240.8 0.0 copy-start
  240.8 0.0 copy-start.5
  240.8 64.1 %all-to-all-done.1.tiles_ref = bf16[192,2,64,128]{3,2,1,0:T(8,128)(2,1)} async-done(((bf16[192,2,64,128]{3,2,1,0:T(8,128)(2,1)}), bf16[192,2,64,128]{3,2,1,0:T(8,128)(2,1)}, u32[]{:S(2)}, u32[]{:S(2)}) %all-to-all-start.1) | async-done | bytes 6291488 | tf_op jit(solution)/shard_map/all_to_all | solution.py:296
  304.9 0.0 copy-start.7
  304.9 8.6 %all-to-all-start.3 = ((bf16[8,256,256]{2,1,0:T(8,128)(2,1)}), bf16[8,256,256]{2,1,0:T(8,128)(2,1)}, u32[]{:S(2)}, u32[]{:S(2)}) async-start(bf16[8,256,256]{2,1,0:T(8,128)(2,1)} %bitcast.10), calls=%async_computation.3 | async-start | bytes 2097152 | tf_op jit(solution)/shard_map/all_to_all | solution.py:296
  313.5 0.0 copy-done
  313.5 0.0 copy-done.5
  313.5 0.0 copy-done.7
  313.5 0.0 copy-start.8
  313.5 1.4 copy-done.8
  314.9 31.8 %memory.1 = (bf16[3072,128]{1,0:T(8,128)(2,1)}, bf16[8,272,128]{2,1,0:T(8,128)(2,1)}) custom-call(s32[1,24]{1,0:T(1,128)S(1)} %bitcast.14, s32[1,192]{1,0:T(1,128)S(1)} %copy-done.5, f32[1]{0:T(128)S(6)} %copy.18.bias_ref, bf16[192,2,64,128]{3,2,1,0:T(8,128)(2,1)} %all-to-all-done.1.tiles_ref, bf16[3072,128]{1,0:T(8,128)(2,1)S(1)} %get-tuple-element.19.queries_ref, ...), custom_call_target="tpu_custom_call" | custom-call | flops 8000000000 | bytes 25165824 | tf_op jit(solution)/shard_map/memory/pallas_call | solution.py:269
  346.7 0.0 all-to-all-done.3
  346.7 4.7 %all-to-all-start.2 = ((bf16[8,272,128]{2,1,0:T(8,128)(2,1)}), bf16[8,272,128]{2,1,0:T(8,128)(2,1)S(1)}, u32[]{:S(2)}, u32[]{:S(2)}) async-start(bf16[8,272,128]{2,1,0:T(8,128)(2,1)} %get-tuple-element.23), calls=%async_computation.2 | async-start | bytes 1114112 | tf_op jit(solution)/shard_map/all_to_all | solution.py:296
  351.5 1.4 convert_reduce_fusion
  352.9 0.7 fusion
  353.6 7.6 %all-to-all-done.2 = bf16[8,272,128]{2,1,0:T(8,128)(2,1)S(1)} async-done(((bf16[8,272,128]{2,1,0:T(8,128)(2,1)}), bf16[8,272,128]{2,1,0:T(8,128)(2,1)S(1)}, u32[]{:S(2)}, u32[]{:S(2)}) %all-to-all-start.2) | async-done | bytes 557088 | tf_op jit(solution)/shard_map/all_to_all | solution.py:296
  361.2 0.1 convert_element_type.6
  361.3 0.7 slice_reduce_fusion
  362.0 0.6 slice_reduce_fusion.1
Async XLA Ops:
  210.1 5.5 %copy-start.1 = (bf16[1,3072,128]{2,1,0:T(8,128)(2,1)S(1)}, bf16[1,3072,128]{2,1,0:T(8,128)(2,1)}, u32[]{:S(2)}) copy-start(bf16[1,3072,128]{2,1,0:T(8,128)(2,1)} %param.19) | copy-start | bytes 2359300
  210.1 5.5 %copy-start.2 = (bf16[2048,128]{1,0:T(8,128)(2,1)S(1)}, bf16[2048,128]{1,0:T(8,128)(2,1)}, u32[]{:S(2)}) copy-start(bf16[2048,128]{1,0:T(8,128)(2,1)} %wq_ref.1) | copy-start | bytes 1572868
  210.2 5.5 %copy-start.3 = (bf16[2048,128]{1,0:T(8,128)(2,1)S(1)}, bf16[2048,128]{1,0:T(8,128)(2,1)}, u32[]{:S(2)}) copy-start(bf16[2048,128]{1,0:T(8,128)(2,1)} %wk_ref.1) | copy-start | bytes 1572868
  210.2 5.5 %copy-start.4 = (bf16[2048,128]{1,0:T(8,128)(2,1)S(1)}, bf16[2048,128]{1,0:T(8,128)(2,1)}, u32[]{:S(2)}) copy-start(bf16[2048,128]{1,0:T(8,128)(2,1)} %wv_ref.1) | copy-start | bytes 1572868
  210.2 94.7 %all-to-all-start.1 = ((bf16[192,2,64,128]{3,2,1,0:T(8,128)(2,1)}), bf16[192,2,64,128]{3,2,1,0:T(8,128)(2,1)}, u32[]{:S(2)}, u32[]{:S(2)}) async-start(bf16[192,2,64,128]{3,2,1,0:T(8,128)(2,1)} %serve.1), calls=%async_computation.1 | async-start | bytes 12582912 | tf_op jit(solution)/shard_map/all_to_all | solution.py:296
  239.7 1.1 copy-start.6
  240.8 72.7 %copy-start = (s32[1,1,24]{2,1,0:T(1,128)S(1)}, s32[1,1,24]{2,1,0:T(1,128)}, u32[]{:S(2)}) copy-start(s32[1,1,24]{2,1,0:T(1,128)} %param.18) | copy-start | bytes 292
  240.8 72.7 %copy-start.5 = (s32[1,192]{1,0:T(1,128)S(1)}, s32[1,192]{1,0:T(1,128)}, u32[]{:S(2)}) copy-start(s32[1,192]{1,0:T(1,128)} %get-tuple-element.15.slot_ref) | copy-start | bytes 2308
  304.9 8.6 %copy-start.7 = (f32[3072,128]{1,0:T(8,128)S(1)}, f32[3072,128]{1,0:T(8,128)}, u32[]{:S(2)}) copy-start(f32[3072,128]{1,0:T(8,128)} %copy-done.6) | copy-start | bytes 4718596
  304.9 41.8 %all-to-all-start.3 = ((bf16[8,256,256]{2,1,0:T(8,128)(2,1)}), bf16[8,256,256]{2,1,0:T(8,128)(2,1)}, u32[]{:S(2)}, u32[]{:S(2)}) async-start(bf16[8,256,256]{2,1,0:T(8,128)(2,1)} %bitcast.10), calls=%async_computation.3 | async-start | bytes 2097152 | tf_op jit(solution)/shard_map/all_to_all | solution.py:296
  313.5 1.4 copy-start.8
  346.7 14.5 %all-to-all-start.2 = ((bf16[8,272,128]{2,1,0:T(8,128)(2,1)}), bf16[8,272,128]{2,1,0:T(8,128)(2,1)S(1)}, u32[]{:S(2)}, u32[]{:S(2)}) async-start(bf16[8,272,128]{2,1,0:T(8,128)(2,1)} %get-tuple-element.23), calls=%async_computation.2 | async-start | bytes 1114112 | tf_op jit(solution)/shard_map/all_to_all | solution.py:296
where the time goes:
time: 365 us; the launch traced here: 364 us
  Pallas kernels  250 us (68%)
  waiting for transfers between devices  71.7 us (20%)
  starting transfers between devices  18 us (5%)
  blocking collectives  13.9 us (4%)
  local copies, waits for them, and re-layouts  4.65 us (1%)
    pallas_call x1, Pallas kernels, serve(): pl.pallas_call(serve_kernel, out_shape=jax.ShapeDtypeStruct((MEMS * CAP,...  192 us
    all_to_all x3, waiting for transfers between devices, exchange(): return lax.all_to_all(array, axis, split_axis=0, concat_axis=0, tiled=True)  71.7 us
    pallas_call x1, Pallas kernels, memory_part(): pl.pallas_call(memory_kernel, grid=(SEGS,), out_shape=(jax.ShapeDtypeStru...  31.8 us
    pallas_call x1, Pallas kernels, local_part(): pl.pallas_call(local_kernel, grid=(SEGS,), out_shape=(jax.ShapeDtypeStruc...  24 us
    all_to_all x3, starting transfers between devices, exchange(): return lax.all_to_all(array, axis, split_axis=0, concat_axis=0, tiled=True)  18 us
    all_to_all x1, blocking collectives, exchange(): return lax.all_to_all(array, axis, split_axis=0, concat_axis=0, tiled=True)  13.9 us
  transfers between devices with their start and end apart: 3, of which 2 were waited for; matrix products, arithmetic and copies ran while one was open for 1% of the time, Pallas kernels for 15%

commit v1 on v0

v1 whole, which is shorter than its diff:
```python
import functools

import jax
import jax.numpy as jnp
from jax import lax
from jax.experimental import pallas as pl
from jax.experimental.pallas import tpu as pltpu
from jax.sharding import PartitionSpec as P

DH = 128
SEG = 512
QB = 128
TILE = 64
TOP = 8
SEGS = 6
TILES_DEV = 24
TOK = 3072
NQB = 24
CAP = 12
MEMS = 16
SIDE = 4
D = 2048
ENTRIES = NQB * TOP
SCALING = DH ** (-0.5)
ROWS_OUT = D // 8
GATE_ROWS = 16
ZS = 4
LOCAL_SEGS = 2
FIRST = (1, 4, 3, 12)
REST = (5, 15, 7, 13, 2, 8, 6, 14, 9, 11, 10, 0)
F32 = jnp.float32
BF16 = jnp.bfloat16
MIB = 1 << 20

NT = (((1,), (1,)), ((), ()))
TN = (((0,), (0,)), ((), ()))


def dot(a, b, dims=(((1,), (0,)), ((), ()))):
    return lax.dot_general(a, b, dims, preferred_element_type=F32)


def iota(shape, dim):
    return lax.broadcasted_iota(jnp.int32, shape, dim)


def gate_row(bias_ref):
    return 1.0 / (1.0 + jnp.exp(-jnp.full((1, DH), bias_ref[0], F32)))


def request_kernel(ids_ref, counts_ref, table_ref, entry_ref):
    ids = ids_ref[...]
    owner = (ids // TILES_DEV).astype(F32)
    local = (ids % TILES_DEV).astype(F32)
    counts = counts_ref[...].astype(F32)
    by_block = (iota((ENTRIES, NQB), 0) // TOP == iota((ENTRIES, NQB), 1)).astype(F32)
    pick = (iota((ENTRIES, TOP), 0) % TOP == iota((ENTRIES, TOP), 1)).astype(F32)
    owner_col = jnp.sum(dot(by_block, owner) * pick, axis=1, keepdims=True)
    local_col = jnp.sum(dot(by_block, local) * pick, axis=1, keepdims=True)
    count_col = jnp.sum(by_block * counts, axis=1, keepdims=True)
    slot_col = (iota((ENTRIES, 1), 0) % TOP).astype(F32)
    owner_col = jnp.where(slot_col < count_col, owner_col, float(MEMS))
    of_block = (iota((NQB, ENTRIES), 1) // TOP == iota((NQB, ENTRIES), 0)).astype(F32)
    of_slot = (iota((TOP, ENTRIES), 1) % TOP == iota((TOP, ENTRIES), 0)).astype(F32)
    owner_row = jnp.sum(dot(owner, of_slot) * of_block, axis=0, keepdims=True)
    count_row = dot(jnp.broadcast_to(counts, (8, NQB)), of_block)[:1]
    slot_row = (iota((1, ENTRIES), 1) % TOP).astype(F32)
    owner_row = jnp.where(slot_row < count_row, owner_row, float(MEMS))
    earlier = iota((ENTRIES, ENTRIES), 1) < iota((ENTRIES, ENTRIES), 0)
    rank_col = jnp.sum(((owner_col == owner_row) & earlier).astype(F32), axis=1, keepdims=True)
    sends = (owner_row == iota((MEMS, ENTRIES), 0).astype(F32)).astype(F32)
    lane = iota((ENTRIES, 128), 1).astype(F32)
    entry_col = iota((ENTRIES, 1), 0).astype(F32) + 1.0
    table_ref[...] = dot(sends, jnp.where(rank_col == lane, local_col, 0.0)).astype(jnp.int32)
    entry_ref[...] = dot(sends, jnp.where(rank_col == lane, entry_col, 0.0)).astype(jnp.int32)


def make_requests(ids, counts):
    return pl.pallas_call(
        request_kernel,
        out_shape=(
            jax.ShapeDtypeStruct((MEMS, 128), jnp.int32),
            jax.ShapeDtypeStruct((MEMS, 128), jnp.int32),
        ),
        name="request",
    )(ids, counts)


def peer(offset, sign):
    me = lax.axis_index("mem")
    row = lax.rem(me // SIDE + sign * (offset // SIDE) + SIDE, SIDE)
    col = lax.rem(lax.rem(me, SIDE) + sign * (offset % SIDE) + SIDE, SIDE)
    return row * SIDE + col


def serve_kernel(offsets, wanted_ref, keys_ref, values_ref, *refs):
    outs = refs[: len(offsets)]
    held, load_sems, store_sem = refs[len(offsets) :]
    for at, offset in enumerate(offsets):
        dest = peer(offset, 1)
        cols = pl.ds(pl.multiple_of(dest * DH, DH), DH)
        sem = load_sems.at[at]

        def issue(rank, _):
            rows = pl.ds(pl.multiple_of(wanted_ref[dest, rank] * TILE, TILE), TILE)
            pltpu.make_async_copy(keys_ref.at[rows, cols], held.at[at, rank, 0], sem).start()
            pltpu.make_async_copy(values_ref.at[rows, cols], held.at[at, rank, 1], sem).start()
            return 0

        lax.fori_loop(0, CAP, issue, 0, unroll=4)
    for at, out_ref in enumerate(outs):
        pltpu.make_async_copy(out_ref, held.at[at], load_sems.at[at]).wait()
        pltpu.make_async_copy(held.at[at], out_ref, store_sem.at[at]).start()
    for at, out_ref in enumerate(outs):
        pltpu.make_async_copy(held.at[at], out_ref, store_sem.at[at]).wait()


def serve(offsets, wanted, keys, values):
    hbm = pl.BlockSpec(memory_space=pl.ANY)
    n = len(offsets)
    return pl.pallas_call(
        functools.partial(serve_kernel, offsets),
        out_shape=[jax.ShapeDtypeStruct((CAP, 2, TILE, DH), BF16)] * n,
        in_specs=[pl.BlockSpec(memory_space=pltpu.SMEM), hbm, hbm],
        out_specs=[hbm] * n,
        scratch_shapes=[
            pltpu.VMEM((n, CAP, 2, TILE, DH), BF16),
            pltpu.SemaphoreType.DMA((n,)),
            pltpu.SemaphoreType.DMA((n,)),
        ],
        compiler_params=pltpu.CompilerParams(vmem_limit_bytes=48 * MIB),
        cost_estimate=pl.CostEstimate(flops=0, bytes_accessed=n * MIB, transcendentals=0),
        name="serve",
    )(wanted, keys, values)


def local_kernel(
    tokens_ref, wq_ref, wk_ref, wv_ref, cot_ref, bias_ref, *refs
):
    before_ref = refs[0] if len(refs) == 6 else None
    queries_ref, out_ref, dq_ref, total, weights = refs[-5:]
    step = pl.program_id(0)

    @pl.when(step == 0)
    def _():
        weights[:, :DH] = wq_ref[...]
        weights[:, DH : 2 * DH] = wk_ref[...]
        weights[:, 2 * DH :] = wv_ref[...]
        total[...] = jnp.zeros_like(total) if before_ref is None else before_ref[...]

    x = tokens_ref[...]
    qkv = dot(x, weights[...]).astype(BF16)
    q, k, v = qkv[:, :DH], qkv[:, DH : 2 * DH], qkv[:, 2 * DH :]
    queries_ref[...] = q
    gate = gate_row(bias_ref)
    grad = ((1.0 - gate) * cot_ref[...].astype(F32)).astype(BF16)
    half = SEG // 2
    grad_k = []
    grad_v = []
    for part in range(2):
        rows = slice(part * half, (part + 1) * half)
        width = (part + 1) * half
        qs, gs, ks, vs = q[rows], grad[rows], k[:width], v[:width]
        scores = dot(qs, ks, NT) * SCALING
        keep = iota((half, width), 0) + part * half >= iota((half, width), 1)
        scores = jnp.where(keep, scores, -jnp.inf)
        raised = jnp.exp(scores - jnp.max(scores, axis=1, keepdims=True))
        probs = raised * (1.0 / jnp.sum(raised, axis=1, keepdims=True))
        rounded = probs.astype(BF16)
        out_ref[rows, :] = dot(rounded, vs)
        back = dot(gs, vs, NT)
        dscore = probs * (back - jnp.sum(back * probs, axis=1, keepdims=True)) * SCALING
        dround = dscore.astype(BF16)
        dq_ref[rows, :] = dot(dround, ks)
        grad_k.append(dot(dround, qs, TN))
        grad_v.append(dot(rounded, gs, TN))
    low = jnp.concatenate([grad_k[0] + grad_k[1][:half], grad_v[0] + grad_v[1][:half]], axis=1)
    high = jnp.concatenate([grad_k[1][half:], grad_v[1][half:]], axis=1)
    both = jnp.concatenate([low, high], axis=0).astype(BF16)
    total[...] += dot(x, both, TN)


def local_part(start, count, tokens, w_query, w_key, w_value, cot, bias, before):
    seg_in = lambda width: pl.BlockSpec((SEG, width), lambda i: (i + start, 0))
    seg = lambda width: pl.BlockSpec((SEG, width), lambda i: (i, 0))
    once = lambda width: pl.BlockSpec((D, width), lambda i: (0, 0), pipeline_mode=pl.Buffered(1))
    given = () if before is None else (before,)
    return pl.pallas_call(
        local_kernel,
        grid=(count,),
        out_shape=(
            jax.ShapeDtypeStruct((SEG * count, DH), BF16),
            jax.ShapeDtypeStruct((SEG * count, DH), F32),
            jax.ShapeDtypeStruct((SEG * count, DH), F32),
            jax.ShapeDtypeStruct((D, 2 * DH), F32),
        ),
        in_specs=[
            seg_in(D), once(DH), once(DH), once(DH), seg_in(DH), pl.BlockSpec(memory_space=pltpu.SMEM)
        ] + [once(2 * DH)] * len(given),
        out_specs=(seg(DH), seg(DH), seg(DH), once(2 * DH)),
        scratch_shapes=[pltpu.VMEM((D, 3 * DH), BF16)],
        compiler_params=pltpu.CompilerParams(
            dimension_semantics=("arbitrary",), vmem_limit_bytes=32 * MIB
        ),
        cost_estimate=pl.CostEstimate(
            flops=2_400_000_000 * count, bytes_accessed=3 * count * MIB, transcendentals=270_000 * count
        ),
        name="local",
    )(tokens, w_query, w_key, w_value, cot, bias, *given)


CLASSES = ((2, 4), (4, 3), (8, 2))


def attend(block, valid, tiles_n, refs):
    count, gate, tiles, queries_ref, local_ref, ldq_ref, cot_ref, attended_ref, grads = refs
    width = tiles_n * TILE
    rows = pl.ds(pl.multiple_of(block * QB, QB), QB)
    entries = pl.ds(block * TOP, tiles_n)
    keys = tiles[entries, 0].reshape(width, DH)
    values = tiles[entries, 1].reshape(width, DH)
    up = cot_ref[rows, :].astype(F32)
    local = local_ref[rows, :]
    scores = dot(queries_ref[rows, :], keys, NT) * SCALING
    back = dot((gate * up).astype(BF16), values, NT)
    scores = jnp.where(iota((QB, width), 1) < count * TILE, scores, -jnp.inf)
    raised = jnp.exp(scores - jnp.max(scores, axis=1, keepdims=True))
    probs = raised * (1.0 / jnp.sum(raised, axis=1, keepdims=True))
    out = dot(probs.astype(BF16), values)
    dscore = probs * (back - jnp.sum(back * probs, axis=1, keepdims=True)) * SCALING
    dq = dot(dscore.astype(BF16), keys)
    attended_ref[rows, :] = (gate * out + (1.0 - gate) * local).astype(BF16)
    grads[rows, :] = (dq + ldq_ref[rows, :]).astype(BF16)
    term = jnp.sum(up * (out - local), axis=0, keepdims=True)
    return jnp.where(valid, term, 0.0)


def memory_kernel(counts_ref, entry_ref, bias_ref, *refs):
    tile_refs = refs[:MEMS]
    queries_ref, local_ref, ldq_ref, cot_ref, tokens_ref = refs[MEMS : MEMS + 5]
    attended_ref, mine_ref, other_ref = refs[MEMS + 5 : MEMS + 8]
    tiles, tokens, total, grads, gate_sum, lists, sems, token_sems = refs[MEMS + 8 :]

    for offset in range(MEMS):
        source = peer(offset, -1)

        def issue(rank, _):
            entry = entry_ref[source, rank] - 1

            @pl.when(entry >= 0)
            def _():
                pltpu.make_async_copy(
                    tile_refs[offset].at[rank], tiles.at[entry], sems.at[entry]
                ).start()

            return 0

        lax.fori_loop(0, CAP, issue, 0)
    for part in range(SEGS):
        rows = pl.ds(part * SEG, SEG)
        pltpu.make_async_copy(tokens_ref.at[rows], tokens.at[rows], token_sems.at[part]).start()

    def sort(block, sizes):
        count = counts_ref[0, block]
        sizes = list(sizes)
        low = 0
        for at, (tiles_n, _) in enumerate(CLASSES):
            here = (count > low) & (count <= tiles_n)

            @pl.when(here)
            def _(at=at, tiles_n=tiles_n):
                lists[at, sizes[at]] = block

                def clear(slot, _):
                    tiles[block * TOP + slot] = jnp.zeros((2, TILE, DH), BF16)
                    return 0

                lax.fori_loop(count, tiles_n, clear, 0)

            sizes[at] = sizes[at] + here.astype(jnp.int32)
            low = tiles_n
        return tuple(sizes)

    sizes = lax.fori_loop(0, NQB, sort, (jnp.int32(0),) * len(CLASSES))
    gate = gate_row(bias_ref)
    gate_sum[...] = jnp.zeros_like(gate_sum)
    for at, (tiles_n, group) in enumerate(CLASSES):

        def batch(i, _, at=at, tiles_n=tiles_n, group=group):
            members = []
            for k in range(group):
                valid = i * group + k < sizes[at]
                block = lists[at, jnp.minimum(i * group + k, sizes[at] - 1)]
                count = counts_ref[0, block]
                members.append((block, valid, count))

                def arrive(slot, _):
                    entry = block * TOP + slot
                    pltpu.make_async_copy(
                        tile_refs[0].at[0], tiles.at[entry], sems.at[entry]
                    ).wait()
                    return 0

                lax.fori_loop(0, jnp.where(valid, count, 0), arrive, 0)
            terms = jnp.zeros((1, DH), F32)
            for block, valid, count in members:
                terms += attend(
                    block, valid, tiles_n,
                    (count, gate, tiles, queries_ref, local_ref, ldq_ref, cot_ref, attended_ref, grads),
                )
            gate_sum[...] += terms
            return 0

        lax.fori_loop(0, pl.cdiv(sizes[at], group), batch, 0)
    for part in range(SEGS):
        rows = pl.ds(part * SEG, SEG)
        pltpu.make_async_copy(tokens_ref.at[rows], tokens.at[rows], token_sems.at[part]).wait()
        term = dot(grads[rows, :], tokens[rows, :], TN)
        if part == 0:
            total[...] = term
        else:
            total[...] += term
    turned = total[...].T
    core = lax.rem(lax.axis_index("dp"), 2)
    extra = split_gate(gate_sum[...])
    for z in range(ZS):
        low = turned[2 * z * ROWS_OUT : (2 * z + 1) * ROWS_OUT]
        high = turned[(2 * z + 1) * ROWS_OUT : (2 * z + 2) * ROWS_OUT]
        mine_ref[z, :ROWS_OUT, :] = jnp.where(core == 0, low, high)
        mine_ref[z, ROWS_OUT:, :] = extra.astype(F32)
        other_ref[z, :ROWS_OUT, :] = jnp.where(core == 0, high, low).astype(BF16)
        other_ref[z, ROWS_OUT:, :] = extra


def split_gate(term):
    high = term.astype(BF16)
    rest = term - high.astype(F32)
    mid = rest.astype(BF16)
    low = (rest - mid.astype(F32)).astype(BF16)
    at = iota((GATE_ROWS, DH), 0)
    spread = lambda row: jnp.broadcast_to(row.astype(F32), (GATE_ROWS, DH))
    extra = jnp.where(at == 0, spread(high), jnp.where(at == 1, spread(mid), spread(low)))
    return jnp.where(at < 3, extra, 0.0).astype(BF16)


def memory_part(counts, entries, bias, tiles, queries, local, ldq, cot, tokens):
    smem = pl.BlockSpec(memory_space=pltpu.SMEM)
    vmem = pl.BlockSpec(memory_space=pltpu.VMEM)
    hbm = pl.BlockSpec(memory_space=pl.ANY)
    rows = ROWS_OUT + GATE_ROWS
    return pl.pallas_call(
        memory_kernel,
        out_shape=(
            jax.ShapeDtypeStruct((TOK, DH), BF16),
            jax.ShapeDtypeStruct((ZS, rows, DH), F32),
            jax.ShapeDtypeStruct((ZS, rows, DH), BF16),
        ),
        in_specs=[smem] * 3 + [hbm] * MEMS + [vmem] * 4 + [hbm],
        out_specs=(vmem, vmem, vmem),
        scratch_shapes=[
            pltpu.VMEM((ENTRIES, 2, TILE, DH), BF16),
            pltpu.VMEM((TOK, D), BF16),
            pltpu.VMEM((DH, D), F32),
            pltpu.VMEM((TOK, DH), BF16),
            pltpu.VMEM((1, DH), F32),
            pltpu.SMEM((len(CLASSES), 32), jnp.int32),
            pltpu.SemaphoreType.DMA((ENTRIES,)),
            pltpu.SemaphoreType.DMA((SEGS,)),
        ],
        compiler_params=pltpu.CompilerParams(vmem_limit_bytes=40 * MIB),
        cost_estimate=pl.CostEstimate(
            flops=8_000_000_000, bytes_accessed=24 * MIB, transcendentals=1_600_000
        ),
        name="memory",
    )(counts, entries, bias, *tiles, queries, local, ldq, cot, tokens)


def pair_kernel(mine_ref, got_ref, *outs):
    z = lax.axis_index("dp") // 2
    for step in range(ZS):
        at = lax.rem(z + step, ZS)
        both = mine_ref[at] + got_ref[at].astype(F32)
        gate = jnp.sum(both[ROWS_OUT : ROWS_OUT + 3], axis=0, keepdims=True)
        extra = split_gate(gate)
        outs[step][:ROWS_OUT, :] = both[:ROWS_OUT].astype(outs[step].dtype)
        outs[step][ROWS_OUT:, :] = extra.astype(outs[step].dtype)


def pair_sum(mine, got):
    rows = mine.shape[1:]
    return pl.pallas_call(
        pair_kernel,
        out_shape=[jax.ShapeDtypeStruct(rows, F32)] + [jax.ShapeDtypeStruct(rows, BF16)] * (ZS - 1),
        name="pair",
    )(mine, got)


def last_kernel(bias_ref, own_ref, one_ref, two_ref, three_ref, share_ref, gate_ref):
    sums = own_ref[...] + one_ref[...].astype(F32) + two_ref[...].astype(F32) + three_ref[...].astype(F32)
    share_ref[...] = sums[:ROWS_OUT]
    gate = gate_row(bias_ref)
    term = jnp.sum(sums[ROWS_OUT : ROWS_OUT + 3], axis=0, keepdims=True)
    whole = jnp.sum(term, axis=1, keepdims=True)
    gate_ref[...] = jnp.broadcast_to(whole, (1, DH)) * gate * (1.0 - gate)


def last_sum(bias, parts):
    vmem = pl.BlockSpec(memory_space=pltpu.VMEM)
    return pl.pallas_call(
        last_kernel,
        out_shape=(jax.ShapeDtypeStruct((ROWS_OUT, DH), F32), jax.ShapeDtypeStruct((1, DH), F32)),
        in_specs=[pl.BlockSpec(memory_space=pltpu.SMEM)] + [vmem] * ZS,
        out_specs=(vmem, vmem),
        name="last",
    )(bias, *parts)


def swap_cores(array):
    return lax.ppermute(array, "dp", [(i, i ^ 1) for i in range(2 * ZS)])


def along_z(array, step):
    return lax.ppermute(array, "dp", [(i, (i + 2 * step) % (2 * ZS)) for i in range(2 * ZS)])


def along_mem(array, offset):
    pairs = []
    for i in range(MEMS):
        row = (i // SIDE + offset // SIDE) % SIDE
        col = (i % SIDE + offset % SIDE) % SIDE
        pairs.append((i, row * SIDE + col))
    return lax.ppermute(array, "mem", pairs)


def exchange(array, axis):
    return lax.all_to_all(array, axis, split_axis=0, concat_axis=0, tiled=True)


def on_device(
    tokens,
    w_query,
    w_key,
    w_value,
    gate_bias,
    memory_keys,
    memory_values,
    retrieval_ids,
    retrieval_counts,
    cotangent,
):
    hidden = tokens[0]
    cot = cotangent[0]
    counts = retrieval_counts.reshape(1, NQB)
    table, entries = make_requests(retrieval_ids.reshape(NQB, TOP), counts)
    wanted = exchange(table, "mem")
    keys, values = memory_keys[0], memory_values[0]
    tiles = [None] * MEMS
    for offset, sent in zip(FIRST, serve(FIRST, wanted, keys, values)):
        tiles[offset] = along_mem(sent, offset)
    for offset, sent in zip(REST, serve(REST, wanted, keys, values)):
        tiles[offset] = along_mem(sent, offset) if offset else sent
    hidden, own = lax.optimization_barrier((hidden, tiles[0]))
    tiles[0] = own
    grad_kv = None
    pieces = []
    for start in range(0, SEGS, LOCAL_SEGS):
        *piece, grad_kv = local_part(
            start, LOCAL_SEGS, hidden, w_query, w_key, w_value, cot, gate_bias, grad_kv
        )
        pieces.append(piece)
    queries, local, ldq = (jnp.concatenate(parts, axis=0) for parts in zip(*pieces))
    shares_kv = exchange(grad_kv.astype(BF16).reshape(8, ROWS_OUT, 2 * DH), "dp")
    sum_kv = jnp.sum(shares_kv.astype(F32), axis=0)
    attended, mine, other = memory_part(
        counts, entries, gate_bias, tiles, queries, local, ldq, cot, hidden
    )
    own, *others = pair_sum(mine, swap_cores(other))
    parts = [own] + [along_z(part, step + 1) for step, part in enumerate(others)]
    share_q, gate_total = last_sum(gate_bias, parts)
    return (attended[None], share_q, sum_kv[:, :DH], sum_kv[:, DH:], gate_total[0, :1])


def solution(mesh):
    return jax.shard_map(
        on_device,
        mesh=mesh,
        in_specs=(
            P("dp", None, None),
            P(None, "mem"),
            P(None, "mem"),
            P(None, "mem"),
            P("mem"),
            P("dp", "mem", None),
            P("dp", "mem", None),
            P("dp", "mem", None, None),
            P("dp", "mem", None),
            P("dp", None, "mem"),
        ),
        out_specs=(P("dp", None, "mem"), P("dp", "mem"), P("dp", "mem"), P("dp", "mem"), P("mem")),
        check_vma=False,
    )
```

time: 365 us -> 166 us (0.45)
  Pallas kernels: 250 us -> 60.2 us
  waiting for transfers between devices: 71.7 us -> 36.3 us
  starting transfers between devices: 18 us -> 48.8 us
  blocking collectives: 13.9 us -> 0 us
  local copies, waits for them, and re-layouts: 4.65 us -> 14.3 us
    pallas_call x3 -> x8, Pallas kernels: 248 us -> 58.5 us  [the longest x1 24.8 us: memory_part(): pl.pallas_call(memory_kernel, out_shape=(jax.ShapeDtypeStruct((TOK, DH),...]
    all_to_all x3 -> x2, waiting for transfers between devices: 71.7 us -> 5.69 us  [exchange(): return lax.all_to_all(array, axis, split_axis=0, concat_axis=0, tiled=True)]
    ppermute x0 -> x19, starting transfers between devices: none -> 34.3 us  [the longest x15 29.8 us: along_mem(): return lax.ppermute(array, 'mem', pairs)]
    ppermute x0 -> x19, waiting for transfers between devices: none -> 30.6 us  [the longest x15 25.4 us: along_mem(): return lax.ppermute(array, 'mem', pairs)]
    all_to_all x1 -> x0, blocking collectives: 13.9 us -> none  [exchange(): return lax.all_to_all(array, axis, split_axis=0, concat_axis=0, tiled=True)]
    unnamed x19 -> x73, local copies, waits for them, and re-layouts: 3.93 us -> 13.6 us
    all_to_all x3 -> x2, starting transfers between devices: 18 us -> 14.5 us  [exchange(): return lax.all_to_all(array, axis, split_axis=0, concat_axis=0, tiled=True)]
  transfers between devices with their start and end apart: 3 -> 21, of which waited for: 2 -> 11; matrix products, arithmetic and copies ran while one was open for 1% -> 2% of each run, Pallas kernels for 15% -> 32%
where the time goes in v1:
time: 166 us; the launch traced here: 165 us
  Pallas kernels  60.2 us (36%)
  starting transfers between devices  48.8 us (29%)
  waiting for transfers between devices  36.3 us (22%)
  local copies, waits for them, and re-layouts  14.3 us (9%)
  other arithmetic  4.01 us (2%)
  between operations  1.67 us (1%)
    ppermute x15, starting transfers between devices, along_mem(): return lax.ppermute(array, 'mem', pairs)  29.8 us
    ppermute x15, waiting for transfers between devices, along_mem(): return lax.ppermute(array, 'mem', pairs)  25.4 us
    pallas_call x1, Pallas kernels, memory_part(): pl.pallas_call(memory_kernel, out_shape=(jax.ShapeDtypeStruct((TOK, DH),...  24.8 us
    pallas_call x3, Pallas kernels, local_part(): pl.pallas_call(local_kernel, grid=(count,), out_shape=(jax.ShapeDtypeStru...  22 us
    all_to_all x2, starting transfers between devices, exchange(): return lax.all_to_all(array, axis, split_axis=0, concat_axis=0, tiled=True)  14.5 us
    unnamed x73, local copies, waits for them, and re-layouts  13.6 us
    pallas_call x2, Pallas kernels, serve(): pl.pallas_call(functools.partial(serve_kernel, offsets), out_shape=[jax.S...  8.07 us
    all_to_all x2, waiting for transfers between devices, exchange(): return lax.all_to_all(array, axis, split_axis=0, concat_axis=0, tiled=True)  5.69 us
  transfers between devices with their start and end apart: 21, of which 11 were waited for; matrix products, arithmetic and copies ran while one was open for 2% of the time, Pallas kernels for 32%

profile of v1, /device:TPU:1, one launch (start us, length us, event | category | flops | bytes accessed | tf_op | source)
XLA Modules:
  0.0 165.4 jit_solution(7380961634244788705)
XLA Ops:
  0.6 1.4 copy.16
  2.0 1.8 %request.1 = (s32[16,128]{1,0:T(8,128)}, s32[16,128]{1,0:T(8,128)}) custom-call(s32[24,8]{1,0:T(8,128)} %bitcast.31, s32[1,24]{1,0:T(1,128)} %bitcast.16), custom_call_target="tpu_custom_call" | custom-call | tf_op jit(solution)/shard_map/request/pallas_call | solution.py:79
  3.7 7.6 %all-to-all-start = ((s32[16,1,128]{2,1,0:T(1,128)}), s32[16,1,128]{2,1,0:T(1,128)S(1)}, u32[]{:S(2)}, u32[]{:S(2)}) async-start(s32[16,1,128]{2,1,0:T(1,128)} %bitcast.32), calls=%async_computation | async-start | bytes 16384 | tf_op jit(solution)/shard_map/all_to_all | solution.py:436
  12.0 5.7 %all-to-all-done = s32[16,1,128]{2,1,0:T(1,128)S(1)} async-done(((s32[16,1,128]{2,1,0:T(1,128)}), s32[16,1,128]{2,1,0:T(1,128)S(1)}, u32[]{:S(2)}, u32[]{:S(2)}) %all-to-all-start) | async-done | bytes 8224 | tf_op jit(solution)/shard_map/all_to_all | solution.py:436
  17.7 4.8 %serve.2 = (bf16[12,2,64,128]{3,2,1,0:T(8,128)(2,1)}, bf16[12,2,64,128]{3,2,1,0:T(8,128)(2,1)S(1)}, bf16[12,2,64,128]{3,2,1,0:T(8,128)(2,1)}, bf16[12,2,64,128]{...) custom-call(s32[16,128]{1,0:T(8,128)S(1)} %bitcast.14, ...), custom_call_target="tpu_custom_call" | custom-call | bytes 12582912 | tf_op jit(solution)/shard_map/serve/pallas_call | solution.py:121
  22.5 1.2 collective-permute-start.1
  23.7 2.1 %collective-permute-start.10 = (bf16[12,2,64,128]{3,2,1,0:T(8,128)(2,1)S(1)}, bf16[12,2,64,128]{3,2,1,0:T(8,128)(2,1)S(1)}, u32[]{:S(2)}, u32[]{:S(2)}) collective-permute-start(bf16[12,2,64,128]{3,2,1,0:T(8,128)(2,1)S(1)} %get-tuple-element.60), channel_id=1, source_target_pairs={{0,11},{1,8},{2,9},{3,10},{4,15},{5,12},{6,13},{7,14},{8,3},{9,0},... | collective-permute-start | bytes 1179656 | tf_op jit(solution)/shard_map/ppermute | solution.py:432
  25.8 0.9 collective-permute-start.12
  26.7 2.7 %collective-permute-start.13 = (bf16[12,2,64,128]{3,2,1,0:T(8,128)(2,1)S(1)}, bf16[12,2,64,128]{3,2,1,0:T(8,128)(2,1)S(1)}, u32[]{:S(2)}, u32[]{:S(2)}) collective-permute-start(bf16[12,2,64,128]{3,2,1,0:T(8,128)(2,1)S(1)} %get-tuple-element.63), channel_id=1, source_target_pairs={{0,14},{1,15},{2,12},{3,13},{4,2},{5,3},{6,0},{7,1},{8,6},{9,7},{1... | collective-permute-start | bytes 1179656 | tf_op jit(solution)/shard_map/ppermute | solution.py:432
  29.4 0.8 collective-permute-start.14
  30.3 0.0 copy-start.4
  30.3 4.6 %copy-done.4 = bf16[1,3072,2048]{2,1,0:T(8,128)(2,1)S(1)} copy-done((bf16[1,3072,2048]{2,1,0:T(8,128)(2,1)S(1)}, bf16[1,3072,2048]{2,1,0:T(8,128)(2,1)}, u32[]{:S(2)}) %copy-start.4) | copy-done | bytes 12582936
  34.9 7.3 %local.3 = (bf16[1024,128]{1,0:T(8,128)(2,1)S(1)}, f32[1024,128]{1,0:T(8,128)S(1)}, f32[1024,128]{1,0:T(8,128)S(1)}, f32[2048,256]{1,0:T(8,128)S(1)}) custom-call(bf16[3072,2048]{1,0:T(8,128)(2,1)S(1)} %bitcast.19, bf16[2048,128]{1,0:T(8,128)(2,1)S(1)} %copy-done.7, bf16[2048,128]{1,0:T(8,128)(2,1)S(1)} %copy-done.8, bf16[2048,128]{1,0:T(8,128)(2,1)S(1)} %copy-done.9, ...), custom_call_target="tpu_custom_call" | custom-call | flops 4800000000 | bytes 6291456 | tf_op jit(solution)/shard_map/local/pallas_call | solution.py:188
  42.2 7.3 %local.4 = (bf16[1024,128]{1,0:T(8,128)(2,1)S(1)}, f32[1024,128]{1,0:T(8,128)S(1)}, f32[1024,128]{1,0:T(8,128)S(1)}, f32[2048,256]{1,0:T(8,128)S(1)}) custom-call(bf16[3072,2048]{1,0:T(8,128)(2,1)S(1)} %bitcast.20, bf16[2048,128]{1,0:T(8,128)(2,1)S(1)} %copy-done.7, bf16[2048,128]{1,0:T(8,128)(2,1)S(1)} %copy-done.8, bf16[2048,128]{1,0:T(8,128)(2,1)S(1)} %copy-done.9, ...), custom_call_target="tpu_custom_call" | custom-call | flops 4800000000 | bytes 6291456 | tf_op jit(solution)/shard_map/local/pallas_call | solution.py:188
  49.6 0.7 copy-done.1
  50.3 0.8 copy-done.12
  51.0 1.5 collective-permute-start.4
  52.6 0.0 collective-permute-done.10.refs_11_
  52.6 0.8 copy-done.14
  53.3 1.4 collective-permute-start.5
  54.8 3.2 %collective-permute-done.12.refs_13_ = bf16[12,2,64,128]{3,2,1,0:T(8,128)(2,1)S(1)} collective-permute-done((bf16[12,2,64,128]{3,2,1,0:T(8,128)(2,1)S(1)}, bf16[12,2,64,128]{3,2,1,0:T(8,128)(2,1)S(1)}, u32[]{:S(2)}, u32[]{:S(2)}) %collective-permute-start.12) | collective-permute-done | bytes 393248 | tf_op jit(solution)/shard_map/ppermute | solution.py:432
  58.0 0.8 copy-done.16
  58.8 2.4 %collective-permute-start.6 = (bf16[12,2,64,128]{3,2,1,0:T(8,128)(2,1)}, bf16[12,2,64,128]{3,2,1,0:T(8,128)(2,1)}, u32[]{:S(2)}, u32[]{:S(2)}) collective-permute-start(bf16[12,2,64,128]{3,2,1,0:T(8,128)(2,1)} %get-tuple-element.56), channel_id=1, source_target_pairs={{0,7},{1,4},{2,5},{3,6},{4,11},{5,8},{6,9},{7,10},{8,15},{9,12},{1... | collective-permute-start | bytes 1179656 | tf_op jit(solution)/shard_map/ppermute | solution.py:432
  61.1 0.0 collective-permute-done.13.refs_14_
  61.1 0.8 copy-done.18
  61.9 1.0 collective-permute-start.7
  62.9 0.9 collective-permute-done.14.refs_15_
  63.8 0.8 copy-done.20
  64.6 5.5 %collective-permute-start.8 = (bf16[12,2,64,128]{3,2,1,0:T(8,128)(2,1)}, bf16[12,2,64,128]{3,2,1,0:T(8,128)(2,1)}, u32[]{:S(2)}, u32[]{:S(2)}) collective-permute-start(bf16[12,2,64,128]{3,2,1,0:T(8,128)(2,1)} %get-tuple-element.58), channel_id=1, source_target_pairs={{0,9},{1,10},{2,11},{3,8},{4,13},{5,14},{6,15},{7,12},{8,1},{9,2},... | collective-permute-start | bytes 1179656 | tf_op jit(solution)/shard_map/ppermute | solution.py:432
  70.1 7.3 %local.5 = (bf16[1024,128]{1,0:T(8,128)(2,1)S(1)}, f32[1024,128]{1,0:T(8,128)S(1)}, f32[1024,128]{1,0:T(8,128)S(1)}, f32[2048,256]{1,0:T(8,128)S(1)}) custom-call(bf16[3072,2048]{1,0:T(8,128)(2,1)S(1)} %bitcast.21, bf16[2048,128]{1,0:T(8,128)(2,1)S(1)} %copy-done.7, bf16[2048,128]{1,0:T(8,128)(2,1)S(1)} %copy-done.8, bf16[2048,128]{1,0:T(8,128)(2,1)S(1)} %copy-done.9, ...), custom_call_target="tpu_custom_call" | custom-call | flops 4800000000 | bytes 6291456 | tf_op jit(solution)/shard_map/local/pallas_call | solution.py:188
  77.5 0.7 copy-done.2
  78.2 3.3 %serve.3 = (bf16[12,2,64,128]{3,2,1,0:T(8,128)(2,1)S(1)}, bf16[12,2,64,128]{3,2,1,0:T(8,128)(2,1)S(1)}, bf16[12,2,64,128]{3,2,1,0:T(8,128)(2,1)S(1)}, bf16[12,2,64,128]{3,2,1,0:T(8,128)(2,1)S(1)}) custom-call(s32[16,128]{1,0:T(8,128)S(1)} %bitcast.15, bf16[1536,2048]{1,0:T(8,128)(2,1)} %bitcast.27, bf16[1536,2048]{1,0:T(8,128)(2,1)} %bitcast.29), custom_call_target="tpu_custom_call" | custom-call | bytes 4194304 | tf_op jit(solution)/shard_map/serve/pallas_call | solution.py:121
  81.5 1.2 convert_element_type.6
  82.7 0.1 copy-done.28
  82.8 0.1 copy-done.30
  82.9 6.9 %all-to-all-start.1 = ((bf16[8,256,256]{2,1,0:T(8,128)(2,1)}), bf16[8,256,256]{2,1,0:T(8,128)(2,1)}, u32[]{:S(2)}, u32[]{:S(2)}) async-start(bf16[8,256,256]{2,1,0:T(8,128)(2,1)} %bitcast.30), calls=%async_computation.1 | async-start | bytes 2097152 | tf_op jit(solution)/shard_map/all_to_all | solution.py:436
  89.9 1.2 pad_maximum_fusion.2.refs_16_
  91.1 3.0 %collective-permute-start.9 = (bf16[12,2,64,128]{3,2,1,0:T(8,128)(2,1)S(1)}, bf16[12,2,64,128]{3,2,1,0:T(8,128)(2,1)S(1)}, u32[]{:S(2)}, u32[]{:S(2)}) collective-permute-start(bf16[12,2,64,128]{3,2,1,0:T(8,128)(2,1)S(1)} %copy-done.23), channel_id=1, source_target_pairs={{0,10},{1,11},{2,8},{3,9},{4,14},{5,15},{6,12},{7,13},{8,2},{9,3},... | collective-permute-start | bytes 1179656 | tf_op jit(solution)/shard_map/ppermute | solution.py:432
  94.1 0.8 collective-permute-start
  94.9 6.4 %collective-permute-start.11 = (bf16[12,2,64,128]{3,2,1,0:T(8,128)(2,1)S(1)}, bf16[12,2,64,128]{3,2,1,0:T(8,128)(2,1)S(1)}, u32[]{:S(2)}, u32[]{:S(2)}) collective-permute-start(bf16[12,2,64,128]{3,2,1,0:T(8,128)(2,1)S(1)} %copy-done.29), channel_id=1, source_target_pairs={{0,12},{1,13},{2,14},{3,15},{4,0},{5,1},{6,2},{7,3},{8,4},{9,5},{1... | collective-permute-start | bytes 1179656 | tf_op jit(solution)/shard_map/ppermute | solution.py:432
  101.3 10.2 %collective-permute-done.7.refs_8_ = bf16[12,2,64,128]{3,2,1,0:T(8,128)(2,1)} collective-permute-done((bf16[12,2,64,128]{3,2,1,0:T(8,128)(2,1)}, bf16[12,2,64,128]{3,2,1,0:T(8,128)(2,1)}, u32[]{:S(2)}, u32[]{:S(2)}) %collective-permute-start.7) | collective-permute-done | bytes 393248 | tf_op jit(solution)/shard_map/ppermute | solution.py:432
  111.5 0.1 collective-permute-start.3
  111.5 0.0 copy-start.3
  111.6 0.0 copy-start.6
  111.6 0.0 copy-start.31
  111.6 0.2 pad_maximum_fusion
  111.9 3.3 %collective-permute-done.refs_1_ = bf16[12,2,64,128]{3,2,1,0:T(8,128)(2,1)S(1)} collective-permute-done((bf16[12,2,64,128]{3,2,1,0:T(8,128)(2,1)}, bf16[12,2,64,128]{3,2,1,0:T(8,128)(2,1)S(1)}, u32[]{:S(2)}, u32[]{:S(2)}) %collective-permute-start) | collective-permute-done | bytes 393248 | tf_op jit(solution)/shard_map/ppermute | solution.py:432
  115.1 6.5 %collective-permute-done.2.refs_3_ = bf16[12,2,64,128]{3,2,1,0:T(8,128)(2,1)S(1)} collective-permute-done((bf16[12,2,64,128]{3,2,1,0:T(8,128)(2,1)S(1)}, bf16[12,2,64,128]{3,2,1,0:T(8,128)(2,1)S(1)}, u32[]{:S(2)}, u32[]{:S(2)}) %collective-permute-start.2) | collective-permute-done | bytes 393248 | tf_op jit(solution)/shard_map/ppermute | solution.py:432
  121.6 1.3 collective-permute-done.3.refs_4_
  123.0 24.8 %memory.1 = (bf16[3072,128]{1,0:T(8,128)(2,1)}, f32[4,272,128]{2,1,0:T(8,128)S(1)}, bf16[4,272,128]{2,1,0:T(8,128)(2,1)S(1)}) custom-call(s32[1,24]{1,0:T(1,128)S(1)} %bitcast.17, s32[16,128]{1,0:T(8,128)S(1)} %copy-done.31, f32[1]{0:T(128)S(6)} %copy.18.bias_ref, bf16[12,2,64,128]{3,2,1,0:T(8,128)(2,1)S(1)} %copy-done.11, ...), custom_call_target="tpu_custom_call" | custom-call | flops 8000000000 | bytes 25165824 | tf_op jit(solution)/shard_map/memory/pallas_call | solution.py:351
  147.8 0.8 copy-done
  148.6 1.6 collective-permute-done.15.got_ref
  150.2 0.7 copy-done.32
  150.9 1.9 %pair.1 = (f32[272,128]{1,0:T(8,128)}, bf16[272,128]{1,0:T(8,128)(2,1)}, bf16[272,128]{1,0:T(8,128)(2,1)}, bf16[272,128]{1,0:T(8,128)(2,1)}) custom-call(f32[4,272,128]{2,1,0:T(8,128)} %copy-done, bf16[4,272,128]{2,1,0:T(8,128)(2,1)} %copy-done.32), custom_call_target="tpu_custom_call" | custom-call | tf_op jit(solution)/shard_map/pair/pallas_call | solution.py:391
  152.8 1.4 collective-permute-start.16
  154.2 3.1 %collective-permute-start.17 = (bf16[272,128]{1,0:T(8,128)(2,1)}, bf16[272,128]{1,0:T(8,128)(2,1)S(1)}, u32[]{:S(2)}, u32[]{:S(2)}) collective-permute-start(bf16[272,128]{1,0:T(8,128)(2,1)} %get-tuple-element.82), channel_id=1, source_target_pairs={{0,64},{16,80},{32,96},{48,112},{64,0},{80,16},{96,32},{112,48},{1... | collective-permute-start | bytes 208904 | tf_op jit(solution)/shard_map/ppermute | solution.py:423
  157.3 1.3 collective-permute-done.16.one_ref
  158.6 2.1 %collective-permute-done.17.two_ref = bf16[272,128]{1,0:T(8,128)(2,1)S(1)} collective-permute-done((bf16[272,128]{1,0:T(8,128)(2,1)}, bf16[272,128]{1,0:T(8,128)(2,1)S(1)}, u32[]{:S(2)}, u32[]{:S(2)}) %collective-permute-start.17) | collective-permute-done | bytes 69664 | tf_op jit(solution)/shard_map/ppermute | solution.py:423
  160.6 0.3 collective-permute-done.18.three_ref
  160.9 0.3 copy-done.34
  161.2 0.3 copy-done.35
  161.6 1.7 %last.1 = (f32[256,128]{1,0:T(8,128)}, f32[1,128]{1,0:T(1,128)}) custom-call(f32[1]{0:T(128)S(6)} %copy.18.bias_ref, f32[272,128]{1,0:T(8,128)} %get-tuple-element.80.own_ref, bf16[272,128]{1,0:T(8,128)(2,1)} %copy-done.33, bf16[272,128]{1,0:T(8,128)(2,1)} %copy-done.34, bf16[272,128]{1,0:T(8,128)(2,1)} %copy-done.35), custom_call_target="tpu_custom_call" | custom-call | tf_op jit(solution)/shard_map/last/pallas_call | solution.py:409
  163.3 1.4 convert_reduce_fusion
  164.7 0.7 fusion
  (65 shorter events, 0.1 us)
Async XLA Ops:
  3.7 13.9 %all-to-all-start = ((s32[16,1,128]{2,1,0:T(1,128)}), s32[16,1,128]{2,1,0:T(1,128)S(1)}, u32[]{:S(2)}, u32[]{:S(2)}) async-start(s32[16,1,128]{2,1,0:T(1,128)} %bitcast.32), calls=%async_computation | async-start | bytes 16384 | tf_op jit(solution)/shard_map/all_to_all | solution.py:436
  17.7 12.6 %copy-start.5 = (bf16[1,3072,128]{2,1,0:T(8,128)(2,1)S(1)}, bf16[1,3072,128]{2,1,0:T(8,128)(2,1)}, u32[]{:S(2)}) copy-start(bf16[1,3072,128]{2,1,0:T(8,128)(2,1)} %param.19) | copy-start | bytes 2359300
  17.7 12.6 %copy-start.7 = (bf16[2048,128]{1,0:T(8,128)(2,1)S(1)}, bf16[2048,128]{1,0:T(8,128)(2,1)}, u32[]{:S(2)}) copy-start(bf16[2048,128]{1,0:T(8,128)(2,1)} %wq_ref.5) | copy-start | bytes 1572868
  17.7 12.6 %copy-start.8 = (bf16[2048,128]{1,0:T(8,128)(2,1)S(1)}, bf16[2048,128]{1,0:T(8,128)(2,1)}, u32[]{:S(2)}) copy-start(bf16[2048,128]{1,0:T(8,128)(2,1)} %wk_ref.5) | copy-start | bytes 1572868
  17.7 12.6 %copy-start.9 = (bf16[2048,128]{1,0:T(8,128)(2,1)S(1)}, bf16[2048,128]{1,0:T(8,128)(2,1)}, u32[]{:S(2)}) copy-start(bf16[2048,128]{1,0:T(8,128)(2,1)} %wv_ref.5) | copy-start | bytes 1572868
  22.5 19.7 %copy-start.10 = (bf16[12,2,64,128]{3,2,1,0:T(8,128)(2,1)}, bf16[12,2,64,128]{3,2,1,0:T(8,128)(2,1)S(1)}, u32[]{:S(2)}) copy-start(bf16[12,2,64,128]{3,2,1,0:T(8,128)(2,1)S(1)} %get-tuple-element.49.refs_0_) | copy-start | bytes 1179652
  22.5 19.7 %copy-start.22 = (bf16[12,2,64,128]{3,2,1,0:T(8,128)(2,1)}, bf16[12,2,64,128]{3,2,1,0:T(8,128)(2,1)S(1)}, u32[]{:S(2)}) copy-start(bf16[12,2,64,128]{3,2,1,0:T(8,128)(2,1)S(1)} %get-tuple-element.59) | copy-start | bytes 1179652
  22.5 27.7 %collective-permute-start.1 = (bf16[12,2,64,128]{3,2,1,0:T(8,128)(2,1)S(1)}, bf16[12,2,64,128]{3,2,1,0:T(8,128)(2,1)S(1)}, u32[]{:S(2)}, u32[]{:S(2)}) collective-permute-start(bf16[12,2,64,128]{3,2,1,0:T(8,128)(2,1)S(1)} %get-tuple-element.51), channel_id=1, source_target_pairs={{0,2},{1,3},{2,0},{3,1},{4,6},{5,7},{6,4},{7,5},{8,10},{9,11},{10,... | collective-permute-start | bytes 1179656 | tf_op jit(solution)/shard_map/ppermute | solution.py:432
  23.7 28.9 %collective-permute-start.10 = (bf16[12,2,64,128]{3,2,1,0:T(8,128)(2,1)S(1)}, bf16[12,2,64,128]{3,2,1,0:T(8,128)(2,1)S(1)}, u32[]{:S(2)}, u32[]{:S(2)}) collective-permute-start(bf16[12,2,64,128]{3,2,1,0:T(8,128)(2,1)S(1)} %get-tuple-element.60), channel_id=1, source_target_pairs={{0,11},{1,8},{2,9},{3,10},{4,15},{5,12},{6,13},{7,14},{8,3},{9,0},... | collective-permute-start | bytes 1179656 | tf_op jit(solution)/shard_map/ppermute | solution.py:432
  25.8 32.2 %collective-permute-start.12 = (bf16[12,2,64,128]{3,2,1,0:T(8,128)(2,1)S(1)}, bf16[12,2,64,128]{3,2,1,0:T(8,128)(2,1)S(1)}, u32[]{:S(2)}, u32[]{:S(2)}) collective-permute-start(bf16[12,2,64,128]{3,2,1,0:T(8,128)(2,1)S(1)} %get-tuple-element.62), channel_id=1, source_target_pairs={{0,13},{1,14},{2,15},{3,12},{4,1},{5,2},{6,3},{7,0},{8,5},{9,6},{1... | collective-permute-start | bytes 1179656 | tf_op jit(solution)/shard_map/ppermute | solution.py:432
  26.7 34.4 %collective-permute-start.13 = (bf16[12,2,64,128]{3,2,1,0:T(8,128)(2,1)S(1)}, bf16[12,2,64,128]{3,2,1,0:T(8,128)(2,1)S(1)}, u32[]{:S(2)}, u32[]{:S(2)}) collective-permute-start(bf16[12,2,64,128]{3,2,1,0:T(8,128)(2,1)S(1)} %get-tuple-element.63), channel_id=1, source_target_pairs={{0,14},{1,15},{2,12},{3,13},{4,2},{5,3},{6,0},{7,1},{8,6},{9,7},{1... | collective-permute-start | bytes 1179656 | tf_op jit(solution)/shard_map/ppermute | solution.py:432
  29.4 34.4 %collective-permute-start.14 = (bf16[12,2,64,128]{3,2,1,0:T(8,128)(2,1)S(1)}, bf16[12,2,64,128]{3,2,1,0:T(8,128)(2,1)S(1)}, u32[]{:S(2)}, u32[]{:S(2)}) collective-permute-start(bf16[12,2,64,128]{3,2,1,0:T(8,128)(2,1)S(1)} %get-tuple-element.64), channel_id=1, source_target_pairs={{0,15},{1,12},{2,13},{3,14},{4,3},{5,0},{6,1},{7,2},{8,7},{9,4},{1... | collective-permute-start | bytes 1179656 | tf_op jit(solution)/shard_map/ppermute | solution.py:432
  30.3 4.6 %copy-start.4 = (bf16[1,3072,2048]{2,1,0:T(8,128)(2,1)S(1)}, bf16[1,3072,2048]{2,1,0:T(8,128)(2,1)}, u32[]{:S(2)}) copy-start(bf16[1,3072,2048]{2,1,0:T(8,128)(2,1)} %param.10) | copy-start | bytes 37748740
  49.6 0.7 copy-start.1
  50.3 0.8 copy-start.12
  51.0 40.1 %collective-permute-start.4 = (bf16[12,2,64,128]{3,2,1,0:T(8,128)(2,1)}, bf16[12,2,64,128]{3,2,1,0:T(8,128)(2,1)}, u32[]{:S(2)}, u32[]{:S(2)}) collective-permute-start(bf16[12,2,64,128]{3,2,1,0:T(8,128)(2,1)} %get-tuple-element.54), channel_id=1, source_target_pairs={{0,5},{1,6},{2,7},{3,4},{4,9},{5,10},{6,11},{7,8},{8,13},{9,14},{1... | collective-permute-start | bytes 1179656 | tf_op jit(solution)/shard_map/ppermute | solution.py:432
  52.6 0.8 copy-start.14
  53.3 40.7 %collective-permute-start.5 = (bf16[12,2,64,128]{3,2,1,0:T(8,128)(2,1)}, bf16[12,2,64,128]{3,2,1,0:T(8,128)(2,1)}, u32[]{:S(2)}, u32[]{:S(2)}) collective-permute-start(bf16[12,2,64,128]{3,2,1,0:T(8,128)(2,1)} %get-tuple-element.55), channel_id=1, source_target_pairs={{0,6},{1,7},{2,4},{3,5},{4,10},{5,11},{6,8},{7,9},{8,14},{9,15},{1... | collective-permute-start | bytes 1179656 | tf_op jit(solution)/shard_map/ppermute | solution.py:432
  58.0 0.8 copy-start.16
  58.8 36.1 %collective-permute-start.6 = (bf16[12,2,64,128]{3,2,1,0:T(8,128)(2,1)}, bf16[12,2,64,128]{3,2,1,0:T(8,128)(2,1)}, u32[]{:S(2)}, u32[]{:S(2)}) collective-permute-start(bf16[12,2,64,128]{3,2,1,0:T(8,128)(2,1)} %get-tuple-element.56), channel_id=1, source_target_pairs={{0,7},{1,4},{2,5},{3,6},{4,11},{5,8},{6,9},{7,10},{8,15},{9,12},{1... | collective-permute-start | bytes 1179656 | tf_op jit(solution)/shard_map/ppermute | solution.py:432
  61.1 0.8 copy-start.18
  61.9 49.5 %collective-permute-start.7 = (bf16[12,2,64,128]{3,2,1,0:T(8,128)(2,1)}, bf16[12,2,64,128]{3,2,1,0:T(8,128)(2,1)}, u32[]{:S(2)}, u32[]{:S(2)}) collective-permute-start(bf16[12,2,64,128]{3,2,1,0:T(8,128)(2,1)} %get-tuple-element.57), channel_id=1, source_target_pairs={{0,8},{1,9},{2,10},{3,11},{4,12},{5,13},{6,14},{7,15},{8,0},{9,1},... | collective-permute-start | bytes 1179656 | tf_op jit(solution)/shard_map/ppermute | solution.py:432
  63.8 0.8 copy-start.20
  64.6 46.8 %collective-permute-start.8 = (bf16[12,2,64,128]{3,2,1,0:T(8,128)(2,1)}, bf16[12,2,64,128]{3,2,1,0:T(8,128)(2,1)}, u32[]{:S(2)}, u32[]{:S(2)}) collective-permute-start(bf16[12,2,64,128]{3,2,1,0:T(8,128)(2,1)} %get-tuple-element.58), channel_id=1, source_target_pairs={{0,9},{1,10},{2,11},{3,8},{4,13},{5,14},{6,15},{7,12},{8,1},{9,2},... | collective-permute-start | bytes 1179656 | tf_op jit(solution)/shard_map/ppermute | solution.py:432
  77.5 0.7 copy-start.2
  81.4 1.3 copy-start.24
  81.4 1.2 copy-start.26
  81.4 1.4 copy-start.28
  81.4 1.5 copy-start.30
  82.9 80.3 %all-to-all-start.1 = ((bf16[8,256,256]{2,1,0:T(8,128)(2,1)}), bf16[8,256,256]{2,1,0:T(8,128)(2,1)}, u32[]{:S(2)}, u32[]{:S(2)}) async-start(bf16[8,256,256]{2,1,0:T(8,128)(2,1)} %bitcast.30), calls=%async_computation.1 | async-start | bytes 2097152 | tf_op jit(solution)/shard_map/all_to_all | solution.py:436
  89.9 1.2 copy-start.23
  89.9 5.0 %copy-start.29 = (bf16[12,2,64,128]{3,2,1,0:T(8,128)(2,1)S(1)}, bf16[12,2,64,128]{3,2,1,0:T(8,128)(2,1)}, u32[]{:S(2)}) copy-start(bf16[12,2,64,128]{3,2,1,0:T(8,128)(2,1)} %copy-done.28) | copy-start | bytes 1179652
  89.9 21.5 %copy-start.27 = (bf16[12,2,64,128]{3,2,1,0:T(8,128)(2,1)S(1)}, bf16[12,2,64,128]{3,2,1,0:T(8,128)(2,1)}, u32[]{:S(2)}) copy-start(bf16[12,2,64,128]{3,2,1,0:T(8,128)(2,1)} %copy-done.26) | copy-start | bytes 1179652
  89.9 21.6 %copy-start.25 = (bf16[12,2,64,128]{3,2,1,0:T(8,128)(2,1)S(1)}, bf16[12,2,64,128]{3,2,1,0:T(8,128)(2,1)}, u32[]{:S(2)}) copy-start(bf16[12,2,64,128]{3,2,1,0:T(8,128)(2,1)} %copy-done.24) | copy-start | bytes 1179652
  91.1 20.7 %collective-permute-start.9 = (bf16[12,2,64,128]{3,2,1,0:T(8,128)(2,1)S(1)}, bf16[12,2,64,128]{3,2,1,0:T(8,128)(2,1)S(1)}, u32[]{:S(2)}, u32[]{:S(2)}) collective-permute-start(bf16[12,2,64,128]{3,2,1,0:T(8,128)(2,1)S(1)} %copy-done.23), channel_id=1, source_target_pairs={{0,10},{1,11},{2,8},{3,9},{4,14},{5,15},{6,12},{7,13},{8,2},{9,3},... | collective-permute-start | bytes 1179656 | tf_op jit(solution)/shard_map/ppermute | solution.py:432
  94.1 21.1 %collective-permute-start = (bf16[12,2,64,128]{3,2,1,0:T(8,128)(2,1)}, bf16[12,2,64,128]{3,2,1,0:T(8,128)(2,1)S(1)}, u32[]{:S(2)}, u32[]{:S(2)}) collective-permute-start(bf16[12,2,64,128]{3,2,1,0:T(8,128)(2,1)} %copy-done.30), channel_id=1, source_target_pairs={{0,1},{1,2},{2,3},{3,0},{4,5},{5,6},{6,7},{7,4},{8,9},{9,10},{10,1... | collective-permute-start | bytes 1179656 | tf_op jit(solution)/shard_map/ppermute | solution.py:432
  94.9 20.3 %collective-permute-start.11 = (bf16[12,2,64,128]{3,2,1,0:T(8,128)(2,1)S(1)}, bf16[12,2,64,128]{3,2,1,0:T(8,128)(2,1)S(1)}, u32[]{:S(2)}, u32[]{:S(2)}) collective-permute-start(bf16[12,2,64,128]{3,2,1,0:T(8,128)(2,1)S(1)} %copy-done.29), channel_id=1, source_target_pairs={{0,12},{1,13},{2,14},{3,15},{4,0},{5,1},{6,2},{7,3},{8,4},{9,5},{1... | collective-permute-start | bytes 1179656 | tf_op jit(solution)/shard_map/ppermute | solution.py:432
  111.4 10.2 %collective-permute-start.2 = (bf16[12,2,64,128]{3,2,1,0:T(8,128)(2,1)S(1)}, bf16[12,2,64,128]{3,2,1,0:T(8,128)(2,1)S(1)}, u32[]{:S(2)}, u32[]{:S(2)}) collective-permute-start(bf16[12,2,64,128]{3,2,1,0:T(8,128)(2,1)S(1)} %copy-done.27), channel_id=1, source_target_pairs={{0,3},{1,0},{2,1},{3,2},{4,7},{5,4},{6,5},{7,6},{8,11},{9,8},{10,9... | collective-permute-start | bytes 1179656 | tf_op jit(solution)/shard_map/ppermute | solution.py:432
  111.5 11.5 %collective-permute-start.3 = (bf16[12,2,64,128]{3,2,1,0:T(8,128)(2,1)S(1)}, bf16[12,2,64,128]{3,2,1,0:T(8,128)(2,1)S(1)}, u32[]{:S(2)}, u32[]{:S(2)}) collective-permute-start(bf16[12,2,64,128]{3,2,1,0:T(8,128)(2,1)S(1)} %copy-done.25), channel_id=1, source_target_pairs={{0,4},{1,5},{2,6},{3,7},{4,8},{5,9},{6,10},{7,11},{8,12},{9,13},{1... | collective-permute-start | bytes 1179656 | tf_op jit(solution)/shard_map/ppermute | solution.py:432
  111.5 11.4 %copy-start.3 = (s32[1,1,24]{2,1,0:T(1,128)S(1)}, s32[1,1,24]{2,1,0:T(1,128)}, u32[]{:S(2)}) copy-start(s32[1,1,24]{2,1,0:T(1,128)} %param.18) | copy-start | bytes 292
  111.6 11.4 %copy-start.6 = (bf16[1,3072,128]{2,1,0:T(8,128)(2,1)S(1)}, bf16[1,3072,128]{2,1,0:T(8,128)(2,1)}, u32[]{:S(2)}) copy-start(bf16[1,3072,128]{2,1,0:T(8,128)(2,1)} %param.19) | copy-start | bytes 2359300
  111.6 11.4 %copy-start.11 = (bf16[12,2,64,128]{3,2,1,0:T(8,128)(2,1)S(1)}, bf16[12,2,64,128]{3,2,1,0:T(8,128)(2,1)}, u32[]{:S(2)}) copy-start(bf16[12,2,64,128]{3,2,1,0:T(8,128)(2,1)} %copy-done.10) | copy-start | bytes 1179652
  111.6 11.4 %copy-start.13 = (bf16[12,2,64,128]{3,2,1,0:T(8,128)(2,1)S(1)}, bf16[12,2,64,128]{3,2,1,0:T(8,128)(2,1)}, u32[]{:S(2)}) copy-start(bf16[12,2,64,128]{3,2,1,0:T(8,128)(2,1)} %copy-done.12) | copy-start | bytes 1179652
  111.6 11.4 %copy-start.15 = (bf16[12,2,64,128]{3,2,1,0:T(8,128)(2,1)S(1)}, bf16[12,2,64,128]{3,2,1,0:T(8,128)(2,1)}, u32[]{:S(2)}) copy-start(bf16[12,2,64,128]{3,2,1,0:T(8,128)(2,1)} %copy-done.14) | copy-start | bytes 1179652
  111.6 11.4 %copy-start.17 = (bf16[12,2,64,128]{3,2,1,0:T(8,128)(2,1)S(1)}, bf16[12,2,64,128]{3,2,1,0:T(8,128)(2,1)}, u32[]{:S(2)}) copy-start(bf16[12,2,64,128]{3,2,1,0:T(8,128)(2,1)} %copy-done.16) | copy-start | bytes 1179652
  111.6 11.4 %copy-start.19 = (bf16[12,2,64,128]{3,2,1,0:T(8,128)(2,1)S(1)}, bf16[12,2,64,128]{3,2,1,0:T(8,128)(2,1)}, u32[]{:S(2)}) copy-start(bf16[12,2,64,128]{3,2,1,0:T(8,128)(2,1)} %copy-done.18) | copy-start | bytes 1179652
  111.6 11.4 %copy-start.21 = (bf16[12,2,64,128]{3,2,1,0:T(8,128)(2,1)S(1)}, bf16[12,2,64,128]{3,2,1,0:T(8,128)(2,1)}, u32[]{:S(2)}) copy-start(bf16[12,2,64,128]{3,2,1,0:T(8,128)(2,1)} %copy-done.20) | copy-start | bytes 1179652
  111.6 11.4 %copy-start.31 = (s32[16,128]{1,0:T(8,128)S(1)}, s32[16,128]{1,0:T(8,128)}, u32[]{:S(2)}) copy-start(s32[16,128]{1,0:T(8,128)} %get-tuple-element.46.entry_ref) | copy-start | bytes 24580
  147.8 0.8 copy-start
  148.6 1.6 collective-permute-start.15
  150.2 0.7 copy-start.32
  152.8 5.8 %collective-permute-start.16 = (bf16[272,128]{1,0:T(8,128)(2,1)}, bf16[272,128]{1,0:T(8,128)(2,1)S(1)}, u32[]{:S(2)}, u32[]{:S(2)}) collective-permute-start(bf16[272,128]{1,0:T(8,128)(2,1)} %get-tuple-element.81), channel_id=1, source_target_pairs={{0,32},{16,48},{32,64},{48,80},{64,96},{80,112},{96,0},{112,16},{1... | collective-permute-start | bytes 208904 | tf_op jit(solution)/shard_map/ppermute | solution.py:423
  154.2 6.4 %collective-permute-start.17 = (bf16[272,128]{1,0:T(8,128)(2,1)}, bf16[272,128]{1,0:T(8,128)(2,1)S(1)}, u32[]{:S(2)}, u32[]{:S(2)}) collective-permute-start(bf16[272,128]{1,0:T(8,128)(2,1)} %get-tuple-element.82), channel_id=1, source_target_pairs={{0,64},{16,80},{32,96},{48,112},{64,0},{80,16},{96,32},{112,48},{1... | collective-permute-start | bytes 208904 | tf_op jit(solution)/shard_map/ppermute | solution.py:423
  157.3 3.7 %collective-permute-start.18 = (bf16[272,128]{1,0:T(8,128)(2,1)}, bf16[272,128]{1,0:T(8,128)(2,1)S(1)}, u32[]{:S(2)}, u32[]{:S(2)}) collective-permute-start(bf16[272,128]{1,0:T(8,128)(2,1)} %get-tuple-element.83), channel_id=1, source_target_pairs={{0,96},{16,112},{32,0},{48,16},{64,32},{80,48},{96,64},{112,80},{1... | collective-permute-start | bytes 208904 | tf_op jit(solution)/shard_map/ppermute | solution.py:423
  158.5 2.4 %copy-start.33 = (bf16[272,128]{1,0:T(8,128)(2,1)}, bf16[272,128]{1,0:T(8,128)(2,1)S(1)}, u32[]{:S(2)}) copy-start(bf16[272,128]{1,0:T(8,128)(2,1)S(1)} %collective-permute-done.16.one_ref) | copy-start | bytes 208900
  160.6 0.6 copy-start.34
  160.9 0.6 copy-start.35

commit v2 on v0

--- a/solution.py
+++ b/solution.py
@@ -23,6 +23,7 @@
 SCALING = DH ** (-0.5)
 ROWS_OUT = D // 8
 GATE_ROWS = 16
+ZS = 4
 F32 = jnp.float32
 BF16 = jnp.bfloat16
 MIB = 1 << 20
@@ -83,18 +84,23 @@
     )(ids, counts)
 
 
-def serve_kernel(wanted_ref, keys_ref, values_ref, out_ref, sem):
+def serve_kernel(wanted_ref, keys_ref, values_ref, out_ref, held, load_sems, store_sem):
     def issue(i, _):
         dest = i // CAP
         rank = i % CAP
         rows = pl.ds(pl.multiple_of(wanted_ref[dest, rank] * TILE, TILE), TILE)
         cols = pl.ds(pl.multiple_of(dest * DH, DH), DH)
-        pltpu.make_async_copy(keys_ref.at[rows, cols], out_ref.at[i, 0], sem).start()
-        pltpu.make_async_copy(values_ref.at[rows, cols], out_ref.at[i, 1], sem).start()
+        sem = load_sems.at[dest]
+        pltpu.make_async_copy(keys_ref.at[rows, cols], held.at[i, 0], sem).start()
+        pltpu.make_async_copy(values_ref.at[rows, cols], held.at[i, 1], sem).start()
         return 0
 
     lax.fori_loop(0, MEMS * CAP, issue, 0, unroll=4)
-    pltpu.make_async_copy(out_ref, out_ref, sem).wait()
+    for dest in range(MEMS):
+        mine = pl.ds(dest * CAP, CAP)
+        pltpu.make_async_copy(out_ref.at[mine], held.at[mine], load_sems.at[dest]).wait()
+        pltpu.make_async_copy(held.at[mine], out_ref.at[mine], store_sem).start()
+    pltpu.make_async_copy(held, out_ref, store_sem).wait()
 
 
 def serve(wanted, keys, values):
@@ -104,7 +110,12 @@
         out_shape=jax.ShapeDtypeStruct((MEMS * CAP, 2, TILE, DH), BF16),
         in_specs=[pl.BlockSpec(memory_space=pltpu.SMEM), hbm, hbm],
         out_specs=hbm,
-        scratch_shapes=[pltpu.SemaphoreType.DMA(())],
+        scratch_shapes=[
+            pltpu.VMEM((MEMS * CAP, 2, TILE, DH), BF16),
+            pltpu.SemaphoreType.DMA((MEMS,)),
+            pltpu.SemaphoreType.DMA(()),
+        ],
+        compiler_params=pltpu.CompilerParams(vmem_limit_bytes=48 * MIB),
         cost_estimate=pl.CostEstimate(flops=0, bytes_accessed=12 * MIB, transcendentals=0),
         name="serve",
     )(wanted, keys, values)
@@ -112,7 +123,7 @@
 
 def local_kernel(
     tokens_ref, wq_ref, wk_ref, wv_ref, cot_ref, bias_ref,
-    queries_ref, out_ref, dq_ref, grad_ref, weights, total,
+    queries_ref, out_ref, dq_ref, mine_ref, other_ref, weights, total,
 ):
     step = pl.program_id(0)
 
@@ -156,12 +167,19 @@
 
     @pl.when(step == SEGS - 1)
     def _():
-        grad_ref[...] = total[...].astype(BF16)
+        me = lax.axis_index("dp")
+        core = lax.rem(me, 2)
+        for z in range(ZS):
+            owner = lax.rem(me // 2 + z, ZS) * 2
+            for part_ref, side in ((mine_ref, core), (other_ref, 1 - core)):
+                at = pl.ds(pl.multiple_of((owner + side) * ROWS_OUT, ROWS_OUT), ROWS_OUT)
+                part_ref[z] = total[at, :].astype(part_ref.dtype)
 
 
 def local_part(tokens, w_query, w_key, w_value, cot, bias):
     seg = lambda width: pl.BlockSpec((SEG, width), lambda i: (i, 0))
     whole = pl.BlockSpec((D, DH), lambda i: (0, 0), pipeline_mode=pl.Buffered(1))
+    fixed = pl.BlockSpec((ZS, ROWS_OUT, 2 * DH), lambda i: (0, 0, 0))
     return pl.pallas_call(
         local_kernel,
         grid=(SEGS,),
@@ -169,10 +187,11 @@
             jax.ShapeDtypeStruct((TOK, DH), BF16),
             jax.ShapeDtypeStruct((TOK, DH), F32),
             jax.ShapeDtypeStruct((TOK, DH), F32),
-            jax.ShapeDtypeStruct((D, 2 * DH), BF16),
+            jax.ShapeDtypeStruct((ZS, ROWS_OUT, 2 * DH), F32),
+            jax.ShapeDtypeStruct((ZS, ROWS_OUT, 2 * DH), BF16),
         ),
         in_specs=[seg(D), whole, whole, whole, seg(DH), pl.BlockSpec(memory_space=pltpu.SMEM)],
-        out_specs=(seg(DH), seg(DH), seg(DH), pl.BlockSpec((D, 2 * DH), lambda i: (0, 0))),
+        out_specs=(seg(DH), seg(DH), seg(DH), fixed, fixed),
         scratch_shapes=[pltpu.VMEM((D, 3 * DH), BF16), pltpu.VMEM((D, 2 * DH), F32)],
         compiler_params=pltpu.CompilerParams(
             dimension_semantics=("arbitrary",), vmem_limit_bytes=48 * MIB
@@ -184,112 +203,185 @@
     )(tokens, w_query, w_key, w_value, cot, bias)
 
 
+CLASSES = ((2, 6), (4, 3), (8, 3))
+
+
+def attend_all(members, tiles_n, refs):
+    gate, tiles, queries_ref, local_ref, ldq_ref, cot_ref, attended_ref, grads = refs
+    width = tiles_n * TILE
+    at = [pl.ds(pl.multiple_of(block * QB, QB), QB) for block, _, _ in members]
+    entries = [pl.ds(block * TOP, tiles_n) for block, _, _ in members]
+    keys = [tiles[e, 0].reshape(width, DH) for e in entries]
+    values = [tiles[e, 1].reshape(width, DH) for e in entries]
+    up = [cot_ref[rows, :].astype(F32) for rows in at]
+    queries = [queries_ref[rows, :] for rows in at]
+    scores = [dot(k, q, NT) for k, q in zip(keys, queries)]
+    back = [dot(v, (gate * u).astype(BF16), NT) for v, u in zip(values, up)]
+    probs = []
+    for s, (_, _, count) in zip(scores, members):
+        s = jnp.where(iota((width, QB), 0) < count * TILE, s * SCALING, -jnp.inf)
+        raised = jnp.exp(s - jnp.max(s, axis=0, keepdims=True))
+        probs.append(raised * (1.0 / jnp.sum(raised, axis=0, keepdims=True)))
+    out = [dot(p.astype(BF16), v, TN) for p, v in zip(probs, values)]
+    dscore = [
+        p * (b - jnp.sum(b * p, axis=0, keepdims=True)) * SCALING for p, b in zip(probs, back)
+    ]
+    dq = [dot(d.astype(BF16), k, TN) for d, k in zip(dscore, keys)]
+    local = [local_ref[rows, :] for rows in at]
+    ldq = [ldq_ref[rows, :] for rows in at]
+    terms = jnp.zeros((1, DH), F32)
+    for u, o, lo, (_, valid, _) in zip(up, out, local, members):
+        terms += jnp.where(valid, jnp.sum(u * (o - lo), axis=0, keepdims=True), 0.0)
+    for rows, o, lo, d, ld in zip(at, out, local, dq, ldq):
+        attended_ref[rows, :] = (gate * o + (1.0 - gate) * lo).astype(BF16)
+        grads[rows, :] = (d + ld).astype(BF16)
+    return terms
+
+
 def memory_kernel(
     counts_ref, slot_ref, bias_ref, tiles_ref, queries_ref, local_ref, ldq_ref, cot_ref, tokens_ref,
-    attended_ref, grad_ref, tiles, total, grads, gate_sum, sems,
+    attended_ref, mine_ref, other_ref, tiles, tokens, total, grads, gate_sum, lists, sems, token_sems,
 ):
-    step = pl.program_id(0)
-    per_step = SEG // QB
-
-    @pl.when(step == 0)
-    def _():
-        total[...] = jnp.zeros_like(total)
-        gate_sum[...] = jnp.zeros_like(gate_sum)
-
-        def issue(i, _):
-            live = i % TOP < counts_ref[0, i // TOP]
-
-            @pl.when(live)
-            def _():
-                pltpu.make_async_copy(tiles_ref.at[slot_ref[0, i]], tiles.at[i], sems.at[i]).start()
-
-            @pl.when(jnp.logical_not(live))
-            def _():
-                tiles[i] = jnp.zeros((2, TILE, DH), BF16)
-
+    def sort(block, sizes):
+        count = counts_ref[0, block]
+
+        def fetch(slot, _):
+            entry = block * TOP + slot
+            pltpu.make_async_copy(tiles_ref.at[slot_ref[0, entry]], tiles.at[entry], sems.at[entry]).start()
             return 0
 
-        lax.fori_loop(0, ENTRIES, issue, 0)
-
-    def arrive(i, _):
-        entry = step * (per_step * TOP) + i
-
-        @pl.when(entry % TOP < counts_ref[0, entry // TOP])
-        def _():
-            pltpu.make_async_copy(tiles_ref.at[0], tiles.at[entry], sems.at[entry]).wait()
-
-        return 0
-
-    lax.fori_loop(0, per_step * TOP, arrive, 0)
+        lax.fori_loop(0, count, fetch, 0)
+        sizes = list(sizes)
+        low = 0
+        for at, (tiles_n, _) in enumerate(CLASSES):
+            here = (count > low) & (count <= tiles_n)
+
+            @pl.when(here)
+            def _(at=at, tiles_n=tiles_n):
+                lists[at, sizes[at]] = block
+
+                def clear(slot, _):
+                    tiles[block * TOP + slot] = jnp.zeros((2, TILE, DH), BF16)
+                    return 0
+
+                lax.fori_loop(count, tiles_n, clear, 0)
+
+            sizes[at] = sizes[at] + here.astype(jnp.int32)
+            low = tiles_n
+        return tuple(sizes)
+
+    sizes = lax.fori_loop(0, NQB, sort, (jnp.int32(0),) * len(CLASSES))
+    for part in range(SEGS):
+        rows = pl.ds(part * SEG, SEG)
+        pltpu.make_async_copy(tokens_ref.at[rows], tokens.at[rows], token_sems.at[part]).start()
     gate = gate_row(bias_ref)
-    terms = jnp.zeros((1, DH), F32)
-    for part in range(per_step):
-        rows = slice(part * QB, (part + 1) * QB)
-        block = step * per_step + part
-        entries = pl.ds(block * TOP, TOP)
-        keys = tiles[entries, 0].reshape(TOP * TILE, DH)
-        values = tiles[entries, 1].reshape(TOP * TILE, DH)
-        up = cot_ref[rows, :].astype(F32)
-        local = local_ref[rows, :]
-        scores = dot(queries_ref[rows, :], keys, NT) * SCALING
-        live = iota((QB, TOP * TILE), 1) < counts_ref[0, block] * TILE
-        scores = jnp.where(live, scores, -jnp.inf)
-        raised = jnp.exp(scores - jnp.max(scores, axis=1, keepdims=True))
-        probs = raised * (1.0 / jnp.sum(raised, axis=1, keepdims=True))
-        out = dot(probs.astype(BF16), values)
-        back = dot((gate * up).astype(BF16), values, NT)
-        dscore = probs * (back - jnp.sum(back * probs, axis=1, keepdims=True)) * SCALING
-        dq = dot(dscore.astype(BF16), keys)
-        attended_ref[rows, :] = (gate * out + (1.0 - gate) * local).astype(BF16)
-        terms += jnp.sum(up * (out - local), axis=0, keepdims=True)
-        grads[rows, :] = (dq + ldq_ref[rows, :]).astype(BF16)
-    gate_sum[...] += terms
-    total[...] += dot(tokens_ref[...], grads[...], TN)
-
-    @pl.when(step == SEGS - 1)
-    def _():
-        grad_ref[:, :ROWS_OUT, :] = total[...].astype(BF16).reshape(8, ROWS_OUT, DH)
-        term = gate_sum[...]
-        high = term.astype(BF16)
-        rest = term - high.astype(F32)
-        mid = rest.astype(BF16)
-        low = (rest - mid.astype(F32)).astype(BF16)
-        at = iota((GATE_ROWS, DH), 0)
-        spread = lambda row: jnp.broadcast_to(row.astype(F32), (GATE_ROWS, DH))
-        extra = jnp.where(at == 0, spread(high), jnp.where(at == 1, spread(mid), spread(low)))
-        extra = jnp.where(at < 3, extra, 0.0).astype(BF16)
-        for owner in range(8):
-            grad_ref[owner, ROWS_OUT:, :] = extra
+    gate_sum[...] = jnp.zeros_like(gate_sum)
+    for at, (tiles_n, group) in enumerate(CLASSES):
+
+        def batch(i, _, at=at, tiles_n=tiles_n, group=group):
+            members = []
+            for k in range(group):
+                valid = i * group + k < sizes[at]
+                block = lists[at, jnp.minimum(i * group + k, sizes[at] - 1)]
+                count = counts_ref[0, block]
+                members.append((block, valid, count))
+
+                def arrive(slot, _):
+                    entry = block * TOP + slot
+                    pltpu.make_async_copy(
+                        tiles_ref.at[0], tiles.at[entry], sems.at[entry]
+                    ).wait()
+                    return 0
+
+                lax.fori_loop(0, jnp.where(valid, count, 0), arrive, 0)
+            terms = attend_all(
+                members, tiles_n,
+                (gate, tiles, queries_ref, local_ref, ldq_ref, cot_ref, attended_ref, grads),
+            )
+            gate_sum[...] += terms
+            return 0
+
+        lax.fori_loop(0, pl.cdiv(sizes[at], group), batch, 0)
+    for part in range(SEGS):
+        rows = pl.ds(part * SEG, SEG)
+        pltpu.make_async_copy(tokens_ref.at[rows], tokens.at[rows], token_sems.at[part]).wait()
+        term = dot(grads[rows, :], tokens[rows, :], TN)
+        if part == 0:
+            total[...] = term
+        else:
+            total[...] += term
+    me = lax.axis_index("dp")
+    core = lax.rem(me, 2)
+    extra = split_gate(gate_sum[...])
+    for step in range(ZS):
+        owner = lax.rem(me // 2 + step, ZS) * 2
+        for out_ref, side in ((mine_ref, core), (other_ref, 1 - core)):
+            cols = pl.ds(pl.multiple_of((owner + side) * ROWS_OUT, ROWS_OUT), ROWS_OUT)
+            out_ref[step, :ROWS_OUT, :] = total[:, cols].T.astype(out_ref.dtype)
+        mine_ref[step, ROWS_OUT:, :] = extra[0]
+        other_ref[step, ROWS_OUT:, :] = extra[1].astype(BF16)
+
+
+def split_gate(term):
+    high = term.astype(BF16).astype(F32)
+    mid = (term - high).astype(BF16).astype(F32)
+    low = term - high - mid
+    at = iota((GATE_ROWS, DH), 0)
+    spread = lambda row: jnp.broadcast_to(row, (GATE_ROWS, DH))
+    parts = []
+    for first in (0, 3):
+        row = jnp.where(at == first, spread(high), jnp.where(at == first + 1, spread(mid), spread(low)))
+        parts.append(jnp.where((at >= first) & (at < first + 3), row, 0.0))
+    return parts
 
 
 def memory_part(counts, slots, bias, tiles, queries, local, ldq, cot, tokens):
-    seg = lambda width: pl.BlockSpec((SEG, width), lambda i: (i, 0))
     smem = pl.BlockSpec(memory_space=pltpu.SMEM)
+    vmem = pl.BlockSpec(memory_space=pltpu.VMEM)
+    hbm = pl.BlockSpec(memory_space=pl.ANY)
     rows = ROWS_OUT + GATE_ROWS
     return pl.pallas_call(
         memory_kernel,
-        grid=(SEGS,),
         out_shape=(
             jax.ShapeDtypeStruct((TOK, DH), BF16),
-            jax.ShapeDtypeStruct((8, rows, DH), BF16),
-        ),
-        in_specs=[smem, smem, smem, pl.BlockSpec(memory_space=pl.ANY), seg(DH), seg(DH), seg(DH), seg(DH), seg(D)],
-        out_specs=(seg(DH), pl.BlockSpec((8, rows, DH), lambda i: (0, 0, 0))),
+            jax.ShapeDtypeStruct((ZS, rows, DH), F32),
+            jax.ShapeDtypeStruct((ZS, rows, DH), BF16),
+        ),
+        in_specs=[smem] * 3 + [hbm] + [vmem] * 4 + [hbm],
+        out_specs=(vmem, vmem, vmem),
         scratch_shapes=[
             pltpu.VMEM((ENTRIES, 2, TILE, DH), BF16),
-            pltpu.VMEM((D, DH), F32),
-            pltpu.VMEM((SEG, DH), BF16),
+            pltpu.VMEM((TOK, D), BF16),
+            pltpu.VMEM((DH, D), F32),
+            pltpu.VMEM((TOK, DH), BF16),
             pltpu.VMEM((1, DH), F32),
+            pltpu.SMEM((len(CLASSES), 32), jnp.int32),
             pltpu.SemaphoreType.DMA((ENTRIES,)),
+            pltpu.SemaphoreType.DMA((SEGS,)),
         ],
-        compiler_params=pltpu.CompilerParams(
-            dimension_semantics=("arbitrary",), vmem_limit_bytes=48 * MIB
-        ),
+        compiler_params=pltpu.CompilerParams(vmem_limit_bytes=48 * MIB),
         cost_estimate=pl.CostEstimate(
             flops=8_000_000_000, bytes_accessed=24 * MIB, transcendentals=1_600_000
         ),
         name="memory",
     )(counts, slots, bias, tiles, queries, local, ldq, cot, tokens)
+
+
+def swap_cores(array):
+    return lax.ppermute(array, "dp", [(i, i ^ 1) for i in range(2 * ZS)])
+
+
+def along_z(array, step):
+    return lax.ppermute(array, "dp", [(i, (i + 2 * step) % (2 * ZS)) for i in range(2 * ZS)])
+
+
+def reduce_docs(mine, other):
+    got = swap_cores(other)
+    total = mine[0] + got[0].astype(F32)
+    for step in range(1, ZS):
+        both = (mine[step] + got[step].astype(F32)).astype(BF16)
+        total = total + along_z(both, step).astype(F32)
+    return total
 
 
 def exchange(array, axis):
@@ -316,17 +408,17 @@
     sent = serve(wanted, memory_keys[0], memory_values[0])
     hidden, sent = lax.optimization_barrier((hidden, sent))
     tiles = exchange(sent, "mem")
-    queries, local, ldq, grad_kv = local_part(hidden, w_query, w_key, w_value, cot, gate_bias)
-    shares_kv = exchange(grad_kv.reshape(8, ROWS_OUT, 2 * DH), "dp")
-    sum_kv = jnp.sum(shares_kv.astype(F32), axis=0)
-    attended, grad_q = memory_part(
+    queries, local, ldq, mine, other = local_part(hidden, w_query, w_key, w_value, cot, gate_bias)
+    sum_kv = reduce_docs(mine, other)
+    share_k, share_v = sum_kv[:, :DH], sum_kv[:, DH:]
+    counts, share_k, share_v = lax.optimization_barrier((counts, share_k, share_v))
+    attended, mine, other = memory_part(
         counts, slots, gate_bias, tiles, queries, local, ldq, cot, hidden
     )
-    shares_q = exchange(grad_q, "dp").astype(F32)
-    share_q = jnp.sum(shares_q[:, :ROWS_OUT], axis=0)
+    total = reduce_docs(mine, other)
     gate = jax.nn.sigmoid(gate_bias)
-    gate_total = jnp.sum(shares_q[:, ROWS_OUT : ROWS_OUT + 3]) * gate * (1.0 - gate)
-    return (attended[None], share_q, sum_kv[:, :DH], sum_kv[:, DH:], gate_total)
+    gate_total = jnp.sum(total[ROWS_OUT : ROWS_OUT + 6]) * gate * (1.0 - gate)
+    return (attended[None], total[:ROWS_OUT], share_k, share_v, gate_total)
 
 
 def solution(mesh):

time: 365 us -> 153 us (0.42)
  Pallas kernels: 250 us -> 44.1 us
  waiting for transfers between devices: 71.7 us -> 61.5 us
    pallas_call x1, Pallas kernels: 192 us -> 6.05 us  [serve(): pl.pallas_call(serve_kernel, out_shape=jax.ShapeDtypeStruct((MEMS * CAP,...]
    all_to_all x3 -> x1, waiting for transfers between devices: 71.7 us -> 50 us  [exchange(): return lax.all_to_all(array, axis, split_axis=0, concat_axis=0, tiled=True)]
    pallas_call x1, Pallas kernels: 31.8 us -> 12.5 us  [memory_part(): pl.pallas_call(memory_kernel, out_shape=(jax.ShapeDtypeStruct((TOK, DH),...]
    ppermute x0 -> x8, starting transfers between devices: none -> 16.2 us  [the longest x6 11 us: along_z(): lax.ppermute(array, 'dp', [(i, (i + 2 * step) % (2 * ZS)) for i in range(...]
    all_to_all x3 -> x1, starting transfers between devices: 18 us -> 4.78 us  [exchange(): return lax.all_to_all(array, axis, split_axis=0, concat_axis=0, tiled=True)]
    ppermute x0 -> x8, waiting for transfers between devices: none -> 11.5 us  [the longest x6 8.78 us: along_z(): lax.ppermute(array, 'dp', [(i, (i + 2 * step) % (2 * ZS)) for i in range(...]
  transfers between devices with their start and end apart: 3 -> 9, of which waited for: 2 -> 7; matrix products, arithmetic and copies ran while one was open for 1% -> 1% of each run, Pallas kernels for 15% -> 16%
where the time goes in v2:
time: 153 us; the launch traced here: 150 us
  waiting for transfers between devices  61.5 us (40%)
  Pallas kernels  44.1 us (29%)
  starting transfers between devices  21 us (14%)
  blocking collectives  13.9 us (9%)
  local copies, waits for them, and re-layouts  5.59 us (4%)
  between operations  3.28 us (2%)
    all_to_all x1, waiting for transfers between devices, exchange(): return lax.all_to_all(array, axis, split_axis=0, concat_axis=0, tiled=True)  50 us
    pallas_call x1, Pallas kernels, local_part(): pl.pallas_call(local_kernel, grid=(SEGS,), out_shape=(jax.ShapeDtypeStruc...  23.8 us
    all_to_all x1, blocking collectives, exchange(): return lax.all_to_all(array, axis, split_axis=0, concat_axis=0, tiled=True)  13.9 us
    pallas_call x1, Pallas kernels, memory_part(): pl.pallas_call(memory_kernel, out_shape=(jax.ShapeDtypeStruct((TOK, DH),...  12.5 us
    ppermute x6, starting transfers between devices, along_z(): lax.ppermute(array, 'dp', [(i, (i + 2 * step) % (2 * ZS)) for i in range(...  11 us
    ppermute x6, waiting for transfers between devices, along_z(): lax.ppermute(array, 'dp', [(i, (i + 2 * step) % (2 * ZS)) for i in range(...  8.78 us
    pallas_call x1, Pallas kernels, serve(): pl.pallas_call(serve_kernel, out_shape=jax.ShapeDtypeStruct((MEMS * CAP,...  6.05 us
    ppermute x2, starting transfers between devices, swap_cores(): return lax.ppermute(array, 'dp', [(i, i ^ 1) for i in range(2 * ZS)])  5.14 us
  transfers between devices with their start and end apart: 9, of which 7 were waited for; matrix products, arithmetic and copies ran while one was open for 1% of the time, Pallas kernels for 16%

profile of v2, /device:TPU:1, one launch (start us, length us, event | category | flops | bytes accessed | tf_op | source)
XLA Modules:
  0.0 150.2 jit_solution(7806644194061902160)
XLA Ops:
  0.6 1.4 copy.16
  2.0 1.8 %request.1 = (s32[16,128]{1,0:T(8,128)}, s32[1,192]{1,0:T(1,128)}) custom-call(s32[24,8]{1,0:T(8,128)} %bitcast.43, s32[1,24]{1,0:T(1,128)} %bitcast.37), custom_call_target="tpu_custom_call" | custom-call | tf_op jit(solution)/shard_map/request/pallas_call | solution.py:77
  3.8 13.9 %all_to_all.16 = s32[16,1,128]{2,1,0:T(1,128)S(1)} all-to-all(s32[16,1,128]{2,1,0:T(1,128)} %bitcast.44), channel_id=1, replica_groups=mesh['dp'=8,'mem'=16] {'mem'}, dimensions={0} | all-to-all | bytes 16384 | tf_op jit(solution)/shard_map/all_to_all | solution.py:388
  17.7 6.0 %serve.1 = bf16[192,2,64,128]{3,2,1,0:T(8,128)(2,1)} custom-call(s32[16,128]{1,0:T(8,128)S(1)} %bitcast.36, bf16[1536,2048]{1,0:T(8,128)(2,1)} %bitcast.41, bf16[1536,2048]{1,0:T(8,128)(2,1)} %bitcast.42), custom_call_target="tpu_custom_call" | custom-call | bytes 12582912 | tf_op jit(solution)/shard_map/serve/pallas_call | solution.py:108
  23.7 0.0 copy-start.1
  23.7 0.0 copy-start.2
  23.7 0.0 copy-start.3
  23.8 0.0 copy-start.4
  23.8 4.8 %all-to-all-start.1 = ((bf16[192,2,64,128]{3,2,1,0:T(8,128)(2,1)}), bf16[192,2,64,128]{3,2,1,0:T(8,128)(2,1)}, u32[]{:S(2)}, u32[]{:S(2)}) async-start(bf16[192,2,64,128]{3,2,1,0:T(8,128)(2,1)} %serve.1), calls=%async_computation.1 | async-start | bytes 12582912 | tf_op jit(solution)/shard_map/all_to_all | solution.py:388
  29.2 0.0 copy-done.1
  29.2 0.0 copy-done.2
  29.2 0.0 copy-done.3
  29.2 0.0 copy-done.4
  29.3 0.0 copy-start
  29.3 0.0 copy-start.5
  29.3 23.8 %local.1 = (bf16[3072,128]{1,0:T(8,128)(2,1)S(1)}, f32[3072,128]{1,0:T(8,128)}, f32[3072,128]{1,0:T(8,128)}, f32[4,256,256]{2,1,0:T(8,128)S(1)}, bf16[4,256,256]{2,1,0:T(8,128)(2,1)S(1)}) custom-call(bf16[3072,2048]{1,0:T(8,128)(2,1)} %bitcast.45, bf16[2048,128]{1,0:T(8,128)(2,1)S(1)} %copy-done.2, bf16[2048,128]{1,0:T(8,128)(2,1)S(1)} %copy-done.3, ...), custom_call_target="tpu_custom_call" | custom-call | flops 14000000000 | bytes 20971520 | tf_op jit(solution)/shard_map/local/pallas_call | solution.py:183
  53.1 2.1 %collective-permute-start = (bf16[4,256,256]{2,1,0:T(8,128)(2,1)S(1)}, bf16[4,256,256]{2,1,0:T(8,128)(2,1)S(1)}, u32[]{:S(2)}, u32[]{:S(2)}) collective-permute-start(bf16[4,256,256]{2,1,0:T(8,128)(2,1)S(1)} %get-tuple-element.23), channel_id=1, source_target_pairs={{0,16},{16,0},{32,48},{48,32},{64,80},{80,64},{96,112},{112,96},{1... | collective-permute-start | bytes 1572872 | tf_op jit(solution)/shard_map/ppermute | solution.py:371
  55.2 1.5 %collective-permute-done = bf16[4,256,256]{2,1,0:T(8,128)(2,1)S(1)} collective-permute-done((bf16[4,256,256]{2,1,0:T(8,128)(2,1)S(1)}, bf16[4,256,256]{2,1,0:T(8,128)(2,1)S(1)}, u32[]{:S(2)}, u32[]{:S(2)}) %collective-permute-start) | collective-permute-done | bytes 524320 | tf_op jit(solution)/shard_map/ppermute | solution.py:371
  56.7 0.1 fusion.4
  56.8 1.7 %collective-permute-start.1 = (bf16[256,256]{1,0:T(8,128)(2,1)S(1)}, bf16[256,256]{1,0:T(8,128)(2,1)S(1)}, u32[]{:S(2)}, u32[]{:S(2)}) collective-permute-start(bf16[256,256]{1,0:T(8,128)(2,1)S(1)} %get-tuple-element.35), channel_id=1, source_target_pairs={{0,32},{16,48},{32,64},{48,80},{64,96},{80,112},{96,0},{112,16},{1... | collective-permute-start | bytes 393224 | tf_op jit(solution)/shard_map/ppermute | solution.py:375
  58.5 2.2 %collective-permute-start.3 = (bf16[256,256]{1,0:T(8,128)(2,1)S(1)}, bf16[256,256]{1,0:T(8,128)(2,1)S(1)}, u32[]{:S(2)}, u32[]{:S(2)}) collective-permute-start(bf16[256,256]{1,0:T(8,128)(2,1)S(1)} %get-tuple-element.36), channel_id=1, source_target_pairs={{0,96},{16,112},{32,0},{48,16},{64,32},{80,48},{96,64},{112,80},{1... | collective-permute-start | bytes 393224 | tf_op jit(solution)/shard_map/ppermute | solution.py:375
  60.8 1.2 collective-permute-start.2
  62.0 2.4 %collective-permute-done.1 = bf16[256,256]{1,0:T(8,128)(2,1)S(1)} collective-permute-done((bf16[256,256]{1,0:T(8,128)(2,1)S(1)}, bf16[256,256]{1,0:T(8,128)(2,1)S(1)}, u32[]{:S(2)}, u32[]{:S(2)}) %collective-permute-start.1) | collective-permute-done | bytes 131104 | tf_op jit(solution)/shard_map/ppermute | solution.py:375
  64.4 0.0 collective-permute-done.3
  64.4 3.7 %collective-permute-done.2 = bf16[256,256]{1,0:T(8,128)(2,1)S(1)} collective-permute-done((bf16[256,256]{1,0:T(8,128)(2,1)S(1)}, bf16[256,256]{1,0:T(8,128)(2,1)S(1)}, u32[]{:S(2)}, u32[]{:S(2)}) %collective-permute-start.2) | collective-permute-done | bytes 131104 | tf_op jit(solution)/shard_map/ppermute | solution.py:375
  68.0 0.1 fusion.1
  68.1 0.7 fusion.10
  68.8 50.0 %all-to-all-done.1.tiles_ref = bf16[192,2,64,128]{3,2,1,0:T(8,128)(2,1)} async-done(((bf16[192,2,64,128]{3,2,1,0:T(8,128)(2,1)}), bf16[192,2,64,128]{3,2,1,0:T(8,128)(2,1)}, u32[]{:S(2)}, u32[]{:S(2)}) %all-to-all-start.1) | async-done | bytes 6291488 | tf_op jit(solution)/shard_map/all_to_all | solution.py:388
  118.8 0.0 copy-done
  118.9 0.0 copy-done.5
  118.9 0.0 copy-start.6
  118.9 1.4 copy-done.6
  120.3 0.0 copy-start.7
  120.3 1.4 copy-done.7
  121.7 12.5 %memory.1 = (bf16[3072,128]{1,0:T(8,128)(2,1)}, f32[4,272,128]{2,1,0:T(8,128)S(1)}, bf16[4,272,128]{2,1,0:T(8,128)(2,1)S(1)}) custom-call(s32[1,24]{1,0:T(1,128)S(1)} %bitcast.38, s32[1,192]{1,0:T(1,128)S(1)} %copy-done.5, f32[1]{0:T(128)S(6)} %copy.18.bias_ref, bf16[192,2,64,128]{3,2,1,0:T(8,128)(2,1)} %all-to-all-done.1.tiles_ref, ...), custom_call_target="tpu_custom_call" | custom-call | flops 8000000000 | bytes 25165824 | tf_op jit(solution)/shard_map/memory/pallas_call | solution.py:343
  134.1 3.0 %collective-permute-start.4 = (bf16[4,272,128]{2,1,0:T(8,128)(2,1)S(1)}, bf16[4,272,128]{2,1,0:T(8,128)(2,1)S(1)}, u32[]{:S(2)}, u32[]{:S(2)}) collective-permute-start(bf16[4,272,128]{2,1,0:T(8,128)(2,1)S(1)} %get-tuple-element.32), channel_id=1, source_target_pairs={{0,16},{16,0},{32,48},{48,32},{64,80},{80,64},{96,112},{112,96},{1... | collective-permute-start | bytes 835592 | tf_op jit(solution)/shard_map/ppermute | solution.py:371
  137.2 1.2 collective-permute-done.4
  138.4 0.1 fusion.7
  138.4 4.0 %collective-permute-start.5 = (bf16[272,128]{1,0:T(8,128)(2,1)S(1)}, bf16[272,128]{1,0:T(8,128)(2,1)S(1)}, u32[]{:S(2)}, u32[]{:S(2)}) collective-permute-start(bf16[272,128]{1,0:T(8,128)(2,1)S(1)} %get-tuple-element.38), channel_id=1, source_target_pairs={{0,32},{16,48},{32,64},{48,80},{64,96},{80,112},{96,0},{112,16},{1... | collective-permute-start | bytes 208904 | tf_op jit(solution)/shard_map/ppermute | solution.py:375
  142.5 0.0 collective-permute-start.7
  142.5 1.9 %collective-permute-start.6 = (bf16[272,128]{1,0:T(8,128)(2,1)S(1)}, bf16[272,128]{1,0:T(8,128)(2,1)S(1)}, u32[]{:S(2)}, u32[]{:S(2)}) collective-permute-start(bf16[272,128]{1,0:T(8,128)(2,1)S(1)} %get-tuple-element.40), channel_id=1, source_target_pairs={{0,64},{16,80},{32,96},{48,112},{64,0},{80,16},{96,32},{112,48},{1... | collective-permute-start | bytes 208904 | tf_op jit(solution)/shard_map/ppermute | solution.py:375
  144.4 0.0 collective-permute-done.5
  144.4 1.2 collective-permute-done.7
  145.6 1.5 %collective-permute-done.6 = bf16[272,128]{1,0:T(8,128)(2,1)S(1)} collective-permute-done((bf16[272,128]{1,0:T(8,128)(2,1)S(1)}, bf16[272,128]{1,0:T(8,128)(2,1)S(1)}, u32[]{:S(2)}, u32[]{:S(2)}) %collective-permute-start.6) | collective-permute-done | bytes 69664 | tf_op jit(solution)/shard_map/ppermute | solution.py:375
  147.2 0.6 slice_reduce_fusion
  147.8 0.7 slice.90
  (1 shorter events, 0.0 us)
Async XLA Ops:
  23.7 5.5 %copy-start.1 = (bf16[1,3072,128]{2,1,0:T(8,128)(2,1)S(1)}, bf16[1,3072,128]{2,1,0:T(8,128)(2,1)}, u32[]{:S(2)}) copy-start(bf16[1,3072,128]{2,1,0:T(8,128)(2,1)} %param.19) | copy-start | bytes 2359300
  23.7 5.5 %copy-start.2 = (bf16[2048,128]{1,0:T(8,128)(2,1)S(1)}, bf16[2048,128]{1,0:T(8,128)(2,1)}, u32[]{:S(2)}) copy-start(bf16[2048,128]{1,0:T(8,128)(2,1)} %wq_ref.1) | copy-start | bytes 1572868
  23.7 5.5 %copy-start.3 = (bf16[2048,128]{1,0:T(8,128)(2,1)S(1)}, bf16[2048,128]{1,0:T(8,128)(2,1)}, u32[]{:S(2)}) copy-start(bf16[2048,128]{1,0:T(8,128)(2,1)} %wk_ref.1) | copy-start | bytes 1572868
  23.8 5.5 %copy-start.4 = (bf16[2048,128]{1,0:T(8,128)(2,1)S(1)}, bf16[2048,128]{1,0:T(8,128)(2,1)}, u32[]{:S(2)}) copy-start(bf16[2048,128]{1,0:T(8,128)(2,1)} %wv_ref.1) | copy-start | bytes 1572868
  23.8 95.1 %all-to-all-start.1 = ((bf16[192,2,64,128]{3,2,1,0:T(8,128)(2,1)}), bf16[192,2,64,128]{3,2,1,0:T(8,128)(2,1)}, u32[]{:S(2)}, u32[]{:S(2)}) async-start(bf16[192,2,64,128]{3,2,1,0:T(8,128)(2,1)} %serve.1), calls=%async_computation.1 | async-start | bytes 12582912 | tf_op jit(solution)/shard_map/all_to_all | solution.py:388
  29.3 89.6 %copy-start = (s32[1,1,24]{2,1,0:T(1,128)S(1)}, s32[1,1,24]{2,1,0:T(1,128)}, u32[]{:S(2)}) copy-start(s32[1,1,24]{2,1,0:T(1,128)} %param.18) | copy-start | bytes 292
  29.3 89.6 %copy-start.5 = (s32[1,192]{1,0:T(1,128)S(1)}, s32[1,192]{1,0:T(1,128)}, u32[]{:S(2)}) copy-start(s32[1,192]{1,0:T(1,128)} %get-tuple-element.25.slot_ref) | copy-start | bytes 2308
  53.1 3.6 %collective-permute-start = (bf16[4,256,256]{2,1,0:T(8,128)(2,1)S(1)}, bf16[4,256,256]{2,1,0:T(8,128)(2,1)S(1)}, u32[]{:S(2)}, u32[]{:S(2)}) collective-permute-start(bf16[4,256,256]{2,1,0:T(8,128)(2,1)S(1)} %get-tuple-element.23), channel_id=1, source_target_pairs={{0,16},{16,0},{32,48},{48,32},{64,80},{80,64},{96,112},{112,96},{1... | collective-permute-start | bytes 1572872 | tf_op jit(solution)/shard_map/ppermute | solution.py:371
  56.8 7.5 %collective-permute-start.1 = (bf16[256,256]{1,0:T(8,128)(2,1)S(1)}, bf16[256,256]{1,0:T(8,128)(2,1)S(1)}, u32[]{:S(2)}, u32[]{:S(2)}) collective-permute-start(bf16[256,256]{1,0:T(8,128)(2,1)S(1)} %get-tuple-element.35), channel_id=1, source_target_pairs={{0,32},{16,48},{32,64},{48,80},{64,96},{80,112},{96,0},{112,16},{1... | collective-permute-start | bytes 393224 | tf_op jit(solution)/shard_map/ppermute | solution.py:375
  58.5 5.8 %collective-permute-start.3 = (bf16[256,256]{1,0:T(8,128)(2,1)S(1)}, bf16[256,256]{1,0:T(8,128)(2,1)S(1)}, u32[]{:S(2)}, u32[]{:S(2)}) collective-permute-start(bf16[256,256]{1,0:T(8,128)(2,1)S(1)} %get-tuple-element.36), channel_id=1, source_target_pairs={{0,96},{16,112},{32,0},{48,16},{64,32},{80,48},{96,64},{112,80},{1... | collective-permute-start | bytes 393224 | tf_op jit(solution)/shard_map/ppermute | solution.py:375
  60.8 7.3 %collective-permute-start.2 = (bf16[256,256]{1,0:T(8,128)(2,1)S(1)}, bf16[256,256]{1,0:T(8,128)(2,1)S(1)}, u32[]{:S(2)}, u32[]{:S(2)}) collective-permute-start(bf16[256,256]{1,0:T(8,128)(2,1)S(1)} %get-tuple-element.37), channel_id=1, source_target_pairs={{0,64},{16,80},{32,96},{48,112},{64,0},{80,16},{96,32},{112,48},{1... | collective-permute-start | bytes 393224 | tf_op jit(solution)/shard_map/ppermute | solution.py:375
  118.9 1.4 copy-start.6
  120.3 1.4 copy-start.7
  134.1 4.2 %collective-permute-start.4 = (bf16[4,272,128]{2,1,0:T(8,128)(2,1)S(1)}, bf16[4,272,128]{2,1,0:T(8,128)(2,1)S(1)}, u32[]{:S(2)}, u32[]{:S(2)}) collective-permute-start(bf16[4,272,128]{2,1,0:T(8,128)(2,1)S(1)} %get-tuple-element.32), channel_id=1, source_target_pairs={{0,16},{16,0},{32,48},{48,32},{64,80},{80,64},{96,112},{112,96},{1... | collective-permute-start | bytes 835592 | tf_op jit(solution)/shard_map/ppermute | solution.py:371
  138.4 6.0 %collective-permute-start.5 = (bf16[272,128]{1,0:T(8,128)(2,1)S(1)}, bf16[272,128]{1,0:T(8,128)(2,1)S(1)}, u32[]{:S(2)}, u32[]{:S(2)}) collective-permute-start(bf16[272,128]{1,0:T(8,128)(2,1)S(1)} %get-tuple-element.38), channel_id=1, source_target_pairs={{0,32},{16,48},{32,64},{48,80},{64,96},{80,112},{96,0},{112,16},{1... | collective-permute-start | bytes 208904 | tf_op jit(solution)/shard_map/ppermute | solution.py:375
  142.5 3.2 %collective-permute-start.7 = (bf16[272,128]{1,0:T(8,128)(2,1)S(1)}, bf16[272,128]{1,0:T(8,128)(2,1)S(1)}, u32[]{:S(2)}, u32[]{:S(2)}) collective-permute-start(bf16[272,128]{1,0:T(8,128)(2,1)S(1)} %get-tuple-element.39), channel_id=1, source_target_pairs={{0,96},{16,112},{32,0},{48,16},{64,32},{80,48},{96,64},{112,80},{1... | collective-permute-start | bytes 208904 | tf_op jit(solution)/shard_map/ppermute | solution.py:375
  142.5 4.7 %collective-permute-start.6 = (bf16[272,128]{1,0:T(8,128)(2,1)S(1)}, bf16[272,128]{1,0:T(8,128)(2,1)S(1)}, u32[]{:S(2)}, u32[]{:S(2)}) collective-permute-start(bf16[272,128]{1,0:T(8,128)(2,1)S(1)} %get-tuple-element.40), channel_id=1, source_target_pairs={{0,64},{16,80},{32,96},{48,112},{64,0},{80,16},{96,32},{112,48},{1... | collective-permute-start | bytes 208904 | tf_op jit(solution)/shard_map/ppermute | solution.py:375

commit v3 on v2

--- a/solution.py
+++ b/solution.py
@@ -51,14 +51,14 @@
     counts = counts_ref[...].astype(F32)
     by_block = (iota((ENTRIES, NQB), 0) // TOP == iota((ENTRIES, NQB), 1)).astype(F32)
     pick = (iota((ENTRIES, TOP), 0) % TOP == iota((ENTRIES, TOP), 1)).astype(F32)
-    owner_col = jnp.sum(dot(by_block, owner) * pick, axis=1, keepdims=True)
-    local_col = jnp.sum(dot(by_block, local) * pick, axis=1, keepdims=True)
+    owner_col = jnp.sum(dot(by_block, owner, NT) * pick, axis=1, keepdims=True)
+    local_col = jnp.sum(dot(by_block, local, NT) * pick, axis=1, keepdims=True)
     count_col = jnp.sum(by_block * counts, axis=1, keepdims=True)
     slot_col = (iota((ENTRIES, 1), 0) % TOP).astype(F32)
     owner_col = jnp.where(slot_col < count_col, owner_col, float(MEMS))
     of_block = (iota((NQB, ENTRIES), 1) // TOP == iota((NQB, ENTRIES), 0)).astype(F32)
     of_slot = (iota((TOP, ENTRIES), 1) % TOP == iota((TOP, ENTRIES), 0)).astype(F32)
-    owner_row = jnp.sum(dot(owner, of_slot) * of_block, axis=0, keepdims=True)
+    owner_row = jnp.sum(dot(owner, of_slot, TN) * of_block, axis=0, keepdims=True)
     count_row = dot(jnp.broadcast_to(counts, (8, NQB)), of_block)[:1]
     slot_row = (iota((1, ENTRIES), 1) % TOP).astype(F32)
     owner_row = jnp.where(slot_row < count_row, owner_row, float(MEMS))
@@ -207,7 +207,7 @@
 
 
 def attend_all(members, tiles_n, refs):
-    gate, tiles, queries_ref, local_ref, ldq_ref, cot_ref, attended_ref, grads = refs
+    gate, tiles, queries_ref, cot_ref, outs, dqs = refs
     width = tiles_n * TILE
     at = [pl.ds(pl.multiple_of(block * QB, QB), QB) for block, _, _ in members]
     entries = [pl.ds(block * TOP, tiles_n) for block, _, _ in members]
@@ -227,22 +227,21 @@
         p * (b - jnp.sum(b * p, axis=0, keepdims=True)) * SCALING for p, b in zip(probs, back)
     ]
     dq = [dot(d.astype(BF16), k, TN) for d, k in zip(dscore, keys)]
-    local = [local_ref[rows, :] for rows in at]
-    ldq = [ldq_ref[rows, :] for rows in at]
-    terms = jnp.zeros((1, DH), F32)
-    for u, o, lo, (_, valid, _) in zip(up, out, local, members):
-        terms += jnp.where(valid, jnp.sum(u * (o - lo), axis=0, keepdims=True), 0.0)
-    for rows, o, lo, d, ld in zip(at, out, local, dq, ldq):
-        attended_ref[rows, :] = (gate * o + (1.0 - gate) * lo).astype(BF16)
-        grads[rows, :] = (d + ld).astype(BF16)
-    return terms
+    for rows, o, d in zip(at, out, dq):
+        outs[rows, :] = o
+        dqs[rows, :] = d
 
 
 def memory_kernel(
-    counts_ref, slot_ref, bias_ref, tiles_ref, queries_ref, local_ref, ldq_ref, cot_ref, tokens_ref,
-    attended_ref, mine_ref, other_ref, tiles, tokens, total, grads, gate_sum, lists, sems, token_sems,
+    counts_ref, slot_ref, bias_ref, tiles_ref, queries_in, local_in, ldq_in, cot_in, tokens_ref,
+    attended_out, mine_ref, other_ref, tiles, tokens, total, grads, gate_sum, lists, sizes,
+    local_ref, ldq_ref, outs, dqs, queries_ref, cot_ref, attended_ref, sems, token_sems, row_sems,
+    out_sems,
 ):
-    def sort(block, sizes):
+    pltpu.make_async_copy(queries_in, queries_ref, row_sems.at[2]).start()
+    pltpu.make_async_copy(cot_in, cot_ref, row_sems.at[3]).start()
+
+    def sort(block, _):
         count = counts_ref[0, block]
 
         def fetch(slot, _):
@@ -251,31 +250,30 @@
             return 0
 
         lax.fori_loop(0, count, fetch, 0)
-        sizes = list(sizes)
-        low = 0
-        for at, (tiles_n, _) in enumerate(CLASSES):
-            here = (count > low) & (count <= tiles_n)
-
-            @pl.when(here)
-            def _(at=at, tiles_n=tiles_n):
-                lists[at, sizes[at]] = block
-
-                def clear(slot, _):
-                    tiles[block * TOP + slot] = jnp.zeros((2, TILE, DH), BF16)
-                    return 0
-
-                lax.fori_loop(count, tiles_n, clear, 0)
-
-            sizes[at] = sizes[at] + here.astype(jnp.int32)
-            low = tiles_n
-        return tuple(sizes)
-
-    sizes = lax.fori_loop(0, NQB, sort, (jnp.int32(0),) * len(CLASSES))
+        at = (count > 2).astype(jnp.int32) + (count > 4).astype(jnp.int32)
+        place = sizes[at]
+        lists[at, place] = block
+        sizes[at] = place + 1
+
+        def clear(slot, _):
+            tiles[block * TOP + slot] = jnp.zeros((2, TILE, DH), BF16)
+            return 0
+
+        lax.fori_loop(count, lax.shift_left(2, at), clear, 0)
+        return 0
+
+    for at in range(len(CLASSES)):
+        sizes[at] = 0
+    lax.fori_loop(0, NQB, sort, 0)
+    pltpu.make_async_copy(local_in, local_ref, row_sems.at[0]).start()
+    pltpu.make_async_copy(ldq_in, ldq_ref, row_sems.at[1]).start()
     for part in range(SEGS):
         rows = pl.ds(part * SEG, SEG)
         pltpu.make_async_copy(tokens_ref.at[rows], tokens.at[rows], token_sems.at[part]).start()
     gate = gate_row(bias_ref)
     gate_sum[...] = jnp.zeros_like(gate_sum)
+    pltpu.make_async_copy(queries_in, queries_ref, row_sems.at[2]).wait()
+    pltpu.make_async_copy(cot_in, cot_ref, row_sems.at[3]).wait()
     for at, (tiles_n, group) in enumerate(CLASSES):
 
         def batch(i, _, at=at, tiles_n=tiles_n, group=group):
@@ -294,14 +292,21 @@
                     return 0
 
                 lax.fori_loop(0, jnp.where(valid, count, 0), arrive, 0)
-            terms = attend_all(
-                members, tiles_n,
-                (gate, tiles, queries_ref, local_ref, ldq_ref, cot_ref, attended_ref, grads),
-            )
-            gate_sum[...] += terms
+            attend_all(members, tiles_n, (gate, tiles, queries_ref, cot_ref, outs, dqs))
             return 0
 
         lax.fori_loop(0, pl.cdiv(sizes[at], group), batch, 0)
+    pltpu.make_async_copy(local_in, local_ref, row_sems.at[0]).wait()
+    pltpu.make_async_copy(ldq_in, ldq_ref, row_sems.at[1]).wait()
+    for part in range(SEGS):
+        rows = pl.ds(part * SEG, SEG)
+        local = local_ref[rows, :]
+        out = outs[rows, :]
+        attended_ref[rows, :] = (gate * out + (1.0 - gate) * local).astype(BF16)
+        pltpu.make_async_copy(attended_ref.at[rows], attended_out.at[rows], out_sems.at[part]).start()
+        terms = cot_ref[rows, :].astype(F32) * (out - local)
+        gate_sum[...] += jnp.sum(terms, axis=0, keepdims=True)
+        grads[rows, :] = (dqs[rows, :] + ldq_ref[rows, :]).astype(BF16)
     for part in range(SEGS):
         rows = pl.ds(part * SEG, SEG)
         pltpu.make_async_copy(tokens_ref.at[rows], tokens.at[rows], token_sems.at[part]).wait()
@@ -320,6 +325,9 @@
             out_ref[step, :ROWS_OUT, :] = total[:, cols].T.astype(out_ref.dtype)
         mine_ref[step, ROWS_OUT:, :] = extra[0]
         other_ref[step, ROWS_OUT:, :] = extra[1].astype(BF16)
+    for part in range(SEGS):
+        rows = pl.ds(part * SEG, SEG)
+        pltpu.make_async_copy(attended_ref.at[rows], attended_out.at[rows], out_sems.at[part]).wait()
 
 
 def split_gate(term):
@@ -347,8 +355,8 @@
             jax.ShapeDtypeStruct((ZS, rows, DH), F32),
             jax.ShapeDtypeStruct((ZS, rows, DH), BF16),
         ),
-        in_specs=[smem] * 3 + [hbm] + [vmem] * 4 + [hbm],
-        out_specs=(vmem, vmem, vmem),
+        in_specs=[smem] * 3 + [hbm] * 6,
+        out_specs=(hbm, vmem, vmem),
         scratch_shapes=[
             pltpu.VMEM((ENTRIES, 2, TILE, DH), BF16),
             pltpu.VMEM((TOK, D), BF16),
@@ -356,10 +364,20 @@
             pltpu.VMEM((TOK, DH), BF16),
             pltpu.VMEM((1, DH), F32),
             pltpu.SMEM((len(CLASSES), 32), jnp.int32),
+            pltpu.SMEM((len(CLASSES),), jnp.int32),
+            pltpu.VMEM((TOK, DH), F32),
+            pltpu.VMEM((TOK, DH), F32),
+            pltpu.VMEM((TOK, DH), F32),
+            pltpu.VMEM((TOK, DH), F32),
+            pltpu.VMEM((TOK, DH), BF16),
+            pltpu.VMEM((TOK, DH), BF16),
+            pltpu.VMEM((TOK, DH), BF16),
             pltpu.SemaphoreType.DMA((ENTRIES,)),
             pltpu.SemaphoreType.DMA((SEGS,)),
+            pltpu.SemaphoreType.DMA((4,)),
+            pltpu.SemaphoreType.DMA((SEGS,)),
         ],
-        compiler_params=pltpu.CompilerParams(vmem_limit_bytes=48 * MIB),
+        compiler_params=pltpu.CompilerParams(vmem_limit_bytes=59 * MIB),
         cost_estimate=pl.CostEstimate(
             flops=8_000_000_000, bytes_accessed=24 * MIB, transcendentals=1_600_000
         ),
@@ -377,11 +395,11 @@
 
 def reduce_docs(mine, other):
     got = swap_cores(other)
-    total = mine[0] + got[0].astype(F32)
+    parts = [mine[0] + got[0].astype(F32)]
     for step in range(1, ZS):
         both = (mine[step] + got[step].astype(F32)).astype(BF16)
-        total = total + along_z(both, step).astype(F32)
-    return total
+        parts.append(along_z(both, step).astype(F32))
+    return parts
 
 
 def exchange(array, axis):
@@ -403,22 +421,24 @@
     hidden = tokens[0]
     cot = cotangent[0]
     counts = retrieval_counts.reshape(1, NQB)
-    table, slots = make_requests(retrieval_ids.reshape(NQB, TOP), counts)
+    table, slots = make_requests(retrieval_ids.reshape(NQB, TOP).T, counts)
     wanted = exchange(table, "mem")
     sent = serve(wanted, memory_keys[0], memory_values[0])
     hidden, sent = lax.optimization_barrier((hidden, sent))
     tiles = exchange(sent, "mem")
     queries, local, ldq, mine, other = local_part(hidden, w_query, w_key, w_value, cot, gate_bias)
-    sum_kv = reduce_docs(mine, other)
+    sum_kv = sum(reduce_docs(mine, other))
     share_k, share_v = sum_kv[:, :DH], sum_kv[:, DH:]
     counts, share_k, share_v = lax.optimization_barrier((counts, share_k, share_v))
     attended, mine, other = memory_part(
         counts, slots, gate_bias, tiles, queries, local, ldq, cot, hidden
     )
-    total = reduce_docs(mine, other)
+    parts = reduce_docs(mine, other)
+    share_q = sum(part[:ROWS_OUT] for part in parts)
+    gate_rows = sum(part[ROWS_OUT : ROWS_OUT + 6] for part in parts)
     gate = jax.nn.sigmoid(gate_bias)
-    gate_total = jnp.sum(total[ROWS_OUT : ROWS_OUT + 6]) * gate * (1.0 - gate)
-    return (attended[None], total[:ROWS_OUT], share_k, share_v, gate_total)
+    gate_total = jnp.sum(gate_rows) * gate * (1.0 - gate)
+    return (attended[None], share_q, share_k, share_v, gate_total)
 
 
 def solution(mesh):

time: 153 us -> 152 us (level); the launches traced: 150 us -> 152 us
  local copies, waits for them, and re-layouts: 5.59 us -> 0.75 us
  starting transfers between devices: 21 us -> 23.2 us
  other arithmetic: 0.85 us -> 2.66 us
    unnamed x17 -> x10, local copies, waits for them, and re-layouts: 4.21 us -> 0.03 us
    add x2 -> x3, other arithmetic: 0.12 us -> 1.94 us  [the longest x1 1.17 us: reduce_docs(): parts = [mine[0] + got[0].astype(F32)]]
    ppermute x2, starting transfers between devices: 5.14 us -> 6.7 us  [swap_cores(): return lax.ppermute(array, 'dp', [(i, i ^ 1) for i in range(2 * ZS)])]
where the time goes in v3:
time: 152 us
  waiting for transfers between devices  62.7 us (41%)
  Pallas kernels  45.6 us (30%)
  starting transfers between devices  23.2 us (15%)
  blocking collectives  13.9 us (9%)
  between operations  3.28 us (2%)
  other arithmetic  2.66 us (2%)
    all_to_all x1, waiting for transfers between devices, exchange(): return lax.all_to_all(array, axis, split_axis=0, concat_axis=0, tiled=True)  49.5 us
    pallas_call x1, Pallas kernels, local_part(): pl.pallas_call(local_kernel, grid=(SEGS,), out_shape=(jax.ShapeDtypeStruc...  23.8 us
    pallas_call x1, Pallas kernels, memory_part(): pl.pallas_call(memory_kernel, out_shape=(jax.ShapeDtypeStruct((TOK, DH),...  13.9 us
    all_to_all x1, blocking collectives, exchange(): return lax.all_to_all(array, axis, split_axis=0, concat_axis=0, tiled=True)  13.9 us
    ppermute x6, starting transfers between devices, along_z(): lax.ppermute(array, 'dp', [(i, (i + 2 * step) % (2 * ZS)) for i in range(...  11.7 us
    ppermute x6, waiting for transfers between devices, along_z(): lax.ppermute(array, 'dp', [(i, (i + 2 * step) % (2 * ZS)) for i in range(...  10.3 us
    ppermute x2, starting transfers between devices, swap_cores(): return lax.ppermute(array, 'dp', [(i, i ^ 1) for i in range(2 * ZS)])  6.7 us
    pallas_call x1, Pallas kernels, serve(): pl.pallas_call(serve_kernel, out_shape=jax.ShapeDtypeStruct((MEMS * CAP,...  6.07 us
  transfers between devices with their start and end apart: 9, of which 7 were waited for; matrix products, arithmetic and copies ran while one was open for 1% of the time, Pallas kernels for 16%

profile of v3, /device:TPU:1, one launch (start us, length us, event | category | flops | bytes accessed | tf_op | source)
XLA Modules:
  0.0 152.0 jit_solution(6907033074295100237)
XLA Ops:
  0.6 1.7 %request.1 = (s32[16,128]{1,0:T(8,128)}, s32[1,192]{1,0:T(1,128)}) custom-call(s32[8,24]{1,0:T(8,128)} %bitcast.46, s32[1,24]{1,0:T(1,128)} %bitcast.47), custom_call_target="tpu_custom_call" | custom-call | tf_op jit(solution)/shard_map/request/pallas_call | solution.py:77
  2.4 13.9 %all_to_all.16 = s32[16,1,128]{2,1,0:T(1,128)S(1)} all-to-all(s32[16,1,128]{2,1,0:T(1,128)} %bitcast.45), channel_id=1, replica_groups=mesh['dp'=8,'mem'=16] {'mem'}, dimensions={0} | all-to-all | bytes 16384 | tf_op jit(solution)/shard_map/all_to_all | solution.py:406
  16.3 6.1 %serve.1 = bf16[192,2,64,128]{3,2,1,0:T(8,128)(2,1)} custom-call(s32[16,128]{1,0:T(8,128)S(1)} %bitcast.40, bf16[1536,2048]{1,0:T(8,128)(2,1)} %bitcast.43, bf16[1536,2048]{1,0:T(8,128)(2,1)} %bitcast.44), custom_call_target="tpu_custom_call" | custom-call | bytes 12582912 | tf_op jit(solution)/shard_map/serve/pallas_call | solution.py:108
  22.4 0.0 copy-start
  22.4 0.0 copy-start.1
  22.4 0.0 copy-start.2
  22.4 0.0 copy-start.3
  22.4 4.8 %all-to-all-start.1 = ((bf16[192,2,64,128]{3,2,1,0:T(8,128)(2,1)}), bf16[192,2,64,128]{3,2,1,0:T(8,128)(2,1)}, u32[]{:S(2)}, u32[]{:S(2)}) async-start(bf16[192,2,64,128]{3,2,1,0:T(8,128)(2,1)} %serve.1), calls=%async_computation.1 | async-start | bytes 12582912 | tf_op jit(solution)/shard_map/all_to_all | solution.py:406
  27.9 0.0 copy-done
  27.9 0.0 copy-done.1
  27.9 0.0 copy-done.2
  27.9 0.0 copy-done.3
  27.9 23.8 %local.1 = (bf16[3072,128]{1,0:T(8,128)(2,1)S(1)}, f32[3072,128]{1,0:T(8,128)}, f32[3072,128]{1,0:T(8,128)}, f32[4,256,256]{2,1,0:T(8,128)S(1)}, bf16[4,256,256]{2,1,0:T(8,128)(2,1)S(1)}) custom-call(bf16[3072,2048]{1,0:T(8,128)(2,1)} %bitcast.49, bf16[2048,128]{1,0:T(8,128)(2,1)S(1)} %copy-done.1, bf16[2048,128]{1,0:T(8,128)(2,1)S(1)} %copy-done.2, ...), custom_call_target="tpu_custom_call" | custom-call | flops 14000000000 | bytes 20971520 | tf_op jit(solution)/shard_map/local/pallas_call | solution.py:183
  51.7 0.0 copy-start.4
  51.7 2.2 %collective-permute-start = (bf16[4,256,256]{2,1,0:T(8,128)(2,1)S(1)}, bf16[4,256,256]{2,1,0:T(8,128)(2,1)S(1)}, u32[]{:S(2)}, u32[]{:S(2)}) collective-permute-start(bf16[4,256,256]{2,1,0:T(8,128)(2,1)S(1)} %get-tuple-element.23), channel_id=1, source_target_pairs={{0,16},{16,0},{32,48},{48,32},{64,80},{80,64},{96,112},{112,96},{1... | collective-permute-start | bytes 1572872 | tf_op jit(solution)/shard_map/ppermute | solution.py:389
  53.9 1.5 %collective-permute-done = bf16[4,256,256]{2,1,0:T(8,128)(2,1)S(1)} collective-permute-done((bf16[4,256,256]{2,1,0:T(8,128)(2,1)S(1)}, bf16[4,256,256]{2,1,0:T(8,128)(2,1)S(1)}, u32[]{:S(2)}, u32[]{:S(2)}) %collective-permute-start) | collective-permute-done | bytes 524320 | tf_op jit(solution)/shard_map/ppermute | solution.py:389
  55.5 0.1 fusion.2
  55.6 1.6 %collective-permute-start.1 = (bf16[256,256]{1,0:T(8,128)(2,1)S(1)}, bf16[256,256]{1,0:T(8,128)(2,1)S(1)}, u32[]{:S(2)}, u32[]{:S(2)}) collective-permute-start(bf16[256,256]{1,0:T(8,128)(2,1)S(1)} %get-tuple-element.35), channel_id=1, source_target_pairs={{0,32},{16,48},{32,64},{48,80},{64,96},{80,112},{96,0},{112,16},{1... | collective-permute-start | bytes 393224 | tf_op jit(solution)/shard_map/ppermute | solution.py:393
  57.2 2.5 %collective-permute-start.3 = (bf16[256,256]{1,0:T(8,128)(2,1)S(1)}, bf16[256,256]{1,0:T(8,128)(2,1)S(1)}, u32[]{:S(2)}, u32[]{:S(2)}) collective-permute-start(bf16[256,256]{1,0:T(8,128)(2,1)S(1)} %get-tuple-element.36), channel_id=1, source_target_pairs={{0,96},{16,112},{32,0},{48,16},{64,32},{80,48},{96,64},{112,80},{1... | collective-permute-start | bytes 393224 | tf_op jit(solution)/shard_map/ppermute | solution.py:393
  59.6 1.1 collective-permute-start.2
  60.7 2.5 %collective-permute-done.1 = bf16[256,256]{1,0:T(8,128)(2,1)S(1)} collective-permute-done((bf16[256,256]{1,0:T(8,128)(2,1)S(1)}, bf16[256,256]{1,0:T(8,128)(2,1)S(1)}, u32[]{:S(2)}, u32[]{:S(2)}) %collective-permute-start.1) | collective-permute-done | bytes 131104 | tf_op jit(solution)/shard_map/ppermute | solution.py:393
  63.2 0.0 collective-permute-done.3
  63.2 3.7 %collective-permute-done.2 = bf16[256,256]{1,0:T(8,128)(2,1)S(1)} collective-permute-done((bf16[256,256]{1,0:T(8,128)(2,1)S(1)}, bf16[256,256]{1,0:T(8,128)(2,1)S(1)}, u32[]{:S(2)}, u32[]{:S(2)}) %collective-permute-start.2) | collective-permute-done | bytes 131104 | tf_op jit(solution)/shard_map/ppermute | solution.py:393
  66.9 0.1 fusion.1
  67.0 0.0 copy-done.4
  67.0 0.7 fusion.9
  67.7 49.5 %all-to-all-done.1.tiles_ref = bf16[192,2,64,128]{3,2,1,0:T(8,128)(2,1)} async-done(((bf16[192,2,64,128]{3,2,1,0:T(8,128)(2,1)}), bf16[192,2,64,128]{3,2,1,0:T(8,128)(2,1)}, u32[]{:S(2)}, u32[]{:S(2)}) %all-to-all-start.1) | async-done | bytes 6291488 | tf_op jit(solution)/shard_map/all_to_all | solution.py:406
  117.2 13.9 %memory.1 = (bf16[3072,128]{1,0:T(8,128)(2,1)}, f32[4,272,128]{2,1,0:T(8,128)}, bf16[4,272,128]{2,1,0:T(8,128)(2,1)}) custom-call(s32[1,24]{1,0:T(1,128)} %bitcast.48, s32[1,192]{1,0:T(1,128)} %get-tuple-element.25.slot_ref, f32[1]{0:T(128)S(6)} %copy.16.bias_ref, bf16[192,2,64,128]{3,2,1,0:T(8,128)(2,1)} %all-to-all-done.1.tiles_ref, ...), custom_call_target="tpu_custom_call" | custom-call | flops 8000000000 | bytes 25165824 | tf_op jit(solution)/shard_map/memory/pallas_call | solution.py:351
  131.1 4.5 %collective-permute-start.4 = (bf16[4,272,128]{2,1,0:T(8,128)(2,1)}, bf16[4,272,128]{2,1,0:T(8,128)(2,1)S(1)}, u32[]{:S(2)}, u32[]{:S(2)}) collective-permute-start(bf16[4,272,128]{2,1,0:T(8,128)(2,1)} %get-tuple-element.32), channel_id=1, source_target_pairs={{0,16},{16,0},{32,48},{48,32},{64,80},{80,64},{96,112},{112,96},{1... | collective-permute-start | bytes 835592 | tf_op jit(solution)/shard_map/ppermute | solution.py:389
  135.6 1.4 collective-permute-done.4
  137.0 1.2 convert_add_fusion
  138.2 4.6 %collective-permute-start.7 = (bf16[272,128]{1,0:T(8,128)(2,1)S(1)}, bf16[272,128]{1,0:T(8,128)(2,1)S(1)}, u32[]{:S(2)}, u32[]{:S(2)}) collective-permute-start(bf16[272,128]{1,0:T(8,128)(2,1)S(1)} %get-tuple-element.39), channel_id=1, source_target_pairs={{0,96},{16,112},{32,0},{48,16},{64,32},{80,48},{96,64},{112,80},{1... | collective-permute-start | bytes 208904 | tf_op jit(solution)/shard_map/ppermute | solution.py:393
  142.8 1.1 collective-permute-start.6
  143.9 0.8 collective-permute-start.5
  144.8 0.0 collective-permute-done.7
  144.8 2.7 %collective-permute-done.6 = bf16[272,128]{1,0:T(8,128)(2,1)S(1)} collective-permute-done((bf16[272,128]{1,0:T(8,128)(2,1)S(1)}, bf16[272,128]{1,0:T(8,128)(2,1)S(1)}, u32[]{:S(2)}, u32[]{:S(2)}) %collective-permute-start.6) | collective-permute-done | bytes 69664 | tf_op jit(solution)/shard_map/ppermute | solution.py:393
  147.5 1.5 collective-permute-done.5
  149.0 0.6 fusion.8
  149.6 0.7 slice_add_fusion
  (3 shorter events, 0.0 us)
Async XLA Ops:
  22.4 5.5 %copy-start = (bf16[1,3072,128]{2,1,0:T(8,128)(2,1)S(1)}, bf16[1,3072,128]{2,1,0:T(8,128)(2,1)}, u32[]{:S(2)}) copy-start(bf16[1,3072,128]{2,1,0:T(8,128)(2,1)} %param.19) | copy-start | bytes 2359300
  22.4 5.5 %copy-start.1 = (bf16[2048,128]{1,0:T(8,128)(2,1)S(1)}, bf16[2048,128]{1,0:T(8,128)(2,1)}, u32[]{:S(2)}) copy-start(bf16[2048,128]{1,0:T(8,128)(2,1)} %wq_ref.1) | copy-start | bytes 1572868
  22.4 5.5 %copy-start.2 = (bf16[2048,128]{1,0:T(8,128)(2,1)S(1)}, bf16[2048,128]{1,0:T(8,128)(2,1)}, u32[]{:S(2)}) copy-start(bf16[2048,128]{1,0:T(8,128)(2,1)} %wk_ref.1) | copy-start | bytes 1572868
  22.4 5.5 %copy-start.3 = (bf16[2048,128]{1,0:T(8,128)(2,1)S(1)}, bf16[2048,128]{1,0:T(8,128)(2,1)}, u32[]{:S(2)}) copy-start(bf16[2048,128]{1,0:T(8,128)(2,1)} %wv_ref.1) | copy-start | bytes 1572868
  22.4 94.8 %all-to-all-start.1 = ((bf16[192,2,64,128]{3,2,1,0:T(8,128)(2,1)}), bf16[192,2,64,128]{3,2,1,0:T(8,128)(2,1)}, u32[]{:S(2)}, u32[]{:S(2)}) async-start(bf16[192,2,64,128]{3,2,1,0:T(8,128)(2,1)} %serve.1), calls=%async_computation.1 | async-start | bytes 12582912 | tf_op jit(solution)/shard_map/all_to_all | solution.py:406
  51.7 15.3 %copy-start.4 = (bf16[3072,128]{1,0:T(8,128)(2,1)}, bf16[3072,128]{1,0:T(8,128)(2,1)S(1)}, u32[]{:S(2)}) copy-start(bf16[3072,128]{1,0:T(8,128)(2,1)S(1)} %get-tuple-element.27.queries_in) | copy-start | bytes 2359300
  51.7 3.8 %collective-permute-start = (bf16[4,256,256]{2,1,0:T(8,128)(2,1)S(1)}, bf16[4,256,256]{2,1,0:T(8,128)(2,1)S(1)}, u32[]{:S(2)}, u32[]{:S(2)}) collective-permute-start(bf16[4,256,256]{2,1,0:T(8,128)(2,1)S(1)} %get-tuple-element.23), channel_id=1, source_target_pairs={{0,16},{16,0},{32,48},{48,32},{64,80},{80,64},{96,112},{112,96},{1... | collective-permute-start | bytes 1572872 | tf_op jit(solution)/shard_map/ppermute | solution.py:389
  55.6 7.7 %collective-permute-start.1 = (bf16[256,256]{1,0:T(8,128)(2,1)S(1)}, bf16[256,256]{1,0:T(8,128)(2,1)S(1)}, u32[]{:S(2)}, u32[]{:S(2)}) collective-permute-start(bf16[256,256]{1,0:T(8,128)(2,1)S(1)} %get-tuple-element.35), channel_id=1, source_target_pairs={{0,32},{16,48},{32,64},{48,80},{64,96},{80,112},{96,0},{112,16},{1... | collective-permute-start | bytes 393224 | tf_op jit(solution)/shard_map/ppermute | solution.py:393
  57.2 6.1 %collective-permute-start.3 = (bf16[256,256]{1,0:T(8,128)(2,1)S(1)}, bf16[256,256]{1,0:T(8,128)(2,1)S(1)}, u32[]{:S(2)}, u32[]{:S(2)}) collective-permute-start(bf16[256,256]{1,0:T(8,128)(2,1)S(1)} %get-tuple-element.36), channel_id=1, source_target_pairs={{0,96},{16,112},{32,0},{48,16},{64,32},{80,48},{96,64},{112,80},{1... | collective-permute-start | bytes 393224 | tf_op jit(solution)/shard_map/ppermute | solution.py:393
  59.6 7.3 %collective-permute-start.2 = (bf16[256,256]{1,0:T(8,128)(2,1)S(1)}, bf16[256,256]{1,0:T(8,128)(2,1)S(1)}, u32[]{:S(2)}, u32[]{:S(2)}) collective-permute-start(bf16[256,256]{1,0:T(8,128)(2,1)S(1)} %get-tuple-element.37), channel_id=1, source_target_pairs={{0,64},{16,80},{32,96},{48,112},{64,0},{80,16},{96,32},{112,48},{1... | collective-permute-start | bytes 393224 | tf_op jit(solution)/shard_map/ppermute | solution.py:393
  131.1 5.9 %collective-permute-start.4 = (bf16[4,272,128]{2,1,0:T(8,128)(2,1)}, bf16[4,272,128]{2,1,0:T(8,128)(2,1)S(1)}, u32[]{:S(2)}, u32[]{:S(2)}) collective-permute-start(bf16[4,272,128]{2,1,0:T(8,128)(2,1)} %get-tuple-element.32), channel_id=1, source_target_pairs={{0,16},{16,0},{32,48},{48,32},{64,80},{80,64},{96,112},{112,96},{1... | collective-permute-start | bytes 835592 | tf_op jit(solution)/shard_map/ppermute | solution.py:389
  138.2 6.6 %collective-permute-start.7 = (bf16[272,128]{1,0:T(8,128)(2,1)S(1)}, bf16[272,128]{1,0:T(8,128)(2,1)S(1)}, u32[]{:S(2)}, u32[]{:S(2)}) collective-permute-start(bf16[272,128]{1,0:T(8,128)(2,1)S(1)} %get-tuple-element.39), channel_id=1, source_target_pairs={{0,96},{16,112},{32,0},{48,16},{64,32},{80,48},{96,64},{112,80},{1... | collective-permute-start | bytes 208904 | tf_op jit(solution)/shard_map/ppermute | solution.py:393
  142.8 4.7 %collective-permute-start.6 = (bf16[272,128]{1,0:T(8,128)(2,1)S(1)}, bf16[272,128]{1,0:T(8,128)(2,1)S(1)}, u32[]{:S(2)}, u32[]{:S(2)}) collective-permute-start(bf16[272,128]{1,0:T(8,128)(2,1)S(1)} %get-tuple-element.40), channel_id=1, source_target_pairs={{0,64},{16,80},{32,96},{48,112},{64,0},{80,16},{96,32},{112,48},{1... | collective-permute-start | bytes 208904 | tf_op jit(solution)/shard_map/ppermute | solution.py:393
  143.9 5.0 %collective-permute-start.5 = (bf16[272,128]{1,0:T(8,128)(2,1)S(1)}, bf16[272,128]{1,0:T(8,128)(2,1)S(1)}, u32[]{:S(2)}, u32[]{:S(2)}) collective-permute-start(bf16[272,128]{1,0:T(8,128)(2,1)S(1)} %get-tuple-element.41), channel_id=1, source_target_pairs={{0,32},{16,48},{32,64},{48,80},{64,96},{80,112},{96,0},{112,16},{1... | collective-permute-start | bytes 208904 | tf_op jit(solution)/shard_map/ppermute | solution.py:393

commit v4 on v3

--- a/solution.py
+++ b/solution.py
@@ -85,21 +85,25 @@
 
 
 def serve_kernel(wanted_ref, keys_ref, values_ref, out_ref, held, load_sems, store_sem):
-    def issue(i, _):
-        dest = i // CAP
-        rank = i % CAP
-        rows = pl.ds(pl.multiple_of(wanted_ref[dest, rank] * TILE, TILE), TILE)
-        cols = pl.ds(pl.multiple_of(dest * DH, DH), DH)
-        sem = load_sems.at[dest]
-        pltpu.make_async_copy(keys_ref.at[rows, cols], held.at[i, 0], sem).start()
-        pltpu.make_async_copy(values_ref.at[rows, cols], held.at[i, 1], sem).start()
-        return 0
-
-    lax.fori_loop(0, MEMS * CAP, issue, 0, unroll=4)
-    for dest in range(MEMS):
+    def store(dest):
         mine = pl.ds(dest * CAP, CAP)
         pltpu.make_async_copy(out_ref.at[mine], held.at[mine], load_sems.at[dest]).wait()
         pltpu.make_async_copy(held.at[mine], out_ref.at[mine], store_sem).start()
+
+    def issue(dest, _):
+        cols = pl.ds(pl.multiple_of(dest * DH, DH), DH)
+        sem = load_sems.at[dest]
+        for rank in range(CAP):
+            rows = pl.ds(pl.multiple_of(wanted_ref[dest, rank] * TILE, TILE), TILE)
+            slot = held.at[dest * CAP + rank]
+            pltpu.make_async_copy(keys_ref.at[rows, cols], slot.at[0], sem).start()
+            pltpu.make_async_copy(values_ref.at[rows, cols], slot.at[1], sem).start()
+
+        return 0
+
+    lax.fori_loop(0, MEMS, issue, 0)
+    for dest in range(MEMS):
+        store(dest)
     pltpu.make_async_copy(held, out_ref, store_sem).wait()
 
 
@@ -203,7 +207,7 @@
     )(tokens, w_query, w_key, w_value, cot, bias)
 
 
-CLASSES = ((2, 6), (4, 3), (8, 3))
+CLASSES = ((2, 6), (4, 3), (8, 6))
 
 
 def attend_all(members, tiles_n, refs):

time: 152 us -> 152 us (level)
  starting transfers between devices: 23.2 us -> 21.4 us
    ppermute x2, starting transfers between devices: 6.7 us -> 4.75 us  [swap_cores(): return lax.ppermute(array, 'dp', [(i, i ^ 1) for i in range(2 * ZS)])]
  transfers between devices with their start and end apart: 9 -> 9, of which waited for: 7 -> 8; matrix products, arithmetic and copies ran while one was open for 1% -> 1% of each run, Pallas kernels for 16% -> 16%
where the time goes in v4:
time: 152 us; the launch traced here: 151 us
  waiting for transfers between devices  63.5 us (42%)
  Pallas kernels  45.3 us (30%)
  starting transfers between devices  21.4 us (14%)
  blocking collectives  13.9 us (9%)
  between operations  3.27 us (2%)
  other arithmetic  2.66 us (2%)
    all_to_all x1, waiting for transfers between devices, exchange(): return lax.all_to_all(array, axis, split_axis=0, concat_axis=0, tiled=True)  49.6 us
    pallas_call x1, Pallas kernels, local_part(): pl.pallas_call(local_kernel, grid=(SEGS,), out_shape=(jax.ShapeDtypeStruc...  23.8 us
    pallas_call x1, Pallas kernels, memory_part(): pl.pallas_call(memory_kernel, out_shape=(jax.ShapeDtypeStruct((TOK, DH),...  14.2 us
    all_to_all x1, blocking collectives, exchange(): return lax.all_to_all(array, axis, split_axis=0, concat_axis=0, tiled=True)  13.9 us
    ppermute x6, starting transfers between devices, along_z(): lax.ppermute(array, 'dp', [(i, (i + 2 * step) % (2 * ZS)) for i in range(...  11.9 us
    ppermute x6, waiting for transfers between devices, along_z(): lax.ppermute(array, 'dp', [(i, (i + 2 * step) % (2 * ZS)) for i in range(...  10.9 us
    pallas_call x1, Pallas kernels, serve(): pl.pallas_call(serve_kernel, out_shape=jax.ShapeDtypeStruct((MEMS * CAP,...  5.56 us
    all_to_all x1, starting transfers between devices, exchange(): return lax.all_to_all(array, axis, split_axis=0, concat_axis=0, tiled=True)  4.78 us
  transfers between devices with their start and end apart: 9, of which 8 were waited for; matrix products, arithmetic and copies ran while one was open for 1% of the time, Pallas kernels for 16%

profile of v4, /device:TPU:1, one launch (start us, length us, event | category | flops | bytes accessed | tf_op | source)
XLA Modules:
  0.0 150.8 jit_solution(11008343769561400102)
XLA Ops:
  0.6 1.7 %request.1 = (s32[16,128]{1,0:T(8,128)}, s32[1,192]{1,0:T(1,128)}) custom-call(s32[8,24]{1,0:T(8,128)} %bitcast.46, s32[1,24]{1,0:T(1,128)} %bitcast.47), custom_call_target="tpu_custom_call" | custom-call | tf_op jit(solution)/shard_map/request/pallas_call | solution.py:77
  2.4 13.9 %all_to_all.16 = s32[16,1,128]{2,1,0:T(1,128)S(1)} all-to-all(s32[16,1,128]{2,1,0:T(1,128)} %bitcast.45), channel_id=1, replica_groups=mesh['dp'=8,'mem'=16] {'mem'}, dimensions={0} | all-to-all | bytes 16384 | tf_op jit(solution)/shard_map/all_to_all | solution.py:410
  16.3 5.6 %serve.1 = bf16[192,2,64,128]{3,2,1,0:T(8,128)(2,1)} custom-call(s32[16,128]{1,0:T(8,128)S(1)} %bitcast.40, bf16[1536,2048]{1,0:T(8,128)(2,1)} %bitcast.43, bf16[1536,2048]{1,0:T(8,128)(2,1)} %bitcast.44), custom_call_target="tpu_custom_call" | custom-call | bytes 12582912 | tf_op jit(solution)/shard_map/serve/pallas_call | solution.py:112
  21.9 0.0 copy-start
  21.9 0.0 copy-start.1
  21.9 0.0 copy-start.2
  21.9 0.0 copy-start.3
  21.9 4.8 %all-to-all-start.1 = ((bf16[192,2,64,128]{3,2,1,0:T(8,128)(2,1)}), bf16[192,2,64,128]{3,2,1,0:T(8,128)(2,1)}, u32[]{:S(2)}, u32[]{:S(2)}) async-start(bf16[192,2,64,128]{3,2,1,0:T(8,128)(2,1)} %serve.1), calls=%async_computation.1 | async-start | bytes 12582912 | tf_op jit(solution)/shard_map/all_to_all | solution.py:410
  27.3 0.0 copy-done
  27.4 0.0 copy-done.1
  27.4 0.0 copy-done.2
  27.4 0.0 copy-done.3
  27.4 23.8 %local.1 = (bf16[3072,128]{1,0:T(8,128)(2,1)S(1)}, f32[3072,128]{1,0:T(8,128)}, f32[3072,128]{1,0:T(8,128)}, f32[4,256,256]{2,1,0:T(8,128)S(1)}, bf16[4,256,256]{2,1,0:T(8,128)(2,1)S(1)}) custom-call(bf16[3072,2048]{1,0:T(8,128)(2,1)} %bitcast.49, bf16[2048,128]{1,0:T(8,128)(2,1)S(1)} %copy-done.1, bf16[2048,128]{1,0:T(8,128)(2,1)S(1)} %copy-done.2, ...), custom_call_target="tpu_custom_call" | custom-call | flops 14000000000 | bytes 20971520 | tf_op jit(solution)/shard_map/local/pallas_call | solution.py:187
  51.2 0.0 copy-start.4
  51.2 2.3 %collective-permute-start = (bf16[4,256,256]{2,1,0:T(8,128)(2,1)S(1)}, bf16[4,256,256]{2,1,0:T(8,128)(2,1)S(1)}, u32[]{:S(2)}, u32[]{:S(2)}) collective-permute-start(bf16[4,256,256]{2,1,0:T(8,128)(2,1)S(1)} %get-tuple-element.23), channel_id=1, source_target_pairs={{0,16},{16,0},{32,48},{48,32},{64,80},{80,64},{96,112},{112,96},{1... | collective-permute-start | bytes 1572872 | tf_op jit(solution)/shard_map/ppermute | solution.py:393
  53.5 1.5 %collective-permute-done = bf16[4,256,256]{2,1,0:T(8,128)(2,1)S(1)} collective-permute-done((bf16[4,256,256]{2,1,0:T(8,128)(2,1)S(1)}, bf16[4,256,256]{2,1,0:T(8,128)(2,1)S(1)}, u32[]{:S(2)}, u32[]{:S(2)}) %collective-permute-start) | collective-permute-done | bytes 524320 | tf_op jit(solution)/shard_map/ppermute | solution.py:393
  55.0 0.1 fusion.2
  55.1 1.9 %collective-permute-start.1 = (bf16[256,256]{1,0:T(8,128)(2,1)S(1)}, bf16[256,256]{1,0:T(8,128)(2,1)S(1)}, u32[]{:S(2)}, u32[]{:S(2)}) collective-permute-start(bf16[256,256]{1,0:T(8,128)(2,1)S(1)} %get-tuple-element.35), channel_id=1, source_target_pairs={{0,32},{16,48},{32,64},{48,80},{64,96},{80,112},{96,0},{112,16},{1... | collective-permute-start | bytes 393224 | tf_op jit(solution)/shard_map/ppermute | solution.py:397
  57.0 1.8 %collective-permute-start.3 = (bf16[256,256]{1,0:T(8,128)(2,1)S(1)}, bf16[256,256]{1,0:T(8,128)(2,1)S(1)}, u32[]{:S(2)}, u32[]{:S(2)}) collective-permute-start(bf16[256,256]{1,0:T(8,128)(2,1)S(1)} %get-tuple-element.36), channel_id=1, source_target_pairs={{0,96},{16,112},{32,0},{48,16},{64,32},{80,48},{96,64},{112,80},{1... | collective-permute-start | bytes 393224 | tf_op jit(solution)/shard_map/ppermute | solution.py:397
  58.8 2.0 %collective-permute-start.2 = (bf16[256,256]{1,0:T(8,128)(2,1)S(1)}, bf16[256,256]{1,0:T(8,128)(2,1)S(1)}, u32[]{:S(2)}, u32[]{:S(2)}) collective-permute-start(bf16[256,256]{1,0:T(8,128)(2,1)S(1)} %get-tuple-element.37), channel_id=1, source_target_pairs={{0,64},{16,80},{32,96},{48,112},{64,0},{80,16},{96,32},{112,48},{1... | collective-permute-start | bytes 393224 | tf_op jit(solution)/shard_map/ppermute | solution.py:397
  60.9 1.6 %collective-permute-done.1 = bf16[256,256]{1,0:T(8,128)(2,1)S(1)} collective-permute-done((bf16[256,256]{1,0:T(8,128)(2,1)S(1)}, bf16[256,256]{1,0:T(8,128)(2,1)S(1)}, u32[]{:S(2)}, u32[]{:S(2)}) %collective-permute-start.1) | collective-permute-done | bytes 131104 | tf_op jit(solution)/shard_map/ppermute | solution.py:397
  62.4 0.0 collective-permute-done.3
  62.4 3.7 %collective-permute-done.2 = bf16[256,256]{1,0:T(8,128)(2,1)S(1)} collective-permute-done((bf16[256,256]{1,0:T(8,128)(2,1)S(1)}, bf16[256,256]{1,0:T(8,128)(2,1)S(1)}, u32[]{:S(2)}, u32[]{:S(2)}) %collective-permute-start.2) | collective-permute-done | bytes 131104 | tf_op jit(solution)/shard_map/ppermute | solution.py:397
  66.1 0.1 fusion.1
  66.2 0.0 copy-done.4
  66.2 0.7 fusion.9
  66.9 49.6 %all-to-all-done.1.tiles_ref = bf16[192,2,64,128]{3,2,1,0:T(8,128)(2,1)} async-done(((bf16[192,2,64,128]{3,2,1,0:T(8,128)(2,1)}), bf16[192,2,64,128]{3,2,1,0:T(8,128)(2,1)}, u32[]{:S(2)}, u32[]{:S(2)}) %all-to-all-start.1) | async-done | bytes 6291488 | tf_op jit(solution)/shard_map/all_to_all | solution.py:410
  116.5 14.2 %memory.1 = (bf16[3072,128]{1,0:T(8,128)(2,1)}, f32[4,272,128]{2,1,0:T(8,128)}, bf16[4,272,128]{2,1,0:T(8,128)(2,1)}) custom-call(s32[1,24]{1,0:T(1,128)} %bitcast.48, s32[1,192]{1,0:T(1,128)} %get-tuple-element.25.slot_ref, f32[1]{0:T(128)S(6)} %copy.16.bias_ref, bf16[192,2,64,128]{3,2,1,0:T(8,128)(2,1)} %all-to-all-done.1.tiles_ref, ...), custom_call_target="tpu_custom_call" | custom-call | flops 8000000000 | bytes 25165824 | tf_op jit(solution)/shard_map/memory/pallas_call | solution.py:355
  130.7 2.5 %collective-permute-start.4 = (bf16[4,272,128]{2,1,0:T(8,128)(2,1)}, bf16[4,272,128]{2,1,0:T(8,128)(2,1)S(1)}, u32[]{:S(2)}, u32[]{:S(2)}) collective-permute-start(bf16[4,272,128]{2,1,0:T(8,128)(2,1)} %get-tuple-element.32), channel_id=1, source_target_pairs={{0,16},{16,0},{32,48},{48,32},{64,80},{80,64},{96,112},{112,96},{1... | collective-permute-start | bytes 835592 | tf_op jit(solution)/shard_map/ppermute | solution.py:393
  133.2 1.4 collective-permute-done.4
  134.6 1.2 convert_add_fusion
  135.8 5.4 %collective-permute-start.7 = (bf16[272,128]{1,0:T(8,128)(2,1)S(1)}, bf16[272,128]{1,0:T(8,128)(2,1)S(1)}, u32[]{:S(2)}, u32[]{:S(2)}) collective-permute-start(bf16[272,128]{1,0:T(8,128)(2,1)S(1)} %get-tuple-element.39), channel_id=1, source_target_pairs={{0,96},{16,112},{32,0},{48,16},{64,32},{80,48},{96,64},{112,80},{1... | collective-permute-start | bytes 208904 | tf_op jit(solution)/shard_map/ppermute | solution.py:397
  141.2 0.0 collective-permute-start.6
  141.2 0.7 collective-permute-start.5
  142.0 1.3 collective-permute-done.7
  143.3 2.6 %collective-permute-done.6 = bf16[272,128]{1,0:T(8,128)(2,1)S(1)} collective-permute-done((bf16[272,128]{1,0:T(8,128)(2,1)S(1)}, bf16[272,128]{1,0:T(8,128)(2,1)S(1)}, u32[]{:S(2)}, u32[]{:S(2)}) %collective-permute-start.6) | collective-permute-done | bytes 69664 | tf_op jit(solution)/shard_map/ppermute | solution.py:397
  146.0 1.7 %collective-permute-done.5 = bf16[272,128]{1,0:T(8,128)(2,1)S(1)} collective-permute-done((bf16[272,128]{1,0:T(8,128)(2,1)S(1)}, bf16[272,128]{1,0:T(8,128)(2,1)S(1)}, u32[]{:S(2)}, u32[]{:S(2)}) %collective-permute-start.5) | collective-permute-done | bytes 69664 | tf_op jit(solution)/shard_map/ppermute | solution.py:397
  147.7 0.6 fusion.8
  148.3 0.7 slice_add_fusion
  (3 shorter events, 0.0 us)
Async XLA Ops:
  21.9 5.5 %copy-start = (bf16[1,3072,128]{2,1,0:T(8,128)(2,1)S(1)}, bf16[1,3072,128]{2,1,0:T(8,128)(2,1)}, u32[]{:S(2)}) copy-start(bf16[1,3072,128]{2,1,0:T(8,128)(2,1)} %param.19) | copy-start | bytes 2359300
  21.9 5.5 %copy-start.1 = (bf16[2048,128]{1,0:T(8,128)(2,1)S(1)}, bf16[2048,128]{1,0:T(8,128)(2,1)}, u32[]{:S(2)}) copy-start(bf16[2048,128]{1,0:T(8,128)(2,1)} %wq_ref.1) | copy-start | bytes 1572868
  21.9 5.5 %copy-start.2 = (bf16[2048,128]{1,0:T(8,128)(2,1)S(1)}, bf16[2048,128]{1,0:T(8,128)(2,1)}, u32[]{:S(2)}) copy-start(bf16[2048,128]{1,0:T(8,128)(2,1)} %wk_ref.1) | copy-start | bytes 1572868
  21.9 5.5 %copy-start.3 = (bf16[2048,128]{1,0:T(8,128)(2,1)S(1)}, bf16[2048,128]{1,0:T(8,128)(2,1)}, u32[]{:S(2)}) copy-start(bf16[2048,128]{1,0:T(8,128)(2,1)} %wv_ref.1) | copy-start | bytes 1572868
  21.9 94.6 %all-to-all-start.1 = ((bf16[192,2,64,128]{3,2,1,0:T(8,128)(2,1)}), bf16[192,2,64,128]{3,2,1,0:T(8,128)(2,1)}, u32[]{:S(2)}, u32[]{:S(2)}) async-start(bf16[192,2,64,128]{3,2,1,0:T(8,128)(2,1)} %serve.1), calls=%async_computation.1 | async-start | bytes 12582912 | tf_op jit(solution)/shard_map/all_to_all | solution.py:410
  51.2 15.0 %copy-start.4 = (bf16[3072,128]{1,0:T(8,128)(2,1)}, bf16[3072,128]{1,0:T(8,128)(2,1)S(1)}, u32[]{:S(2)}) copy-start(bf16[3072,128]{1,0:T(8,128)(2,1)S(1)} %get-tuple-element.27.queries_in) | copy-start | bytes 2359300
  51.2 3.8 %collective-permute-start = (bf16[4,256,256]{2,1,0:T(8,128)(2,1)S(1)}, bf16[4,256,256]{2,1,0:T(8,128)(2,1)S(1)}, u32[]{:S(2)}, u32[]{:S(2)}) collective-permute-start(bf16[4,256,256]{2,1,0:T(8,128)(2,1)S(1)} %get-tuple-element.23), channel_id=1, source_target_pairs={{0,16},{16,0},{32,48},{48,32},{64,80},{80,64},{96,112},{112,96},{1... | collective-permute-start | bytes 1572872 | tf_op jit(solution)/shard_map/ppermute | solution.py:393
  55.1 7.3 %collective-permute-start.1 = (bf16[256,256]{1,0:T(8,128)(2,1)S(1)}, bf16[256,256]{1,0:T(8,128)(2,1)S(1)}, u32[]{:S(2)}, u32[]{:S(2)}) collective-permute-start(bf16[256,256]{1,0:T(8,128)(2,1)S(1)} %get-tuple-element.35), channel_id=1, source_target_pairs={{0,32},{16,48},{32,64},{48,80},{64,96},{80,112},{96,0},{112,16},{1... | collective-permute-start | bytes 393224 | tf_op jit(solution)/shard_map/ppermute | solution.py:397
  57.0 5.4 %collective-permute-start.3 = (bf16[256,256]{1,0:T(8,128)(2,1)S(1)}, bf16[256,256]{1,0:T(8,128)(2,1)S(1)}, u32[]{:S(2)}, u32[]{:S(2)}) collective-permute-start(bf16[256,256]{1,0:T(8,128)(2,1)S(1)} %get-tuple-element.36), channel_id=1, source_target_pairs={{0,96},{16,112},{32,0},{48,16},{64,32},{80,48},{96,64},{112,80},{1... | collective-permute-start | bytes 393224 | tf_op jit(solution)/shard_map/ppermute | solution.py:397
  58.8 7.3 %collective-permute-start.2 = (bf16[256,256]{1,0:T(8,128)(2,1)S(1)}, bf16[256,256]{1,0:T(8,128)(2,1)S(1)}, u32[]{:S(2)}, u32[]{:S(2)}) collective-permute-start(bf16[256,256]{1,0:T(8,128)(2,1)S(1)} %get-tuple-element.37), channel_id=1, source_target_pairs={{0,64},{16,80},{32,96},{48,112},{64,0},{80,16},{96,32},{112,48},{1... | collective-permute-start | bytes 393224 | tf_op jit(solution)/shard_map/ppermute | solution.py:397
  130.7 3.9 %collective-permute-start.4 = (bf16[4,272,128]{2,1,0:T(8,128)(2,1)}, bf16[4,272,128]{2,1,0:T(8,128)(2,1)S(1)}, u32[]{:S(2)}, u32[]{:S(2)}) collective-permute-start(bf16[4,272,128]{2,1,0:T(8,128)(2,1)} %get-tuple-element.32), channel_id=1, source_target_pairs={{0,16},{16,0},{32,48},{48,32},{64,80},{80,64},{96,112},{112,96},{1... | collective-permute-start | bytes 835592 | tf_op jit(solution)/shard_map/ppermute | solution.py:393
  135.8 7.5 %collective-permute-start.7 = (bf16[272,128]{1,0:T(8,128)(2,1)S(1)}, bf16[272,128]{1,0:T(8,128)(2,1)S(1)}, u32[]{:S(2)}, u32[]{:S(2)}) collective-permute-start(bf16[272,128]{1,0:T(8,128)(2,1)S(1)} %get-tuple-element.39), channel_id=1, source_target_pairs={{0,96},{16,112},{32,0},{48,16},{64,32},{80,48},{96,64},{112,80},{1... | collective-permute-start | bytes 208904 | tf_op jit(solution)/shard_map/ppermute | solution.py:397
  141.2 4.8 %collective-permute-start.6 = (bf16[272,128]{1,0:T(8,128)(2,1)S(1)}, bf16[272,128]{1,0:T(8,128)(2,1)S(1)}, u32[]{:S(2)}, u32[]{:S(2)}) collective-permute-start(bf16[272,128]{1,0:T(8,128)(2,1)S(1)} %get-tuple-element.40), channel_id=1, source_target_pairs={{0,64},{16,80},{32,96},{48,112},{64,0},{80,16},{96,32},{112,48},{1... | collective-permute-start | bytes 208904 | tf_op jit(solution)/shard_map/ppermute | solution.py:397
  141.2 6.5 %collective-permute-start.5 = (bf16[272,128]{1,0:T(8,128)(2,1)S(1)}, bf16[272,128]{1,0:T(8,128)(2,1)S(1)}, u32[]{:S(2)}, u32[]{:S(2)}) collective-permute-start(bf16[272,128]{1,0:T(8,128)(2,1)S(1)} %get-tuple-element.41), channel_id=1, source_target_pairs={{0,32},{16,48},{32,64},{48,80},{64,96},{80,112},{96,0},{112,16},{1... | collective-permute-start | bytes 208904 | tf_op jit(solution)/shard_map/ppermute | solution.py:397

commit v5 on v4

--- a/solution.py
+++ b/solution.py
@@ -101,7 +101,7 @@
 
         return 0
 
-    lax.fori_loop(0, MEMS, issue, 0)
+    lax.fori_loop(0, MEMS, issue, 0, unroll=2)
     for dest in range(MEMS):
         store(dest)
     pltpu.make_async_copy(held, out_ref, store_sem).wait()

time: 152 us -> 151 us (level)
  Pallas kernels: 45.3 us -> 47 us
    ppermute x6, starting transfers between devices: 11.9 us -> 9.57 us  [along_z(): lax.ppermute(array, 'dp', [(i, (i + 2 * step) % (2 * ZS)) for i in range(...]
where the time goes in v5:
time: 151 us; the launch traced here: 150 us
  waiting for transfers between devices  62.6 us (41%)
  Pallas kernels  47 us (31%)
  starting transfers between devices  20.1 us (13%)
  blocking collectives  13.9 us (9%)
  between operations  3.27 us (2%)
  other arithmetic  2.66 us (2%)
    all_to_all x1, waiting for transfers between devices, exchange(): return lax.all_to_all(array, axis, split_axis=0, concat_axis=0, tiled=True)  49.3 us
    pallas_call x1, Pallas kernels, local_part(): pl.pallas_call(local_kernel, grid=(SEGS,), out_shape=(jax.ShapeDtypeStruc...  23.8 us
    pallas_call x1, Pallas kernels, memory_part(): pl.pallas_call(memory_kernel, out_shape=(jax.ShapeDtypeStruct((TOK, DH),...  15.5 us
    all_to_all x1, blocking collectives, exchange(): return lax.all_to_all(array, axis, split_axis=0, concat_axis=0, tiled=True)  13.9 us
    ppermute x6, waiting for transfers between devices, along_z(): lax.ppermute(array, 'dp', [(i, (i + 2 * step) % (2 * ZS)) for i in range(...  10.4 us
    ppermute x6, starting transfers between devices, along_z(): lax.ppermute(array, 'dp', [(i, (i + 2 * step) % (2 * ZS)) for i in range(...  9.57 us
    pallas_call x1, Pallas kernels, serve(): pl.pallas_call(serve_kernel, out_shape=jax.ShapeDtypeStruct((MEMS * CAP,...  5.86 us
    ppermute x2, starting transfers between devices, swap_cores(): return lax.ppermute(array, 'dp', [(i, i ^ 1) for i in range(2 * ZS)])  5.76 us
  transfers between devices with their start and end apart: 9, of which 8 were waited for; matrix products, arithmetic and copies ran while one was open for 1% of the time, Pallas kernels for 16%

profile of v5, /device:TPU:1, one launch (start us, length us, event | category | flops | bytes accessed | tf_op | source)
XLA Modules:
  0.0 150.3 jit_solution(4897129336317714974)
XLA Ops:
  0.6 1.7 %request.1 = (s32[16,128]{1,0:T(8,128)}, s32[1,192]{1,0:T(1,128)}) custom-call(s32[8,24]{1,0:T(8,128)} %bitcast.46, s32[1,24]{1,0:T(1,128)} %bitcast.47), custom_call_target="tpu_custom_call" | custom-call | tf_op jit(solution)/shard_map/request/pallas_call | solution.py:77
  2.4 13.9 %all_to_all.16 = s32[16,1,128]{2,1,0:T(1,128)S(1)} all-to-all(s32[16,1,128]{2,1,0:T(1,128)} %bitcast.45), channel_id=1, replica_groups=mesh['dp'=8,'mem'=16] {'mem'}, dimensions={0} | all-to-all | bytes 16384 | tf_op jit(solution)/shard_map/all_to_all | solution.py:410
  16.3 5.9 %serve.1 = bf16[192,2,64,128]{3,2,1,0:T(8,128)(2,1)} custom-call(s32[16,128]{1,0:T(8,128)S(1)} %bitcast.40, bf16[1536,2048]{1,0:T(8,128)(2,1)} %bitcast.43, bf16[1536,2048]{1,0:T(8,128)(2,1)} %bitcast.44), custom_call_target="tpu_custom_call" | custom-call | bytes 12582912 | tf_op jit(solution)/shard_map/serve/pallas_call | solution.py:112
  22.2 0.0 copy-start
  22.2 0.0 copy-start.1
  22.2 0.0 copy-start.2
  22.2 0.0 copy-start.3
  22.2 4.8 %all-to-all-start.1 = ((bf16[192,2,64,128]{3,2,1,0:T(8,128)(2,1)}), bf16[192,2,64,128]{3,2,1,0:T(8,128)(2,1)}, u32[]{:S(2)}, u32[]{:S(2)}) async-start(bf16[192,2,64,128]{3,2,1,0:T(8,128)(2,1)} %serve.1), calls=%async_computation.1 | async-start | bytes 12582912 | tf_op jit(solution)/shard_map/all_to_all | solution.py:410
  27.6 0.0 copy-done
  27.7 0.0 copy-done.1
  27.7 0.0 copy-done.2
  27.7 0.0 copy-done.3
  27.7 23.8 %local.1 = (bf16[3072,128]{1,0:T(8,128)(2,1)S(1)}, f32[3072,128]{1,0:T(8,128)}, f32[3072,128]{1,0:T(8,128)}, f32[4,256,256]{2,1,0:T(8,128)S(1)}, bf16[4,256,256]{2,1,0:T(8,128)(2,1)S(1)}) custom-call(bf16[3072,2048]{1,0:T(8,128)(2,1)} %bitcast.49, bf16[2048,128]{1,0:T(8,128)(2,1)S(1)} %copy-done.1, bf16[2048,128]{1,0:T(8,128)(2,1)S(1)} %copy-done.2, ...), custom_call_target="tpu_custom_call" | custom-call | flops 14000000000 | bytes 20971520 | tf_op jit(solution)/shard_map/local/pallas_call | solution.py:187
  51.5 0.0 copy-start.4
  51.5 2.3 %collective-permute-start = (bf16[4,256,256]{2,1,0:T(8,128)(2,1)S(1)}, bf16[4,256,256]{2,1,0:T(8,128)(2,1)S(1)}, u32[]{:S(2)}, u32[]{:S(2)}) collective-permute-start(bf16[4,256,256]{2,1,0:T(8,128)(2,1)S(1)} %get-tuple-element.23), channel_id=1, source_target_pairs={{0,16},{16,0},{32,48},{48,32},{64,80},{80,64},{96,112},{112,96},{1... | collective-permute-start | bytes 1572872 | tf_op jit(solution)/shard_map/ppermute | solution.py:393
  53.8 1.5 %collective-permute-done = bf16[4,256,256]{2,1,0:T(8,128)(2,1)S(1)} collective-permute-done((bf16[4,256,256]{2,1,0:T(8,128)(2,1)S(1)}, bf16[4,256,256]{2,1,0:T(8,128)(2,1)S(1)}, u32[]{:S(2)}, u32[]{:S(2)}) %collective-permute-start) | collective-permute-done | bytes 524320 | tf_op jit(solution)/shard_map/ppermute | solution.py:393
  55.4 0.1 fusion.2
  55.4 1.7 %collective-permute-start.1 = (bf16[256,256]{1,0:T(8,128)(2,1)S(1)}, bf16[256,256]{1,0:T(8,128)(2,1)S(1)}, u32[]{:S(2)}, u32[]{:S(2)}) collective-permute-start(bf16[256,256]{1,0:T(8,128)(2,1)S(1)} %get-tuple-element.35), channel_id=1, source_target_pairs={{0,32},{16,48},{32,64},{48,80},{64,96},{80,112},{96,0},{112,16},{1... | collective-permute-start | bytes 393224 | tf_op jit(solution)/shard_map/ppermute | solution.py:397
  57.1 2.3 %collective-permute-start.3 = (bf16[256,256]{1,0:T(8,128)(2,1)S(1)}, bf16[256,256]{1,0:T(8,128)(2,1)S(1)}, u32[]{:S(2)}, u32[]{:S(2)}) collective-permute-start(bf16[256,256]{1,0:T(8,128)(2,1)S(1)} %get-tuple-element.36), channel_id=1, source_target_pairs={{0,96},{16,112},{32,0},{48,16},{64,32},{80,48},{96,64},{112,80},{1... | collective-permute-start | bytes 393224 | tf_op jit(solution)/shard_map/ppermute | solution.py:397
  59.4 1.1 collective-permute-start.2
  60.5 2.5 %collective-permute-done.1 = bf16[256,256]{1,0:T(8,128)(2,1)S(1)} collective-permute-done((bf16[256,256]{1,0:T(8,128)(2,1)S(1)}, bf16[256,256]{1,0:T(8,128)(2,1)S(1)}, u32[]{:S(2)}, u32[]{:S(2)}) %collective-permute-start.1) | collective-permute-done | bytes 131104 | tf_op jit(solution)/shard_map/ppermute | solution.py:397
  63.0 0.0 collective-permute-done.3
  63.0 3.7 %collective-permute-done.2 = bf16[256,256]{1,0:T(8,128)(2,1)S(1)} collective-permute-done((bf16[256,256]{1,0:T(8,128)(2,1)S(1)}, bf16[256,256]{1,0:T(8,128)(2,1)S(1)}, u32[]{:S(2)}, u32[]{:S(2)}) %collective-permute-start.2) | collective-permute-done | bytes 131104 | tf_op jit(solution)/shard_map/ppermute | solution.py:397
  66.7 0.1 fusion.1
  66.8 0.0 copy-done.4
  66.8 0.7 fusion.9
  67.5 49.3 %all-to-all-done.1.tiles_ref = bf16[192,2,64,128]{3,2,1,0:T(8,128)(2,1)} async-done(((bf16[192,2,64,128]{3,2,1,0:T(8,128)(2,1)}), bf16[192,2,64,128]{3,2,1,0:T(8,128)(2,1)}, u32[]{:S(2)}, u32[]{:S(2)}) %all-to-all-start.1) | async-done | bytes 6291488 | tf_op jit(solution)/shard_map/all_to_all | solution.py:410
  116.8 15.5 %memory.1 = (bf16[3072,128]{1,0:T(8,128)(2,1)}, f32[4,272,128]{2,1,0:T(8,128)}, bf16[4,272,128]{2,1,0:T(8,128)(2,1)}) custom-call(s32[1,24]{1,0:T(1,128)} %bitcast.48, s32[1,192]{1,0:T(1,128)} %get-tuple-element.25.slot_ref, f32[1]{0:T(128)S(6)} %copy.16.bias_ref, bf16[192,2,64,128]{3,2,1,0:T(8,128)(2,1)} %all-to-all-done.1.tiles_ref, ...), custom_call_target="tpu_custom_call" | custom-call | flops 8000000000 | bytes 25165824 | tf_op jit(solution)/shard_map/memory/pallas_call | solution.py:355
  132.4 3.5 %collective-permute-start.4 = (bf16[4,272,128]{2,1,0:T(8,128)(2,1)}, bf16[4,272,128]{2,1,0:T(8,128)(2,1)S(1)}, u32[]{:S(2)}, u32[]{:S(2)}) collective-permute-start(bf16[4,272,128]{2,1,0:T(8,128)(2,1)} %get-tuple-element.32), channel_id=1, source_target_pairs={{0,16},{16,0},{32,48},{48,32},{64,80},{80,64},{96,112},{112,96},{1... | collective-permute-start | bytes 835592 | tf_op jit(solution)/shard_map/ppermute | solution.py:393
  135.8 1.4 collective-permute-done.4
  137.2 1.2 convert_add_fusion
  138.4 1.5 collective-permute-start.7
  139.9 3.0 %collective-permute-start.6 = (bf16[272,128]{1,0:T(8,128)(2,1)S(1)}, bf16[272,128]{1,0:T(8,128)(2,1)S(1)}, u32[]{:S(2)}, u32[]{:S(2)}) collective-permute-start(bf16[272,128]{1,0:T(8,128)(2,1)S(1)} %get-tuple-element.40), channel_id=1, source_target_pairs={{0,64},{16,80},{32,96},{48,112},{64,0},{80,16},{96,32},{112,48},{1... | collective-permute-start | bytes 208904 | tf_op jit(solution)/shard_map/ppermute | solution.py:397
  142.9 0.0 collective-permute-start.5
  143.0 0.4 collective-permute-done.7
  143.3 1.2 collective-permute-done.6
  144.6 2.7 %collective-permute-done.5 = bf16[272,128]{1,0:T(8,128)(2,1)S(1)} collective-permute-done((bf16[272,128]{1,0:T(8,128)(2,1)S(1)}, bf16[272,128]{1,0:T(8,128)(2,1)S(1)}, u32[]{:S(2)}, u32[]{:S(2)}) %collective-permute-start.5) | collective-permute-done | bytes 69664 | tf_op jit(solution)/shard_map/ppermute | solution.py:397
  147.3 0.6 fusion.8
  147.9 0.7 slice_add_fusion
  (3 shorter events, 0.0 us)
Async XLA Ops:
  22.2 5.5 %copy-start = (bf16[1,3072,128]{2,1,0:T(8,128)(2,1)S(1)}, bf16[1,3072,128]{2,1,0:T(8,128)(2,1)}, u32[]{:S(2)}) copy-start(bf16[1,3072,128]{2,1,0:T(8,128)(2,1)} %param.19) | copy-start | bytes 2359300
  22.2 5.5 %copy-start.1 = (bf16[2048,128]{1,0:T(8,128)(2,1)S(1)}, bf16[2048,128]{1,0:T(8,128)(2,1)}, u32[]{:S(2)}) copy-start(bf16[2048,128]{1,0:T(8,128)(2,1)} %wq_ref.1) | copy-start | bytes 1572868
  22.2 5.5 %copy-start.2 = (bf16[2048,128]{1,0:T(8,128)(2,1)S(1)}, bf16[2048,128]{1,0:T(8,128)(2,1)}, u32[]{:S(2)}) copy-start(bf16[2048,128]{1,0:T(8,128)(2,1)} %wk_ref.1) | copy-start | bytes 1572868
  22.2 5.5 %copy-start.3 = (bf16[2048,128]{1,0:T(8,128)(2,1)S(1)}, bf16[2048,128]{1,0:T(8,128)(2,1)}, u32[]{:S(2)}) copy-start(bf16[2048,128]{1,0:T(8,128)(2,1)} %wv_ref.1) | copy-start | bytes 1572868
  22.2 94.6 %all-to-all-start.1 = ((bf16[192,2,64,128]{3,2,1,0:T(8,128)(2,1)}), bf16[192,2,64,128]{3,2,1,0:T(8,128)(2,1)}, u32[]{:S(2)}, u32[]{:S(2)}) async-start(bf16[192,2,64,128]{3,2,1,0:T(8,128)(2,1)} %serve.1), calls=%async_computation.1 | async-start | bytes 12582912 | tf_op jit(solution)/shard_map/all_to_all | solution.py:410
  51.5 15.3 %copy-start.4 = (bf16[3072,128]{1,0:T(8,128)(2,1)}, bf16[3072,128]{1,0:T(8,128)(2,1)S(1)}, u32[]{:S(2)}) copy-start(bf16[3072,128]{1,0:T(8,128)(2,1)S(1)} %get-tuple-element.27.queries_in) | copy-start | bytes 2359300
  51.5 3.8 %collective-permute-start = (bf16[4,256,256]{2,1,0:T(8,128)(2,1)S(1)}, bf16[4,256,256]{2,1,0:T(8,128)(2,1)S(1)}, u32[]{:S(2)}, u32[]{:S(2)}) collective-permute-start(bf16[4,256,256]{2,1,0:T(8,128)(2,1)S(1)} %get-tuple-element.23), channel_id=1, source_target_pairs={{0,16},{16,0},{32,48},{48,32},{64,80},{80,64},{96,112},{112,96},{1... | collective-permute-start | bytes 1572872 | tf_op jit(solution)/shard_map/ppermute | solution.py:393
  55.4 7.6 %collective-permute-start.1 = (bf16[256,256]{1,0:T(8,128)(2,1)S(1)}, bf16[256,256]{1,0:T(8,128)(2,1)S(1)}, u32[]{:S(2)}, u32[]{:S(2)}) collective-permute-start(bf16[256,256]{1,0:T(8,128)(2,1)S(1)} %get-tuple-element.35), channel_id=1, source_target_pairs={{0,32},{16,48},{32,64},{48,80},{64,96},{80,112},{96,0},{112,16},{1... | collective-permute-start | bytes 393224 | tf_op jit(solution)/shard_map/ppermute | solution.py:397
  57.1 5.9 %collective-permute-start.3 = (bf16[256,256]{1,0:T(8,128)(2,1)S(1)}, bf16[256,256]{1,0:T(8,128)(2,1)S(1)}, u32[]{:S(2)}, u32[]{:S(2)}) collective-permute-start(bf16[256,256]{1,0:T(8,128)(2,1)S(1)} %get-tuple-element.36), channel_id=1, source_target_pairs={{0,96},{16,112},{32,0},{48,16},{64,32},{80,48},{96,64},{112,80},{1... | collective-permute-start | bytes 393224 | tf_op jit(solution)/shard_map/ppermute | solution.py:397
  59.4 7.3 %collective-permute-start.2 = (bf16[256,256]{1,0:T(8,128)(2,1)S(1)}, bf16[256,256]{1,0:T(8,128)(2,1)S(1)}, u32[]{:S(2)}, u32[]{:S(2)}) collective-permute-start(bf16[256,256]{1,0:T(8,128)(2,1)S(1)} %get-tuple-element.37), channel_id=1, source_target_pairs={{0,64},{16,80},{32,96},{48,112},{64,0},{80,16},{96,32},{112,48},{1... | collective-permute-start | bytes 393224 | tf_op jit(solution)/shard_map/ppermute | solution.py:397
  132.4 4.9 %collective-permute-start.4 = (bf16[4,272,128]{2,1,0:T(8,128)(2,1)}, bf16[4,272,128]{2,1,0:T(8,128)(2,1)S(1)}, u32[]{:S(2)}, u32[]{:S(2)}) collective-permute-start(bf16[4,272,128]{2,1,0:T(8,128)(2,1)} %get-tuple-element.32), channel_id=1, source_target_pairs={{0,16},{16,0},{32,48},{48,32},{64,80},{80,64},{96,112},{112,96},{1... | collective-permute-start | bytes 835592 | tf_op jit(solution)/shard_map/ppermute | solution.py:393
  138.4 5.0 %collective-permute-start.7 = (bf16[272,128]{1,0:T(8,128)(2,1)S(1)}, bf16[272,128]{1,0:T(8,128)(2,1)S(1)}, u32[]{:S(2)}, u32[]{:S(2)}) collective-permute-start(bf16[272,128]{1,0:T(8,128)(2,1)S(1)} %get-tuple-element.39), channel_id=1, source_target_pairs={{0,96},{16,112},{32,0},{48,16},{64,32},{80,48},{96,64},{112,80},{1... | collective-permute-start | bytes 208904 | tf_op jit(solution)/shard_map/ppermute | solution.py:397
  139.9 4.7 %collective-permute-start.6 = (bf16[272,128]{1,0:T(8,128)(2,1)S(1)}, bf16[272,128]{1,0:T(8,128)(2,1)S(1)}, u32[]{:S(2)}, u32[]{:S(2)}) collective-permute-start(bf16[272,128]{1,0:T(8,128)(2,1)S(1)} %get-tuple-element.40), channel_id=1, source_target_pairs={{0,64},{16,80},{32,96},{48,112},{64,0},{80,16},{96,32},{112,48},{1... | collective-permute-start | bytes 208904 | tf_op jit(solution)/shard_map/ppermute | solution.py:397
  142.9 4.4 %collective-permute-start.5 = (bf16[272,128]{1,0:T(8,128)(2,1)S(1)}, bf16[272,128]{1,0:T(8,128)(2,1)S(1)}, u32[]{:S(2)}, u32[]{:S(2)}) collective-permute-start(bf16[272,128]{1,0:T(8,128)(2,1)S(1)} %get-tuple-element.41), channel_id=1, source_target_pairs={{0,32},{16,48},{32,64},{48,80},{64,96},{80,112},{96,0},{112,16},{1... | collective-permute-start | bytes 208904 | tf_op jit(solution)/shard_map/ppermute | solution.py:397
